TPU v7x, 32 devices: a whole 2x2x4 slice. The times are simulated.
32 devices in a mesh: head: 2 (over y), seq: 8 (over z, x), rep: 2 (over core).
Axes of the slice: x: 2, y: 2, z: 4, core: 2. Of those that a mesh axis runs over, the one named last changes fastest.
Arguments:
- cache_keys: bfloat16 [8192, 4, 128], P(('rep', 'head', 'seq')), parts along dimension 0, may hold values from -6 to 6
- cache_values: bfloat16 [8192, 4, 128], P(('rep', 'head', 'seq')), parts along dimension 0, may hold values from -6 to 6
- span_slots: int32 [64], P('rep'), parts along dimension 0, may hold values from 0 to 31, each once
- prompt_length: int32 [2], P('rep'), parts along dimension 0, may hold values from 2048 to 4096
- queries: bfloat16 [32, 64, 128], P('rep', 'head'), parts along dimension 0, may hold values from -10 to 10
- new_keys: bfloat16 [32, 4, 128], P('rep', 'head'), parts along dimension 0, may hold values from -10 to 10
- new_values: bfloat16 [32, 4, 128], P('rep', 'head'), parts along dimension 0, may hold values from -6 to 6
- decode_offsets: int32 [32], P('rep'), parts along dimension 0, may hold values from 0 to 7
Outputs:
- relaid_keys: bfloat16 [8192, 4, 128], P(('rep', 'seq'), 'head'), parts along dimension 0
- relaid_values: bfloat16 [8192, 4, 128], P(('rep', 'seq'), 'head'), parts along dimension 0
- attended: bfloat16 [32, 64, 128], P('rep', 'head'), parts along dimension 0
There are 2 independent parts, one for each index of `rep`. A program takes and returns all parts, laid end to end along the dimension named above; each array names one. Nothing has to cross between parts.
Inputs may be any that keep to these rules, and one draw needn't show every extreme that they name: span_slots names every slot of a round once.
All inputs are finite; a program needn't handle non-finite values.
Results may differ from a plain program's by a relative error of at most 0.0035.
Values may be sent and summed in bfloat16 or wider, within the bound.
No kernel may reach another device: no remote copies, remote signals or barrier semaphores. Data moves between devices by JAX's collectives and lax.ppermute only.
A program may use at most 64 MiB of HBM per device.

v0:
```python
import math

import jax
import jax.numpy as jnp
from jax import lax
from jax.sharding import PartitionSpec as P


def joined(shard, axis, combine):
    everything = jax.tree.map(lambda part: lax.all_gather(part, axis), shard)
    first = jax.tree.map(lambda part: part[0], everything)

    def turn(k, so_far):
        return combine(so_far, jax.tree.map(lambda part: part[k], everything))

    return lax.fori_loop(1, lax.axis_size(axis), turn, first)


def partial_softmax(query_block, key_block, value_block, live_rows, score_scale):
    scores = (
        jnp.einsum("tkgd,nkd->ktgn", query_block, key_block, preferred_element_type=jnp.float32)
        * score_scale
    )
    scores = jnp.where(live_rows[None, None, None, :], scores, -1e30)
    row_max = jnp.max(scores, axis=-1)
    weights = jnp.exp(scores - row_max[..., None])
    weight_sum = jnp.sum(weights, axis=-1)
    weighted = jnp.einsum(
        "ktgn,nkd->ktgd",
        weights.astype(jnp.bfloat16),
        value_block,
        preferred_element_type=jnp.float32,
    )
    return (row_max, weight_sum, weighted)


def merge_pair(first, second):
    peak = jnp.maximum(first[0], second[0])
    first_factor = jnp.exp(first[0] - peak)
    second_factor = jnp.exp(second[0] - peak)
    return (
        peak,
        first[1] * first_factor + second[1] * second_factor,
        first[2] * first_factor[..., None] + second[2] * second_factor[..., None],
    )


def finish(
    row_max, weight_sum, weighted, query_local, new_keys, new_values, decode_offsets, score_scale
):
    new_scores = (
        jnp.einsum("tkgd,jkd->ktgj", query_local, new_keys, preferred_element_type=jnp.float32)
        * score_scale
    )
    visible = decode_offsets[None, :] <= decode_offsets[:, None]
    new_scores = jnp.where(visible[None, :, None, :], new_scores, -1e30)
    peak = jnp.maximum(row_max, jnp.max(new_scores, axis=-1))
    carried = jnp.exp(row_max - peak)
    new_weights = jnp.exp(new_scores - peak[..., None])
    total = weight_sum * carried + jnp.sum(new_weights, axis=-1)
    combined = weighted * carried[..., None] + jnp.einsum(
        "ktgj,jkd->ktgd",
        new_weights.astype(jnp.bfloat16),
        new_values,
        preferred_element_type=jnp.float32,
    )
    result = combined / total[..., None]
    head_local, token_count, group_size, head_dim = result.shape
    return (
        jnp.transpose(result, (1, 0, 2, 3))
        .reshape(token_count, head_local * group_size, head_dim)
        .astype(jnp.bfloat16)
    )


def body(
    cache_keys,
    cache_values,
    span_slots,
    prompt_length,
    queries,
    new_keys,
    new_values,
    decode_offsets,
):
    row_count, kv_all, head_dim = cache_keys.shape
    seq_count = lax.axis_size("seq")
    head_count = lax.axis_size("head")
    cycle_size = seq_count * head_count
    slot_count = span_slots.shape[0]
    span_rows = row_count // (2 * seq_count)
    kv_local = kv_all // head_count
    token_count = queries.shape[0]
    group_size = queries.shape[1] // kv_local
    length = prompt_length[0]
    score_scale = 1.0 / math.sqrt(head_dim)
    shard_rows = slot_count * span_rows

    def arrange(stored):
        split = stored.reshape(seq_count, 2 * span_rows, head_count, kv_local, head_dim)
        return jnp.transpose(split, (2, 0, 1, 3, 4))

    flat_keys = arrange(cache_keys).reshape(cycle_size, 2 * span_rows, kv_local, head_dim)
    flat_values = arrange(cache_values).reshape(cycle_size, 2 * span_rows, kv_local, head_dim)
    received = (
        lax.all_to_all(flat_keys, ("head", "seq"), split_axis=0, concat_axis=0, tiled=True),
        lax.all_to_all(flat_values, ("head", "seq"), split_axis=0, concat_axis=0, tiled=True),
    )
    shard_start = lax.axis_index("seq") * shard_rows
    live_shard = shard_start + jnp.arange(shard_rows, dtype=jnp.int32) < length

    def reorder(pieces):
        slotted = pieces.reshape(slot_count, span_rows, kv_local, head_dim)
        ordered = jnp.take(slotted, span_slots, axis=0).reshape(shard_rows, kv_local, head_dim)
        return jnp.where(live_shard[:, None, None], ordered, jnp.zeros((), ordered.dtype))

    relaid_keys = reorder(received[0])
    relaid_values = reorder(received[1])
    query_local = queries.reshape(token_count, kv_local, group_size, head_dim)
    row_max, weight_sum, weighted = partial_softmax(
        query_local, relaid_keys, relaid_values, live_shard, score_scale
    )
    row_max, weight_sum, weighted = joined((row_max, weight_sum, weighted), "seq", merge_pair)
    attended = finish(
        row_max,
        weight_sum,
        weighted,
        query_local,
        new_keys,
        new_values,
        decode_offsets,
        score_scale,
    )
    return (relaid_keys, relaid_values, attended)


def solution(mesh):
    return jax.shard_map(
        body,
        mesh=mesh,
        in_specs=(
            P(("rep", "head", "seq"), None, None),
            P(("rep", "head", "seq"), None, None),
            P("rep"),
            P("rep"),
            P("rep", "head", None),
            P("rep", "head", None),
            P("rep", "head", None),
            P("rep"),
        ),
        out_specs=(
            P(("rep", "seq"), "head", None),
            P(("rep", "seq"), "head", None),
            P("rep", "head", None),
        ),
        check_vma=False,
    )
```

profile of v0, /device:TPU:0, one launch (start us, length us, event | category | flops | bytes accessed | tf_op | source)
XLA Modules:
  0.0 125.0 jit_solution(18142710124813088006)
XLA Ops:
  7.2 1.0 copy.60
  8.2 0.7 copy.61
  8.9 8.3 %all-to-all-start.1 = ((bf16[16,32,2,128]{3,1,2,0:T(8,128)(2,1)}), bf16[16,32,2,128]{3,1,2,0:T(8,128)(2,1)S(1)}, u32[]{:S(2)}, u32[]{:S(2)}) async-start(bf16[16,32,2,128]{3,1,2,0:T(8,128)(2,1)} %bitcast.11), calls=%async_computation.1 | async-start | bytes 524288 | tf_op jit(solution)/shard_map/all_to_all | solution.py:107
  17.3 1.0 copy.56
  18.3 0.7 copy.57
  19.0 8.1 %all-to-all-done.1 = bf16[16,32,2,128]{3,1,2,0:T(8,128)(2,1)S(1)} async-done(((bf16[16,32,2,128]{3,1,2,0:T(8,128)(2,1)}), bf16[16,32,2,128]{3,1,2,0:T(8,128)(2,1)S(1)}, u32[]{:S(2)}, u32[]{:S(2)}) %all-to-all-start.1) | async-done | bytes 262176 | tf_op jit(solution)/shard_map/all_to_all | solution.py:107
  27.1 3.5 %all-to-all-start = ((bf16[16,32,2,128]{3,1,2,0:T(8,128)(2,1)}), bf16[16,32,2,128]{3,1,2,0:T(8,128)(2,1)S(1)}, u32[]{:S(2)}, u32[]{:S(2)}) async-start(bf16[16,32,2,128]{3,1,2,0:T(8,128)(2,1)} %bitcast.6), calls=%async_computation | async-start | bytes 524288 | tf_op jit(solution)/shard_map/all_to_all | solution.py:106
  31.5 0.6 gather_fusion.1
  32.1 7.7 %all-to-all-done = bf16[16,32,2,128]{3,1,2,0:T(8,128)(2,1)S(1)} async-done(((bf16[16,32,2,128]{3,1,2,0:T(8,128)(2,1)}), bf16[16,32,2,128]{3,1,2,0:T(8,128)(2,1)S(1)}, u32[]{:S(2)}, u32[]{:S(2)}) %all-to-all-start) | async-done | bytes 262176 | tf_op jit(solution)/shard_map/all_to_all | solution.py:106
  39.9 0.6 gather_fusion
  40.5 0.1 broadcast_select_fusion
  40.7 0.1 bitcast_select_fusion
  40.8 0.4 fusion.25
  41.2 1.1 fusion.11
  42.4 0.4 fusion.26
  42.8 1.0 copy.70
  43.8 1.0 copy.71
  44.8 31.2 %all-gather = f32[16,16,16]{2,1,0:T(8,128)S(1)} all-gather(f32[2,16,16]{2,1,0:T(8,128)S(1)} %get-tuple-element.215), channel_id=2, replica_groups=mesh['head'=2,'seq'=8,'rep'=2] {'seq'}, dimensions={0}, use_global_device_ids=true | all-gather | bytes 18432 | tf_op jit(solution)/shard_map/all_gather | solution.py:10
  76.0 0.3 fusion.10
  76.3 30.8 %all-gather.1 = f32[16,16,16]{2,1,0:T(8,128)S(1)} all-gather(f32[2,16,16]{2,1,0:T(8,128)S(1)} %fusion.10), channel_id=3, replica_groups=mesh['head'=2,'seq'=8,'rep'=2] {'seq'}, dimensions={0}, use_global_device_ids=true | all-gather | bytes 18432 | tf_op jit(solution)/shard_map/all_gather | solution.py:10
  107.1 1.0 slice.21
  108.1 8.9 %while.19 = (s32[]{:T(128)}, f32[2,16,16]{2,1,0:T(8,128)S(1)}, f32[2,16,16]{2,1,0:T(8,128)S(1)}, f32[2,16,16,128]{3,2,1,0:T(8,128)S(1)}, f32[8,2,16,16]{3,2,1,0:...) while((s32[]{:T(128)}, f32[2,16,16]{2,1,0:T(8,128)S(1)}, ...), condition=%wide.region_3.5_spmd, body=%wide.region_2.4_spmd.sunk | while | flops 199685 | bytes 807063 | solution.py:16
  108.1 1.2 fusion.30
  109.4 1.2 fusion.30
  110.7 1.2 fusion.30
  112.0 1.2 fusion.30
  113.3 1.2 fusion.30
  114.5 1.2 fusion.30
  115.8 1.2 fusion.30
  117.1 0.1 fusion.16
  117.2 0.3 fusion.8
  117.5 0.7 copy.69
  (33 shorter events, 0.4 us)
Async XLA Ops:
  7.2 110.0 %copy-start = (bf16[16,2,128]{2,1,0:T(2,128)(2,1)S(1)}, bf16[16,2,128]{2,1,0:T(2,128)(2,1)}, u32[]{:S(2)}) copy-start(bf16[16,2,128]{2,1,0:T(2,128)(2,1)} %param.18) | copy-start | bytes 24580
  7.2 23.6 %copy-start.4 = (s32[32]{0:T(128)S(1)}, s32[32]{0:T(128)}, u32[]{:S(2)}) copy-start(s32[32]{0:T(128)} %param.14) | copy-start | bytes 388
  8.9 18.2 %all-to-all-start.1 = ((bf16[16,32,2,128]{3,1,2,0:T(8,128)(2,1)}), bf16[16,32,2,128]{3,1,2,0:T(8,128)(2,1)S(1)}, u32[]{:S(2)}, u32[]{:S(2)}) async-start(bf16[16,32,2,128]{3,1,2,0:T(8,128)(2,1)} %bitcast.11), calls=%async_computation.1 | async-start | bytes 524288 | tf_op jit(solution)/shard_map/all_to_all | solution.py:107
  27.1 12.7 %all-to-all-start = ((bf16[16,32,2,128]{3,1,2,0:T(8,128)(2,1)}), bf16[16,32,2,128]{3,1,2,0:T(8,128)(2,1)S(1)}, u32[]{:S(2)}, u32[]{:S(2)}) async-start(bf16[16,32,2,128]{3,1,2,0:T(8,128)(2,1)} %bitcast.6), calls=%async_computation | async-start | bytes 524288 | tf_op jit(solution)/shard_map/all_to_all | solution.py:106
  30.7 76.4 %all-gather.5.cloned.1.call-start = ((), (), s32[]{:S(2)}) async-start(), calls=%async_computation.2 | async-start | bytes 2359296 | tf_op jit(solution)/shard_map/all_gather | solution.py:10
  32.1 8.7 %copy-start.1 = (bf16[16,32,128]{2,1,0:T(8,128)(2,1)S(1)}, bf16[16,32,128]{2,1,0:T(8,128)(2,1)}, u32[]{:S(2)}) copy-start(bf16[16,32,128]{2,1,0:T(8,128)(2,1)} %param.16) | copy-start | bytes 393220
  40.7 1.6 %copy-start.2 = (s32[16]{0:T(128)S(1)}, s32[16]{0:T(128)}, u32[]{:S(2)}) copy-start(s32[16]{0:T(128)} %param.19) | copy-start | bytes 196
  40.7 1.7 %copy-start.3 = (bf16[16,2,128]{2,1,0:T(2,128)(2,1)S(1)}, bf16[16,2,128]{2,1,0:T(2,128)(2,1)}, u32[]{:S(2)}) copy-start(bf16[16,2,128]{2,1,0:T(2,128)(2,1)} %param.17) | copy-start | bytes 24580
Sparse Core Ops, SparseCore 0:
  42.4 48.2 all-gather.4
where the time goes:
time: 126 us; the launch traced here: 125 us
  blocking collectives  62 us (49%)
  waiting for transfers between devices  15.9 us (13%)
  between operations  14.9 us (12%)
  starting transfers between devices  11.9 us (9%)
  other arithmetic  9.49 us (8%)
  local copies, waits for them, and re-layouts  8.38 us (7%)
  matrix products  2.15 us (2%)
    all_gather x2, blocking collectives, joined(): everything = jax.tree.map(lambda part: lax.all_gather(part, axis), shard)  62 us
    add x7, other arithmetic, merge_pair(): first[2] * first_factor[..., None] + second[2] * second_factor[..., None]  8.57 us
    all_to_all x1, starting transfers between devices, body(): lax.all_to_all(flat_values, ('head', 'seq'), split_axis=0, concat_axis=0,...  8.34 us
    all_to_all x1, waiting for transfers between devices, body(): lax.all_to_all(flat_values, ('head', 'seq'), split_axis=0, concat_axis=0,...  8.15 us
    all_to_all x1, waiting for transfers between devices, body(): lax.all_to_all(flat_keys, ('head', 'seq'), split_axis=0, concat_axis=0, t...  7.73 us
    unnamed x14, local copies, waits for them, and re-layouts  3.96 us
    all_to_all x1, starting transfers between devices, body(): lax.all_to_all(flat_keys, ('head', 'seq'), split_axis=0, concat_axis=0, t...  3.53 us
  transfers between devices with their start and end apart: 3, of which 2 were waited for; matrix products, arithmetic and copies ran while one was open for 4% of the time, Pallas kernels for 0%

commit v1 on v0

v1 whole, which is shorter than its diff:
```python
import functools
import math

import jax
import jax.numpy as jnp
from jax import lax
from jax.experimental import pallas as pl
from jax.experimental.pallas import tpu as pltpu
from jax.sharding import PartitionSpec as P

BF16 = jnp.bfloat16
F32 = jnp.float32
DEAD = -1e30
STAT_ROWS = 16
VMEM = pl.BlockSpec(memory_space=pltpu.VMEM)
SMEM = pl.BlockSpec(memory_space=pltpu.SMEM)
ANY = pl.BlockSpec(memory_space=pl.ANY)


def dot_rows(a, b):
    return lax.dot_general(a, b, (((1,), (1,)), ((), ())), preferred_element_type=F32)


def three_parts(x):
    high = x.astype(BF16).astype(F32)
    rest = x - high
    middle = rest.astype(BF16).astype(F32)
    return high, middle, rest - middle


def pack_kernel(keys_ref, values_ref, send_ref, held, in_sems, out_sems):
    head_count = keys_ref.shape[2]
    pieces = [(c, h) for h in range(head_count) for c in range(2)]
    ins = []
    for c, h in pieces:
        source = (keys_ref, values_ref)[c]
        copy = pltpu.make_async_copy(source.at[:, :, h], held.at[c, h], in_sems.at[c, h])
        copy.start()
        ins.append(copy)
    outs = []
    for (c, h), copy in zip(pieces, ins):
        copy.wait()
        out = pltpu.make_async_copy(held.at[c, h], send_ref.at[h, :, c], out_sems.at[c, h])
        out.start()
        outs.append(out)
    for out in outs:
        out.wait()


def pack(cache_keys, cache_values, seq_count, head_count):
    row_count, kv_all, head_dim = cache_keys.shape
    split = (seq_count, row_count // seq_count, head_count, kv_all // head_count, head_dim)
    rows, kv = split[1], split[3]
    return pl.pallas_call(
        pack_kernel,
        out_shape=jax.ShapeDtypeStruct((head_count, seq_count, 2, rows, kv, head_dim), BF16),
        in_specs=[ANY, ANY],
        out_specs=ANY,
        scratch_shapes=[
            pltpu.VMEM((2, head_count, seq_count, rows, kv, head_dim), BF16),
            pltpu.SemaphoreType.DMA((2, head_count)),
            pltpu.SemaphoreType.DMA((2, head_count)),
        ],
        name="pack",
    )(cache_keys.reshape(split), cache_values.reshape(split))


def partial_kernel(score_scale, seq_count, query_ref, got_ref, bias_ref, out_ref, rows_buf, stat_buf):
    tokens, heads, head_dim = query_ref.shape
    kv_count = bias_ref.shape[0]
    columns = bias_ref.shape[1]
    group = heads // kv_count
    keys = got_ref[:, 0].reshape(columns, head_dim)
    values = got_ref[:, 1].reshape(columns, head_dim)
    lane = lax.broadcasted_iota(jnp.int32, (tokens * group, head_dim), 1)
    for g in range(kv_count):
        query = query_ref[:, g * group : (g + 1) * group, :].reshape(tokens * group, head_dim)
        scores = dot_rows(query, keys) * score_scale + bias_ref[g : g + 1, :]
        peak = jnp.max(scores, axis=1, keepdims=True)
        weights = jnp.exp(scores - peak)
        total = jnp.sum(weights, axis=1, keepdims=True)
        weighted = jnp.dot(weights.astype(BF16), values, preferred_element_type=F32)
        stats = jnp.zeros((tokens * group, head_dim), F32)
        for at, part in enumerate(three_parts(peak) + three_parts(total)):
            stats = jnp.where(lane == at, part, stats)
        rows_buf[:, g] = weighted.astype(BF16).reshape(tokens, group, head_dim)
        stat_buf[:, g] = stats.astype(BF16).reshape(tokens, group, head_dim)
    per = tokens * heads // seq_count
    all_rows = rows_buf[...].reshape(tokens * heads, head_dim)
    all_stats = stat_buf[...].reshape(tokens * heads, head_dim)
    pick = (
        lax.broadcasted_iota(jnp.int32, (STAT_ROWS, head_dim), 0)
        == lax.broadcasted_iota(jnp.int32, (STAT_ROWS, head_dim), 1)
    ).astype(F32).astype(BF16)
    turned = dot_rows(pick, all_stats).astype(BF16)
    for s in range(seq_count):
        out_ref[s, :per, :] = all_rows[s * per : (s + 1) * per]
        out_ref[s, per:, :per] = turned[:, s * per : (s + 1) * per]


def partial_rows(query, got, bias, score_scale, seq_count):
    tokens, heads, head_dim = query.shape
    kv_count = bias.shape[0]
    group = heads // kv_count
    per = tokens * heads // seq_count
    return pl.pallas_call(
        functools.partial(partial_kernel, score_scale, seq_count),
        out_shape=jax.ShapeDtypeStruct((seq_count, per + STAT_ROWS, head_dim), BF16),
        in_specs=[VMEM, VMEM, VMEM],
        out_specs=VMEM,
        scratch_shapes=[
            pltpu.VMEM((tokens, kv_count, group, head_dim), BF16),
            pltpu.VMEM((tokens, kv_count, group, head_dim), BF16),
        ],
        name="partial_rows",
    )(query, got, bias)


def new_kernel(score_scale, query_ref, keys_ref, values_ref, bias_ref, weighted_ref, peak_ref, total_ref):
    scores = dot_rows(query_ref[...], keys_ref[...]) * score_scale + bias_ref[...]
    peak = jnp.max(scores, axis=1, keepdims=True)
    weights = jnp.exp(scores - peak)
    total = jnp.sum(weights, axis=1, keepdims=True)
    weighted_ref[...] = jnp.dot(
        weights.astype(BF16), values_ref[...], preferred_element_type=F32
    )
    peak_ref[...] = jnp.broadcast_to(peak, peak_ref.shape)
    total_ref[...] = jnp.broadcast_to(total, total_ref.shape)


def new_rows(query, keys, values, bias, score_scale):
    shape = jax.ShapeDtypeStruct(query.shape, F32)
    return pl.pallas_call(
        functools.partial(new_kernel, score_scale),
        out_shape=(shape, shape, shape),
        in_specs=[VMEM] * 4,
        out_specs=(VMEM, VMEM, VMEM),
        name="new_rows",
    )(query, keys, values, bias)


def merge_kernel(got_ref, weighted_ref, peak_ref, total_ref, out_ref):
    seq_count = got_ref.shape[0]
    per, head_dim = weighted_ref.shape
    eye = (
        lax.broadcasted_iota(jnp.int32, (per, per), 0)
        == lax.broadcasted_iota(jnp.int32, (per, per), 1)
    ).astype(F32).astype(BF16)
    stats = got_ref[:, per:, :per].reshape(seq_count * STAT_ROWS, per)
    turned = dot_rows(eye, stats)

    def column(s, at):
        base = s * STAT_ROWS + at
        parts = [turned[:, base + k : base + k + 1] for k in range(3)]
        return jnp.broadcast_to(parts[0] + parts[1] + parts[2], (per, head_dim))

    peaks = [column(s, 0) for s in range(seq_count)] + [peak_ref[...]]
    peak = functools.reduce(jnp.maximum, peaks)
    scale = jnp.exp(peaks[-1] - peak)
    total = total_ref[...] * scale
    weighted = weighted_ref[...] * scale
    for s in range(seq_count):
        scale = jnp.exp(peaks[s] - peak)
        total = total + column(s, 3) * scale
        weighted = weighted + got_ref[s, :per, :].astype(F32) * scale
    result = (weighted / total).astype(BF16)
    for s in range(seq_count):
        out_ref[s] = result


def merge(got, weighted, peak, total):
    seq_count = got.shape[0]
    return pl.pallas_call(
        merge_kernel,
        out_shape=jax.ShapeDtypeStruct((seq_count,) + weighted.shape, BF16),
        in_specs=[VMEM] * 4,
        out_specs=VMEM,
        name="merge",
    )(got, weighted, peak, total)


def relay_kernel(slots_ref, live_ref, got_ref, keys_ref, values_ref):
    slot_count, span, head_dim = keys_ref.shape
    row = lax.broadcasted_iota(jnp.int32, (span, head_dim), 0)
    live = live_ref[0]

    def one(t, carry):
        slot = slots_ref[t]
        kept = row < live - t * span
        for c, out_ref in enumerate((keys_ref, values_ref)):
            block = got_ref[slot // 2, c, slot % 2].astype(F32)
            out_ref[t] = jnp.where(kept, block, 0.0).astype(BF16)
        return carry

    lax.fori_loop(0, slot_count, one, 0, unroll=4)


def relay(span_slots, live, got):
    cycle, _, _, span, head_dim = got.shape
    shape = jax.ShapeDtypeStruct((span_slots.shape[0], span, head_dim), BF16)
    return pl.pallas_call(
        relay_kernel,
        out_shape=(shape, shape),
        in_specs=[SMEM, SMEM, VMEM],
        out_specs=(VMEM, VMEM),
        name="relay",
    )(span_slots, live, got)


def body(
    cache_keys,
    cache_values,
    span_slots,
    prompt_length,
    queries,
    new_keys,
    new_values,
    decode_offsets,
):
    row_count, kv_all, head_dim = cache_keys.shape
    seq_count = lax.axis_size("seq")
    head_count = lax.axis_size("head")
    cycle_size = seq_count * head_count
    slot_count = span_slots.shape[0]
    span_rows = row_count // (2 * seq_count)
    kv_local = kv_all // head_count
    token_count, heads, _ = queries.shape
    group_size = heads // kv_local
    length = prompt_length[0]
    score_scale = 1.0 / math.sqrt(head_dim)
    shard_rows = slot_count * span_rows
    seq_index = lax.axis_index("seq")
    shard_start = seq_index * shard_rows

    packed = pack(cache_keys, cache_values, seq_count, head_count)
    got = lax.all_to_all(
        packed.reshape(cycle_size, 2, 2 * span_rows * kv_local, head_dim),
        ("head", "seq"),
        split_axis=0,
        concat_axis=0,
        tiled=True,
    )

    spans = jnp.arange(slot_count, dtype=jnp.int32)
    place = jnp.sum(
        jnp.where(span_slots[None, :] == spans[:, None], spans[None, :], 0), axis=1
    )
    column = jnp.arange(shard_rows * kv_local, dtype=jnp.int32)
    position = (
        jnp.broadcast_to(
            (place * span_rows)[:, None], (slot_count, span_rows * kv_local)
        ).reshape(-1)
        + (column // kv_local) % span_rows
        + shard_start
    )
    matches = (column % kv_local)[None, :] == jnp.arange(kv_local, dtype=jnp.int32)[:, None]
    bias = jnp.where(matches & (position < length)[None, :], 0.0, DEAD).astype(F32)

    per = token_count * heads // seq_count
    own_row = seq_index * per + jnp.arange(per, dtype=jnp.int32)
    own_token = own_row // heads
    own_kv = (own_row // group_size) % kv_local
    own_query = lax.dynamic_slice_in_dim(
        queries.reshape(token_count * heads, head_dim), seq_index * per, per, 0
    )
    new_column = jnp.arange(token_count * kv_local, dtype=jnp.int32)
    own_offset = jnp.sum(
        jnp.where(
            own_token[:, None] == jnp.arange(token_count, dtype=jnp.int32)[None, :],
            decode_offsets[None, :],
            0,
        ),
        axis=1,
    )
    visible = jnp.repeat(decode_offsets, kv_local)[None, :] <= own_offset[:, None]
    visible = visible & ((new_column % kv_local)[None, :] == own_kv[:, None])
    new_bias = jnp.where(visible, 0.0, DEAD).astype(F32)
    fresh = new_rows(
        own_query,
        new_keys.reshape(token_count * kv_local, head_dim),
        new_values.reshape(token_count * kv_local, head_dim),
        new_bias,
        score_scale,
    )

    partial = partial_rows(queries, got, bias, score_scale, seq_count)
    shares = lax.all_to_all(partial, "seq", split_axis=0, concat_axis=0, tiled=True)
    merged = merge(shares, *fresh)
    attended = lax.all_to_all(merged, "seq", split_axis=0, concat_axis=0, tiled=True)

    live = jnp.clip(length - shard_start, 0, shard_rows) * kv_local
    relaid_keys, relaid_values = relay(
        span_slots,
        live.reshape(1),
        got.reshape(cycle_size, 2, 2, span_rows * kv_local, head_dim),
    )
    whole = (shard_rows, kv_local, head_dim)
    return (
        relaid_keys.reshape(whole),
        relaid_values.reshape(whole),
        attended.reshape(token_count, heads, head_dim),
    )


def solution(mesh):
    return jax.shard_map(
        body,
        mesh=mesh,
        in_specs=(
            P(("rep", "head", "seq"), None, None),
            P(("rep", "head", "seq"), None, None),
            P("rep"),
            P("rep"),
            P("rep", "head", None),
            P("rep", "head", None),
            P("rep", "head", None),
            P("rep"),
        ),
        out_specs=(
            P(("rep", "seq"), "head", None),
            P(("rep", "seq"), "head", None),
            P("rep", "head", None),
        ),
        check_vma=False,
    )
```

time: 126 us -> 55.5 us (0.44)
  blocking collectives: 62 us -> 0 us
  between operations: 14.9 us -> 1.39 us
  Pallas kernels: 0 us -> 10.8 us
  other arithmetic: 9.49 us -> 1.55 us
  waiting for transfers between devices: 15.9 us -> 22.2 us
  local copies, waits for them, and re-layouts: 8.38 us -> 3.75 us
  starting transfers between devices: 11.9 us -> 15.2 us
  matrix products: 2.15 us -> 0 us
    all_gather x2 -> x0, blocking collectives: 62 us -> none  [joined(): everything = jax.tree.map(lambda part: lax.all_gather(part, axis), shard)]
    pallas_call x0 -> x5, Pallas kernels: none -> 10.8 us  [the longest x1 3.07 us: partial_rows(): pl.pallas_call(functools.partial(partial_kernel, score_scale, seq_count),...]
    add x15 -> x0, other arithmetic: 8.74 us -> none  [the longest x7 8.57 us: merge_pair(): first[2] * first_factor[..., None] + second[2] * second_factor[..., None]]
    all_to_all x2 -> x3, waiting for transfers between devices: 15.9 us -> 22.2 us  [the longest x1 11.9 us: body(): lax.all_to_all(packed.reshape(cycle_size, 2, 2 * span_rows * kv_local, he...]
    all_to_all x2 -> x3, starting transfers between devices: 11.9 us -> 15.2 us  [the longest x1 8.35 us: body(): lax.all_to_all(packed.reshape(cycle_size, 2, 2 * span_rows * kv_local, he...]
    dot_general x4 -> x0, matrix products: 2.15 us -> none  [the longest x1 1.06 us: partial_softmax(): jnp.einsum('ktgn,nkd->ktgd', weights.astype(jnp.bfloat16), value_block, p...]
    unnamed x14 -> x9, local copies, waits for them, and re-layouts: 3.96 us -> 2.12 us
    transpose x2 -> x0, local copies, waits for them, and re-layouts: 1.46 us -> none  [arrange(): return jnp.transpose(split, (2, 0, 1, 3, 4))]
  transfers between devices with their start and end apart: 3 -> 3, of which waited for: 2 -> 3; matrix products, arithmetic and copies ran while one was open for 4% -> 6% of each run, Pallas kernels for 0% -> 7%
where the time goes in v1:
time: 55.5 us; the launch traced here: 54.9 us
  waiting for transfers between devices  22.2 us (40%)
  starting transfers between devices  15.2 us (27%)
  Pallas kernels  10.8 us (19%)
  local copies, waits for them, and re-layouts  3.75 us (7%)
  other arithmetic  1.55 us (3%)
  between operations  1.39 us (3%)
    all_to_all x1, waiting for transfers between devices, body(): lax.all_to_all(packed.reshape(cycle_size, 2, 2 * span_rows * kv_local, he...  11.9 us
    all_to_all x1, starting transfers between devices, body(): lax.all_to_all(packed.reshape(cycle_size, 2, 2 * span_rows * kv_local, he...  8.35 us
    all_to_all x1, waiting for transfers between devices, body(): lax.all_to_all(merged, 'seq', split_axis=0, concat_axis=0, tiled=True)  5.14 us
    all_to_all x1, waiting for transfers between devices, body(): lax.all_to_all(partial, 'seq', split_axis=0, concat_axis=0, tiled=True)  5.1 us
    all_to_all x1, starting transfers between devices, body(): lax.all_to_all(partial, 'seq', split_axis=0, concat_axis=0, tiled=True)  3.43 us
    all_to_all x1, starting transfers between devices, body(): lax.all_to_all(merged, 'seq', split_axis=0, concat_axis=0, tiled=True)  3.37 us
    pallas_call x1, Pallas kernels, partial_rows(): pl.pallas_call(functools.partial(partial_kernel, score_scale, seq_count),...  3.07 us
    pallas_call x1, Pallas kernels, relay(): pl.pallas_call(relay_kernel, out_shape=(shape, shape), in_specs=[SMEM, SM...  2.13 us
  transfers between devices with their start and end apart: 3, of which 3 were waited for; matrix products, arithmetic and copies ran while one was open for 6% of the time, Pallas kernels for 7%

profile of v1, /device:TPU:0, one launch (start us, length us, event | category | flops | bytes accessed | tf_op | source)
XLA Modules:
  0.0 54.9 jit_solution(6841056770089935752)
XLA Ops:
  0.6 1.8 %pack.1 = bf16[2,8,2,32,2,128]{5,4,3,2,1,0:T(2,128)(2,1)} custom-call(bf16[8,32,2,2,128]{4,3,2,1,0:T(2,128)(2,1)} %bitcast.17, bf16[8,32,2,2,128]{4,3,2,1,0:T(2,128)(2,1)} %bitcast.18), custom_call_target="tpu_custom_call" | custom-call | tf_op jit(solution)/shard_map/pack/pallas_call | solution.py:54
  2.5 0.0 copy-start.3
  2.5 8.4 %all-to-all-start = ((bf16[16,2,64,128]{3,2,1,0:T(8,128)(2,1)}), bf16[16,2,64,128]{3,2,1,0:T(8,128)(2,1)S(1)}, u32[]{:S(2)}, u32[]{:S(2)}) async-start(bf16[16,2,64,128]{3,2,1,0:T(8,128)(2,1)} %bitcast.15), calls=%async_computation | async-start | bytes 1048576 | tf_op jit(solution)/shard_map/all_to_all | solution.py:236
  10.8 0.0 copy-done.3
  10.8 0.1 select_reduce_fusion
  11.0 0.0 copy-start.2
  11.6 0.0 copy-done.2
  11.6 0.1 broadcast_in_dim.66
  11.7 0.1 le.15
  11.8 0.1 broadcast_in_dim.63
  11.9 0.1 reshape.147
  12.0 1.3 %constant_dynamic-slice_fusion.query_ref = bf16[64,128]{1,0:T(8,128)(2,1)} fusion(bf16[512,128]{1,0:T(8,128)(2,1)} %bitcast.19, s32[]{:T(128)S(6)} %select_n.88), kind=kLoop, calls=%fused_computation.38 | loop fusion | bytes 32772 | tf_op jit(solution)/shard_map/dynamic_slice | solution.py:263
  13.3 0.1 select_reduce_fusion.1
  13.4 0.6 %and_select_fusion.1.bias_ref = f32[2,1024]{1,0:T(2,128)} fusion(pred[1024]{0:T(1024)(128)(4,1)S(1)} %fusion.4, s32[1024]{0:T(1024)S(1)} %add_select_fusion.2), kind=kLoop, calls=%fused_computation.3 | loop fusion | flops 6144 | bytes 13312 | tf_op jit(solution)/shard_map/jit(_where)/select_n | solution.py:257
  14.0 11.9 %all-to-all-done.got_ref = bf16[16,2,64,128]{3,2,1,0:T(8,128)(2,1)S(1)} async-done(((bf16[16,2,64,128]{3,2,1,0:T(8,128)(2,1)}), bf16[16,2,64,128]{3,2,1,0:T(8,128)(2,1)S(1)}, u32[]{:S(2)}, u32[]{:S(2)}) %all-to-all-start) | async-done | bytes 524320 | tf_op jit(solution)/shard_map/all_to_all | solution.py:236
  26.0 0.0 copy-start
  26.0 0.8 %copy-done = bf16[16,2,64,128]{3,2,1,0:T(8,128)(2,1)} copy-done((bf16[16,2,64,128]{3,2,1,0:T(8,128)(2,1)}, bf16[16,2,64,128]{3,2,1,0:T(8,128)(2,1)S(1)}, u32[]{:S(2)}) %copy-start) | copy-done | bytes 524312
  26.8 3.1 %partial_rows.1 = bf16[8,80,128]{2,1,0:T(8,128)(2,1)} custom-call(bf16[16,32,128]{2,1,0:T(8,128)(2,1)} %query_ref.1, bf16[16,2,64,128]{3,2,1,0:T(8,128)(2,1)} %copy-done, f32[2,1024]{1,0:T(2,128)} %and_select_fusion.1.bias_ref), custom_call_target="tpu_custom_call" | custom-call | tf_op jit(solution)/shard_map/partial_rows/pallas_call | solution.py:106
  29.8 3.4 %all-to-all-start.1 = ((bf16[8,80,128]{2,1,0:T(8,128)(2,1)}), bf16[8,80,128]{2,1,0:T(8,128)(2,1)S(1)}, u32[]{:S(2)}, u32[]{:S(2)}) async-start(bf16[8,80,128]{2,1,0:T(8,128)(2,1)} %partial_rows.1), calls=%async_computation.1 | async-start | bytes 327680 | tf_op jit(solution)/shard_map/all_to_all | solution.py:287
  33.3 0.7 %and_select_fusion.bias_ref = f32[64,32]{1,0:T(8,128)} fusion(s32[32]{0:T(128)S(1)} %and_select_fusion.4, s32[32]{0:T(128)S(1)} %le.15, s32[64]{0:T(128)S(1)} %get-tuple-element.13, s32[64]{0:T(128)S(1)} %select_reduce_fusion.1), kind=kLoop, calls=%fused_computation | loop fusion | flops 8192 | bytes 8960 | tf_op jit(solution)/shard_map/jit(_where)/select_n | solution.py:277
  34.0 1.8 %new_rows.1 = (f32[64,128]{1,0:T(8,128)}, f32[64,128]{1,0:T(8,128)}, f32[64,128]{1,0:T(8,128)}) custom-call(bf16[64,128]{1,0:T(8,128)(2,1)} %constant_dynamic-slice_fusion.query_ref, bf16[32,128]{1,0:T(8,128)(2,1)} %bitcast.20, bf16[32,128]{1,0:T(8,128)(2,1)} %bitcast.21, f32[64,32]{1,0:T(8,128)} %and_select_fusion.bias_ref), custom_call_target="tpu_custom_call" | custom-call | tf_op jit(solution)/shard_map/new_rows/pallas_call | solution.py:133
  35.7 5.1 %all-to-all-done.1.got_ref = bf16[8,80,128]{2,1,0:T(8,128)(2,1)S(1)} async-done(((bf16[8,80,128]{2,1,0:T(8,128)(2,1)}), bf16[8,80,128]{2,1,0:T(8,128)(2,1)S(1)}, u32[]{:S(2)}, u32[]{:S(2)}) %all-to-all-start.1) | async-done | bytes 163872 | tf_op jit(solution)/shard_map/all_to_all | solution.py:287
  40.8 0.0 copy-start.1
  40.8 0.7 %copy-done.1 = bf16[8,80,128]{2,1,0:T(8,128)(2,1)} copy-done((bf16[8,80,128]{2,1,0:T(8,128)(2,1)}, bf16[8,80,128]{2,1,0:T(8,128)(2,1)S(1)}, u32[]{:S(2)}) %copy-start.1) | copy-done | bytes 163864
  41.5 2.1 %merge.1 = bf16[8,64,128]{2,1,0:T(8,128)(2,1)} custom-call(bf16[8,80,128]{2,1,0:T(8,128)(2,1)} %copy-done.1, f32[64,128]{1,0:T(8,128)} %get-tuple-element.10.weighted_ref, f32[64,128]{1,0:T(8,128)} %get-tuple-element.11.peak_ref, f32[64,128]{1,0:T(8,128)} %get-tuple-element.12.total_ref), custom_call_target="tpu_custom_call" | custom-call | tf_op jit(solution)/shard_map/merge/pallas_call | solution.py:173
  43.6 3.4 %all-to-all-start.2 = ((bf16[8,64,128]{2,1,0:T(8,128)(2,1)}), bf16[8,64,128]{2,1,0:T(8,128)(2,1)S(1)}, u32[]{:S(2)}, u32[]{:S(2)}) async-start(bf16[8,64,128]{2,1,0:T(8,128)(2,1)} %merge.1), calls=%async_computation.2 | async-start | bytes 262144 | tf_op jit(solution)/shard_map/all_to_all | solution.py:289
  46.9 2.1 %relay.1 = (bf16[32,32,128]{2,1,0:T(8,128)(2,1)}, bf16[32,32,128]{2,1,0:T(8,128)(2,1)}) custom-call(s32[32]{0:T(128)} %slots_ref.1, s32[1]{0:T(128)} %bitcast.1.live_ref, bf16[16,2,2,32,128]{4,3,2,1,0:T(8,128)(2,1)} %bitcast.14), custom_call_target="tpu_custom_call" | custom-call | tf_op jit(solution)/shard_map/relay/pallas_call | solution.py:201
  49.1 5.1 %all-to-all-done.2 = bf16[8,64,128]{2,1,0:T(8,128)(2,1)S(1)} async-done(((bf16[8,64,128]{2,1,0:T(8,128)(2,1)}), bf16[8,64,128]{2,1,0:T(8,128)(2,1)S(1)}, u32[]{:S(2)}, u32[]{:S(2)}) %all-to-all-start.2) | async-done | bytes 131104 | tf_op jit(solution)/shard_map/all_to_all | solution.py:289
  54.2 0.7 %copy.13 = bf16[16,32,128]{2,1,0:T(8,128)(2,1)} copy(bf16[16,32,128]{2,1,0:T(8,128)(2,1)S(1)} %bitcast.16) | data formatting | bytes 262144
  (5 shorter events, 0.0 us)
Async XLA Ops:
  2.5 8.4 %copy-start.3 = (s32[32]{0:T(128)S(1)}, s32[32]{0:T(128)}, u32[]{:S(2)}) copy-start(s32[32]{0:T(128)} %slots_ref.1) | copy-start | bytes 388
  2.5 23.5 %all-to-all-start = ((bf16[16,2,64,128]{3,2,1,0:T(8,128)(2,1)}), bf16[16,2,64,128]{3,2,1,0:T(8,128)(2,1)S(1)}, u32[]{:S(2)}, u32[]{:S(2)}) async-start(bf16[16,2,64,128]{3,2,1,0:T(8,128)(2,1)} %bitcast.15), calls=%async_computation | async-start | bytes 1048576 | tf_op jit(solution)/shard_map/all_to_all | solution.py:236
  11.0 0.7 %copy-start.2 = (s32[16]{0:T(128)S(1)}, s32[16]{0:T(128)}, u32[]{:S(2)}) copy-start(s32[16]{0:T(128)} %param.15) | copy-start | bytes 196
  26.0 0.8 %copy-start = (bf16[16,2,64,128]{3,2,1,0:T(8,128)(2,1)}, bf16[16,2,64,128]{3,2,1,0:T(8,128)(2,1)S(1)}, u32[]{:S(2)}) copy-start(bf16[16,2,64,128]{3,2,1,0:T(8,128)(2,1)S(1)} %all-to-all-done.got_ref) | copy-start | bytes 1572868
  29.8 11.0 %all-to-all-start.1 = ((bf16[8,80,128]{2,1,0:T(8,128)(2,1)}), bf16[8,80,128]{2,1,0:T(8,128)(2,1)S(1)}, u32[]{:S(2)}, u32[]{:S(2)}) async-start(bf16[8,80,128]{2,1,0:T(8,128)(2,1)} %partial_rows.1), calls=%async_computation.1 | async-start | bytes 327680 | tf_op jit(solution)/shard_map/all_to_all | solution.py:287
  40.8 0.7 %copy-start.1 = (bf16[8,80,128]{2,1,0:T(8,128)(2,1)}, bf16[8,80,128]{2,1,0:T(8,128)(2,1)S(1)}, u32[]{:S(2)}) copy-start(bf16[8,80,128]{2,1,0:T(8,128)(2,1)S(1)} %all-to-all-done.1.got_ref) | copy-start | bytes 491524
  43.6 10.7 %all-to-all-start.2 = ((bf16[8,64,128]{2,1,0:T(8,128)(2,1)}), bf16[8,64,128]{2,1,0:T(8,128)(2,1)S(1)}, u32[]{:S(2)}, u32[]{:S(2)}) async-start(bf16[8,64,128]{2,1,0:T(8,128)(2,1)} %merge.1), calls=%async_computation.2 | async-start | bytes 262144 | tf_op jit(solution)/shard_map/all_to_all | solution.py:289

commit v2 on v1

--- a/solution.py
+++ b/solution.py
@@ -15,6 +15,7 @@
 VMEM = pl.BlockSpec(memory_space=pltpu.VMEM)
 SMEM = pl.BlockSpec(memory_space=pltpu.SMEM)
 ANY = pl.BlockSpec(memory_space=pl.ANY)
+PARAMS = pltpu.CompilerParams(vmem_limit_bytes=16 * 1024 * 1024)
 
 
 def dot_rows(a, b):
@@ -28,23 +29,17 @@
     return high, middle, rest - middle
 
 
-def pack_kernel(keys_ref, values_ref, send_ref, held, in_sems, out_sems):
-    head_count = keys_ref.shape[2]
-    pieces = [(c, h) for h in range(head_count) for c in range(2)]
-    ins = []
-    for c, h in pieces:
-        source = (keys_ref, values_ref)[c]
-        copy = pltpu.make_async_copy(source.at[:, :, h], held.at[c, h], in_sems.at[c, h])
-        copy.start()
-        ins.append(copy)
-    outs = []
-    for (c, h), copy in zip(pieces, ins):
+def pack_kernel(keys_ref, values_ref, send_ref, sems):
+    copies = []
+    for h in range(keys_ref.shape[2]):
+        for c, source in enumerate((keys_ref, values_ref)):
+            copy = pltpu.make_async_copy(
+                source.at[:, :, h], send_ref.at[h, :, c], sems.at[c, h]
+            )
+            copy.start()
+            copies.append(copy)
+    for copy in copies:
         copy.wait()
-        out = pltpu.make_async_copy(held.at[c, h], send_ref.at[h, :, c], out_sems.at[c, h])
-        out.start()
-        outs.append(out)
-    for out in outs:
-        out.wait()
 
 
 def pack(cache_keys, cache_values, seq_count, head_count):
@@ -54,13 +49,10 @@
     return pl.pallas_call(
         pack_kernel,
         out_shape=jax.ShapeDtypeStruct((head_count, seq_count, 2, rows, kv, head_dim), BF16),
-        in_specs=[ANY, ANY],
+        in_specs=[VMEM, VMEM],
         out_specs=ANY,
-        scratch_shapes=[
-            pltpu.VMEM((2, head_count, seq_count, rows, kv, head_dim), BF16),
-            pltpu.SemaphoreType.DMA((2, head_count)),
-            pltpu.SemaphoreType.DMA((2, head_count)),
-        ],
+        scratch_shapes=[pltpu.SemaphoreType.DMA((2, head_count))],
+        compiler_params=PARAMS,
         name="pack",
     )(cache_keys.reshape(split), cache_values.reshape(split))
 
@@ -112,6 +104,7 @@
             pltpu.VMEM((tokens, kv_count, group, head_dim), BF16),
             pltpu.VMEM((tokens, kv_count, group, head_dim), BF16),
         ],
+        compiler_params=PARAMS,
         name="partial_rows",
     )(query, got, bias)
 
@@ -135,6 +128,7 @@
         out_shape=(shape, shape, shape),
         in_specs=[VMEM] * 4,
         out_specs=(VMEM, VMEM, VMEM),
+        compiler_params=PARAMS,
         name="new_rows",
     )(query, keys, values, bias)
 
@@ -175,6 +169,7 @@
         out_shape=jax.ShapeDtypeStruct((seq_count,) + weighted.shape, BF16),
         in_specs=[VMEM] * 4,
         out_specs=VMEM,
+        compiler_params=PARAMS,
         name="merge",
     )(got, weighted, peak, total)
 
@@ -203,6 +198,7 @@
         out_shape=(shape, shape),
         in_specs=[SMEM, SMEM, VMEM],
         out_specs=(VMEM, VMEM),
+        compiler_params=PARAMS,
         name="relay",
     )(span_slots, live, got)
 

time: 55.5 us -> 53 us (0.955)
  Pallas kernels: 10.8 us -> 5.94 us
  waiting for transfers between devices: 22.2 us -> 26 us
  other arithmetic: 1.55 us -> 0.34 us
    all_to_all x1, waiting for transfers between devices: 11.9 us -> 13.8 us  [body(): lax.all_to_all(packed.reshape(cycle_size, 2, 2 * span_rows * kv_local, he...]
    pallas_call x1, Pallas kernels: 1.76 us -> 0.33 us  [new_rows(): pl.pallas_call(functools.partial(new_kernel, score_scale), out_shape=(sha...]
    all_to_all x1, waiting for transfers between devices: 5.1 us -> 6.51 us  [body(): lax.all_to_all(partial, 'seq', split_axis=0, concat_axis=0, tiled=True)]
    dynamic_slice x1, local copies, waits for them, and re-layouts: 1.32 us -> 0.01 us  [body(): lax.dynamic_slice_in_dim(queries.reshape(token_count * heads, head_dim),...]
    pallas_call x1, Pallas kernels: 3.07 us -> 2.01 us  [partial_rows(): pl.pallas_call(functools.partial(partial_kernel, score_scale, seq_count),...]
    unnamed x9 -> x15, local copies, waits for them, and re-layouts: 2.12 us -> 3.18 us
    pallas_call x1, Pallas kernels: 1.81 us -> 0.84 us  [pack(): pl.pallas_call(pack_kernel, out_shape=jax.ShapeDtypeStruct((head_count, s...]
    pallas_call x1, Pallas kernels: 2.07 us -> 1.13 us  [merge(): pl.pallas_call(merge_kernel, out_shape=jax.ShapeDtypeStruct((seq_count,)...]
  transfers between devices with their start and end apart: 3 -> 3, of which waited for: 3 -> 3; matrix products, arithmetic and copies ran while one was open for 6% -> 1% of each run, Pallas kernels for 7% -> 4%
where the time goes in v2:
time: 53 us; the launch traced here: 52.5 us
  waiting for transfers between devices  26 us (49%)
  starting transfers between devices  15.3 us (29%)
  Pallas kernels  5.94 us (11%)
  local copies, waits for them, and re-layouts  3.49 us (7%)
  between operations  1.45 us (3%)
    all_to_all x1, waiting for transfers between devices, body(): lax.all_to_all(packed.reshape(cycle_size, 2, 2 * span_rows * kv_local, he...  13.8 us
    all_to_all x1, starting transfers between devices, body(): lax.all_to_all(packed.reshape(cycle_size, 2, 2 * span_rows * kv_local, he...  8.48 us
    all_to_all x1, waiting for transfers between devices, body(): lax.all_to_all(partial, 'seq', split_axis=0, concat_axis=0, tiled=True)  6.51 us
    all_to_all x1, waiting for transfers between devices, body(): lax.all_to_all(merged, 'seq', split_axis=0, concat_axis=0, tiled=True)  5.65 us
    all_to_all x1, starting transfers between devices, body(): lax.all_to_all(partial, 'seq', split_axis=0, concat_axis=0, tiled=True)  3.43 us
    all_to_all x1, starting transfers between devices, body(): lax.all_to_all(merged, 'seq', split_axis=0, concat_axis=0, tiled=True)  3.37 us
    unnamed x15, local copies, waits for them, and re-layouts  3.18 us
    pallas_call x1, Pallas kernels, partial_rows(): pl.pallas_call(functools.partial(partial_kernel, score_scale, seq_count),...  2.01 us
  transfers between devices with their start and end apart: 3, of which 3 were waited for; matrix products, arithmetic and copies ran while one was open for 1% of the time, Pallas kernels for 4%

profile of v2, /device:TPU:0, one launch (start us, length us, event | category | flops | bytes accessed | tf_op | source)
XLA Modules:
  0.0 52.5 jit_solution(17290112011349950546)
XLA Ops:
  0.6 0.0 copy-start
  0.6 0.9 %copy-done = bf16[256,4,128]{2,1,0:T(4,128)(2,1)S(1)} copy-done((bf16[256,4,128]{2,1,0:T(4,128)(2,1)S(1)}, bf16[256,4,128]{2,1,0:T(4,128)(2,1)}, u32[]{:S(2)}) %copy-start) | copy-done | bytes 262168
  1.6 0.9 %copy-done.1 = bf16[256,4,128]{2,1,0:T(4,128)(2,1)S(1)} copy-done((bf16[256,4,128]{2,1,0:T(4,128)(2,1)S(1)}, bf16[256,4,128]{2,1,0:T(4,128)(2,1)}, u32[]{:S(2)}) %copy-start.1) | copy-done | bytes 262168
  2.5 0.8 %pack.1 = bf16[2,8,2,32,2,128]{5,4,3,2,1,0:T(2,128)(2,1)} custom-call(bf16[8,32,2,2,128]{4,3,2,1,0:T(2,128)(2,1)S(1)} %bitcast.15, bf16[8,32,2,2,128]{4,3,2,1,0:T(2,128)(2,1)S(1)} %bitcast.16), custom_call_target="tpu_custom_call" | custom-call | tf_op jit(solution)/shard_map/pack/pallas_call | solution.py:49
  3.4 0.0 copy-start.5
  3.4 0.0 copy-start.2
  3.4 8.5 %all-to-all-start = ((bf16[16,2,64,128]{3,2,1,0:T(8,128)(2,1)}), bf16[16,2,64,128]{3,2,1,0:T(8,128)(2,1)S(1)}, u32[]{:S(2)}, u32[]{:S(2)}) async-start(bf16[16,2,64,128]{3,2,1,0:T(8,128)(2,1)} %bitcast.4), calls=%async_computation | async-start | bytes 1048576 | tf_op jit(solution)/shard_map/all_to_all | solution.py:232
  11.9 0.0 copy-done.5
  11.9 0.1 select_reduce_fusion
  12.0 0.0 copy-start.6
  12.7 0.0 copy-done.6
  12.7 0.1 broadcast_in_dim.66
  12.8 0.1 le.15
  12.9 0.1 broadcast_in_dim.63
  12.9 0.1 reshape.147
  13.1 0.0 copy-done.2
  13.1 0.1 select_reduce_fusion.1
  13.2 13.8 %all-to-all-done.got_ref = bf16[16,2,64,128]{3,2,1,0:T(8,128)(2,1)S(1)} async-done(((bf16[16,2,64,128]{3,2,1,0:T(8,128)(2,1)}), bf16[16,2,64,128]{3,2,1,0:T(8,128)(2,1)S(1)}, u32[]{:S(2)}, u32[]{:S(2)}) %all-to-all-start) | async-done | bytes 524320 | tf_op jit(solution)/shard_map/all_to_all | solution.py:232
  27.0 2.0 %partial_rows.1 = bf16[8,80,128]{2,1,0:T(8,128)(2,1)} custom-call(bf16[16,32,128]{2,1,0:T(8,128)(2,1)S(1)} %copy-done.2, bf16[16,2,64,128]{3,2,1,0:T(8,128)(2,1)S(1)} %all-to-all-done.got_ref, f32[2,1024]{1,0:T(2,128)S(1)} %and_select_fusion.1.bias_ref), custom_call_target="tpu_custom_call" | custom-call | tf_op jit(solution)/shard_map/partial_rows/pallas_call | solution.py:98
  29.0 3.4 %all-to-all-start.1 = ((bf16[8,80,128]{2,1,0:T(8,128)(2,1)}), bf16[8,80,128]{2,1,0:T(8,128)(2,1)S(1)}, u32[]{:S(2)}, u32[]{:S(2)}) async-start(bf16[8,80,128]{2,1,0:T(8,128)(2,1)} %partial_rows.1), calls=%async_computation.1 | async-start | bytes 327680 | tf_op jit(solution)/shard_map/all_to_all | solution.py:283
  32.5 0.0 copy-start.3
  32.5 0.0 copy-start.4
  32.5 0.1 and_select_fusion.bias_ref
  32.6 0.6 %copy-done.3 = bf16[16,2,128]{2,1,0:T(2,128)(2,1)S(1)} copy-done((bf16[16,2,128]{2,1,0:T(2,128)(2,1)S(1)}, bf16[16,2,128]{2,1,0:T(2,128)(2,1)}, u32[]{:S(2)}) %copy-start.3) | copy-done | bytes 8216
  33.2 0.0 copy-done.4
  33.2 0.3 new_rows.1
  33.5 6.5 %all-to-all-done.1.got_ref = bf16[8,80,128]{2,1,0:T(8,128)(2,1)S(1)} async-done(((bf16[8,80,128]{2,1,0:T(8,128)(2,1)}), bf16[8,80,128]{2,1,0:T(8,128)(2,1)S(1)}, u32[]{:S(2)}, u32[]{:S(2)}) %all-to-all-start.1) | async-done | bytes 163872 | tf_op jit(solution)/shard_map/all_to_all | solution.py:283
  40.0 1.1 %merge.1 = bf16[8,64,128]{2,1,0:T(8,128)(2,1)} custom-call(bf16[8,80,128]{2,1,0:T(8,128)(2,1)S(1)} %all-to-all-done.1.got_ref, f32[64,128]{1,0:T(8,128)S(1)} %get-tuple-element.10.weighted_ref, f32[64,128]{1,0:T(8,128)S(1)} %get-tuple-element.11.peak_ref, f32[64,128]{1,0:T(8,128)S(1)} %get-tuple-element.12.total_ref), custom_call_target="tpu_custom_call" | custom-call | tf_op jit(solution)/shard_map/merge/pallas_call | solution.py:167
  41.2 3.4 %all-to-all-start.2 = ((bf16[8,64,128]{2,1,0:T(8,128)(2,1)}), bf16[8,64,128]{2,1,0:T(8,128)(2,1)S(1)}, u32[]{:S(2)}, u32[]{:S(2)}) async-start(bf16[8,64,128]{2,1,0:T(8,128)(2,1)} %merge.1), calls=%async_computation.2 | async-start | bytes 262144 | tf_op jit(solution)/shard_map/all_to_all | solution.py:285
  44.6 1.6 %relay.1 = (bf16[32,32,128]{2,1,0:T(8,128)(2,1)}, bf16[32,32,128]{2,1,0:T(8,128)(2,1)}) custom-call(s32[32]{0:T(128)S(1)} %copy-done.5, s32[1]{0:T(128)} %bitcast.1.live_ref, bf16[16,2,2,32,128]{4,3,2,1,0:T(8,128)(2,1)S(1)} %bitcast.14), custom_call_target="tpu_custom_call" | custom-call | tf_op jit(solution)/shard_map/relay/pallas_call | solution.py:196
  46.2 5.7 %all-to-all-done.2 = bf16[8,64,128]{2,1,0:T(8,128)(2,1)S(1)} async-done(((bf16[8,64,128]{2,1,0:T(8,128)(2,1)}), bf16[8,64,128]{2,1,0:T(8,128)(2,1)S(1)}, u32[]{:S(2)}, u32[]{:S(2)}) %all-to-all-start.2) | async-done | bytes 131104 | tf_op jit(solution)/shard_map/all_to_all | solution.py:285
  51.8 0.7 %copy.13 = bf16[16,32,128]{2,1,0:T(8,128)(2,1)} copy(bf16[16,32,128]{2,1,0:T(8,128)(2,1)S(1)} %bitcast.20) | data formatting | bytes 262144
  (8 shorter events, 0.1 us)
Async XLA Ops:
  0.6 1.0 %copy-start = (bf16[256,4,128]{2,1,0:T(4,128)(2,1)S(1)}, bf16[256,4,128]{2,1,0:T(4,128)(2,1)}, u32[]{:S(2)}) copy-start(bf16[256,4,128]{2,1,0:T(4,128)(2,1)} %param.8) | copy-start | bytes 786436
  1.6 0.9 %copy-start.1 = (bf16[256,4,128]{2,1,0:T(4,128)(2,1)S(1)}, bf16[256,4,128]{2,1,0:T(4,128)(2,1)}, u32[]{:S(2)}) copy-start(bf16[256,4,128]{2,1,0:T(4,128)(2,1)} %param.9) | copy-start | bytes 786436
  3.4 8.5 %copy-start.5 = (s32[32]{0:T(128)S(1)}, s32[32]{0:T(128)}, u32[]{:S(2)}) copy-start(s32[32]{0:T(128)} %slots_ref.1) | copy-start | bytes 388
  3.4 9.7 %copy-start.2 = (bf16[16,32,128]{2,1,0:T(8,128)(2,1)S(1)}, bf16[16,32,128]{2,1,0:T(8,128)(2,1)}, u32[]{:S(2)}) copy-start(bf16[16,32,128]{2,1,0:T(8,128)(2,1)} %query_ref.1) | copy-start | bytes 393220
  3.4 23.6 %all-to-all-start = ((bf16[16,2,64,128]{3,2,1,0:T(8,128)(2,1)}), bf16[16,2,64,128]{3,2,1,0:T(8,128)(2,1)S(1)}, u32[]{:S(2)}, u32[]{:S(2)}) async-start(bf16[16,2,64,128]{3,2,1,0:T(8,128)(2,1)} %bitcast.4), calls=%async_computation | async-start | bytes 1048576 | tf_op jit(solution)/shard_map/all_to_all | solution.py:232
  12.0 0.7 %copy-start.6 = (s32[16]{0:T(128)S(1)}, s32[16]{0:T(128)}, u32[]{:S(2)}) copy-start(s32[16]{0:T(128)} %param.15) | copy-start | bytes 196
  29.0 11.0 %all-to-all-start.1 = ((bf16[8,80,128]{2,1,0:T(8,128)(2,1)}), bf16[8,80,128]{2,1,0:T(8,128)(2,1)S(1)}, u32[]{:S(2)}, u32[]{:S(2)}) async-start(bf16[8,80,128]{2,1,0:T(8,128)(2,1)} %partial_rows.1), calls=%async_computation.1 | async-start | bytes 327680 | tf_op jit(solution)/shard_map/all_to_all | solution.py:283
  32.5 0.7 %copy-start.3 = (bf16[16,2,128]{2,1,0:T(2,128)(2,1)S(1)}, bf16[16,2,128]{2,1,0:T(2,128)(2,1)}, u32[]{:S(2)}) copy-start(bf16[16,2,128]{2,1,0:T(2,128)(2,1)} %param.13) | copy-start | bytes 24580
  32.5 0.7 %copy-start.4 = (bf16[16,2,128]{2,1,0:T(2,128)(2,1)S(1)}, bf16[16,2,128]{2,1,0:T(2,128)(2,1)}, u32[]{:S(2)}) copy-start(bf16[16,2,128]{2,1,0:T(2,128)(2,1)} %param.14) | copy-start | bytes 24580
  41.2 10.7 %all-to-all-start.2 = ((bf16[8,64,128]{2,1,0:T(8,128)(2,1)}), bf16[8,64,128]{2,1,0:T(8,128)(2,1)S(1)}, u32[]{:S(2)}, u32[]{:S(2)}) async-start(bf16[8,64,128]{2,1,0:T(8,128)(2,1)} %merge.1), calls=%async_computation.2 | async-start | bytes 262144 | tf_op jit(solution)/shard_map/all_to_all | solution.py:285

commit v3 on v1

v3 whole, which is shorter than its diff:
```python
import functools
import math

import jax
import jax.numpy as jnp
from jax import lax
from jax.experimental import pallas as pl
from jax.experimental.pallas import tpu as pltpu
from jax.sharding import PartitionSpec as P


BF16 = jnp.bfloat16
F32 = jnp.float32
DEAD = -1e30
STAT_ROWS = 16
LANES = 128
VMEM = pl.BlockSpec(memory_space=pltpu.VMEM)
SMEM = pl.BlockSpec(memory_space=pltpu.SMEM)
HBM = pl.BlockSpec(memory_space=pltpu.HBM)
PARAMS = pltpu.CompilerParams(vmem_limit_bytes=16 * 1024 * 1024)


def dot_rows(a, b):
    return lax.dot_general(a, b, (((1,), (1,)), ((), ())), preferred_element_type=F32)


def three_parts(x):
    high = x.astype(BF16).astype(F32)
    rest = x - high
    middle = rest.astype(BF16).astype(F32)
    return [high, middle, rest - middle]


def stacked(parts, like):
    row = lax.broadcasted_iota(jnp.int32, like, 0)
    out = jnp.zeros(like, F32)
    for at, part in enumerate(parts):
        out = jnp.where(row == at, part, out)
    return out.astype(BF16)


def eye(rows, columns):
    return (
        lax.broadcasted_iota(jnp.int32, (rows, columns), 0)
        == lax.broadcasted_iota(jnp.int32, (rows, columns), 1)
    ).astype(F32).astype(BF16)


def pack_kernel(head_index_ref, keys_ref, values_ref, send_ref, mine_ref, away_ref, held, in_sems, out_sems, mine_sems, away_sems):
    head_count = keys_ref.shape[2]
    me = head_index_ref[0]
    ins = {}
    for shift in list(range(1, head_count)) + [0]:
        h = lax.rem(me + shift, head_count)
        for c, source in enumerate((keys_ref, values_ref)):
            copy = pltpu.make_async_copy(source.at[:, :, h], held.at[shift, c], in_sems.at[shift, c])
            copy.start()
            ins[shift, c] = copy
    outs = []
    for (shift, c), copy in ins.items():
        copy.wait()
        h = lax.rem(me + shift, head_count)
        block = held.at[shift, c]
        if shift:
            outs.append(pltpu.make_async_copy(block, away_ref.at[shift - 1, c], away_sems.at[shift - 1, c]))
        else:
            outs.append(pltpu.make_async_copy(block, mine_ref.at[c], mine_sems.at[c]))
        outs[-1].start()
        outs.append(pltpu.make_async_copy(block, send_ref.at[h, :, c], out_sems.at[shift, c]))
        outs[-1].start()
    for out in outs:
        out.wait()


def pack(head_index, cache_keys, cache_values, seq_count, head_count):
    row_count, kv_all, head_dim = cache_keys.shape
    split = (seq_count, row_count // seq_count, head_count, kv_all // head_count, head_dim)
    rows, kv = split[1], split[3]
    block = (seq_count, rows, kv, head_dim)
    return pl.pallas_call(
        pack_kernel,
        out_shape=(
            jax.ShapeDtypeStruct((head_count, seq_count, 2, rows, kv, head_dim), BF16),
            jax.ShapeDtypeStruct((2,) + block, BF16),
            jax.ShapeDtypeStruct((head_count - 1, 2) + block, BF16),
        ),
        in_specs=[SMEM, HBM, HBM],
        out_specs=(HBM, VMEM, HBM),
        scratch_shapes=[
            pltpu.VMEM((head_count, 2) + block, BF16),
            pltpu.SemaphoreType.DMA((head_count, 2)),
            pltpu.SemaphoreType.DMA((head_count, 2)),
            pltpu.SemaphoreType.DMA((2,)),
            pltpu.SemaphoreType.DMA((head_count - 1, 2)),
        ],
        name="pack",
    )(head_index, cache_keys.reshape(split), cache_values.reshape(split))


def attend_kernel(score_scale, query_ref, new_keys_ref, new_values_ref, new_bias_ref, bias_ref, *rest):
    *block_refs, out_ref, rows_buf, stat_buf = rest
    tokens, heads, head_dim = query_ref.shape
    kv_count = bias_ref.shape[0]
    group = heads // kv_count
    lane = lax.broadcasted_iota(jnp.int32, (tokens * group, head_dim), 1)
    keys = jnp.concatenate([ref[0] for ref in block_refs], axis=0)
    values = jnp.concatenate([ref[1] for ref in block_refs], axis=0)
    for g in range(kv_count):
        query = query_ref[:, g * group : (g + 1) * group, :].reshape(tokens * group, head_dim)
        scores = dot_rows(query, keys) * score_scale + bias_ref[g : g + 1, :]
        fresh = dot_rows(query, new_keys_ref[...]) * score_scale + new_bias_ref[g]
        peak = jnp.maximum(
            jnp.max(scores, axis=1, keepdims=True), jnp.max(fresh, axis=1, keepdims=True)
        )
        weights = jnp.exp(scores - peak)
        fresh = jnp.exp(fresh - peak)
        total = jnp.sum(weights, axis=1, keepdims=True) + jnp.sum(fresh, axis=1, keepdims=True)
        weighted = jnp.dot(weights.astype(BF16), values, preferred_element_type=F32)
        weighted = weighted + jnp.dot(
            fresh.astype(BF16), new_values_ref[...], preferred_element_type=F32
        )
        stats = jnp.zeros((tokens * group, head_dim), F32)
        for at, part in enumerate(three_parts(peak) + three_parts(total)):
            stats = jnp.where(lane == at, part, stats)
        rows_buf[:, g] = weighted.astype(BF16).reshape(tokens, group, head_dim)
        stat_buf[:, g] = stats.astype(BF16).reshape(tokens, group, head_dim)
    count = tokens * heads
    out_ref[:count, :] = rows_buf[...].reshape(count, head_dim)
    turned = dot_rows(eye(STAT_ROWS, head_dim), stat_buf[...].reshape(count, head_dim))
    for at in range(count // LANES):
        start = count + at * STAT_ROWS
        out_ref[start : start + STAT_ROWS, :] = turned[:, at * LANES : (at + 1) * LANES].astype(BF16)


def attend(query, new_keys, new_values, new_bias, bias, blocks, score_scale):
    tokens, heads, head_dim = query.shape
    kv_count = bias.shape[0]
    group = heads // kv_count
    count = tokens * heads
    return pl.pallas_call(
        functools.partial(attend_kernel, score_scale),
        out_shape=jax.ShapeDtypeStruct((count + count // LANES * STAT_ROWS, head_dim), BF16),
        in_specs=[VMEM] * (5 + len(blocks)),
        out_specs=VMEM,
        scratch_shapes=[
            pltpu.VMEM((tokens, kv_count, group, head_dim), BF16),
            pltpu.VMEM((tokens, kv_count, group, head_dim), BF16),
        ],
        compiler_params=PARAMS,
        name="attend",
    )(query, new_keys, new_values, new_bias, bias, *blocks)


def merge_kernel(last, one_ref, two_ref, out_ref):
    head_dim = one_ref.shape[1]
    count = one_ref.shape[0] * LANES // (LANES + STAT_ROWS)
    turn = eye(LANES, LANES)
    for at in range(count // LANES):
        start = count + at * STAT_ROWS
        peaks, totals = [], []
        for ref in (one_ref, two_ref):
            stats = ref[start : start + STAT_ROWS, :].astype(F32)
            peaks.append(stats[0:1] + stats[1:2] + stats[2:3])
            totals.append(stats[3:4] + stats[4:5] + stats[5:6])
        peak = jnp.maximum(*peaks)
        factors = [jnp.exp(p - peak) for p in peaks]
        total = factors[0] * totals[0] + factors[1] * totals[1]
        if last:
            factors = [f / total for f in factors]
        else:
            out_ref[start : start + STAT_ROWS, :] = stacked(
                three_parts(peak) + three_parts(total), (STAT_ROWS, LANES)
            )
        columns = dot_rows(
            turn, stacked(three_parts(factors[0]) + three_parts(factors[1]), (STAT_ROWS, LANES))
        )
        result = None
        for k, ref in enumerate((one_ref, two_ref)):
            column = columns[:, 3 * k : 3 * k + 1] + columns[:, 3 * k + 1 : 3 * k + 2]
            column = jnp.broadcast_to(column + columns[:, 3 * k + 2 : 3 * k + 3], (LANES, head_dim))
            term = ref[at * LANES : (at + 1) * LANES, :].astype(F32) * column
            result = term if result is None else result + term
        out_ref[at * LANES : (at + 1) * LANES, :] = result.astype(BF16)


def merge(one, two, last):
    rows, head_dim = one.shape
    if last:
        rows = rows * LANES // (LANES + STAT_ROWS)
    return pl.pallas_call(
        functools.partial(merge_kernel, last),
        out_shape=jax.ShapeDtypeStruct((rows, head_dim), BF16),
        in_specs=[VMEM, VMEM],
        out_specs=VMEM,
        compiler_params=PARAMS,
        name="merge",
    )(one, two)


def relay_kernel(slots_ref, live_ref, got_ref, keys_ref, values_ref):
    slot_count, span, head_dim = keys_ref.shape
    row = lax.broadcasted_iota(jnp.int32, (span, head_dim), 0)
    live = live_ref[0]

    def one(t, carry):
        slot = slots_ref[t]
        kept = row < live - t * span
        for c, out_ref in enumerate((keys_ref, values_ref)):
            block = got_ref[slot // 2, c, slot % 2].astype(F32)
            out_ref[t] = jnp.where(kept, block, 0.0).astype(BF16)
        return carry

    lax.fori_loop(0, slot_count, one, 0, unroll=4)


def relay(span_slots, live, got):
    _, _, _, span, head_dim = got.shape
    shape = jax.ShapeDtypeStruct((span_slots.shape[0], span, head_dim), BF16)
    return pl.pallas_call(
        relay_kernel,
        out_shape=(shape, shape),
        in_specs=[SMEM, SMEM, VMEM],
        out_specs=(VMEM, VMEM),
        compiler_params=PARAMS,
        name="relay",
    )(span_slots, live, got)


def step(
    cache_keys,
    cache_values,
    span_slots,
    prompt_length,
    queries,
    new_keys,
    new_values,
    decode_offsets,
):
    row_count, kv_all, head_dim = cache_keys.shape
    seq_count = lax.axis_size("seq")
    head_count = lax.axis_size("head")
    cycle_size = seq_count * head_count
    slot_count = span_slots.shape[0]
    span_rows = row_count // (2 * seq_count)
    kv_local = kv_all // head_count
    token_count, heads, _ = queries.shape
    group_size = heads // kv_local
    length = prompt_length[0]
    score_scale = 1.0 / math.sqrt(head_dim)
    shard_rows = slot_count * span_rows
    seq_index = lax.axis_index("seq")
    head_index = lax.axis_index("head")
    shard_start = seq_index * shard_rows

    packed, mine, away = pack(
        head_index.reshape(1), cache_keys, cache_values, seq_count, head_count
    )
    flat = (2, row_count * kv_local, head_dim)
    blocks = [mine.reshape(flat)]
    for shift in range(1, head_count):
        blocks.append(
            lax.ppermute(
                away[shift - 1].reshape(flat),
                "head",
                [(h, (h + shift) % head_count) for h in range(head_count)],
            )
        )
    got = lax.all_to_all(
        packed.reshape(cycle_size, 2, 2 * span_rows * kv_local, head_dim),
        ("head", "seq"),
        split_axis=0,
        concat_axis=0,
        tiled=True,
    )

    columns = (head_count, seq_count, 2, span_rows, kv_local)

    def index_of(axis):
        return lax.broadcasted_iota(jnp.int32, columns, axis).reshape(head_count, -1)

    source = lax.rem(head_index - index_of(0) + head_count, head_count) * seq_count + seq_index
    slot = 2 * source + index_of(2)
    spans = jnp.arange(slot_count, dtype=jnp.int32)
    wanted = 2 * (
        lax.rem(head_index - jnp.arange(head_count, dtype=jnp.int32) + head_count, head_count)
        * seq_count
        + seq_index
    )
    place = [
        jnp.sum(jnp.where(span_slots[None, :] == (wanted + k)[:, None], spans[None, :], 0), axis=1)
        for k in range(2)
    ]
    span_at = jnp.where(index_of(2) == 0, place[0][:, None], place[1][:, None])
    position = (index_of(1) * slot_count + span_at) * span_rows + index_of(3)
    alive = (position < length).reshape(-1)
    column_kv = index_of(4).reshape(-1)
    kv_range = jnp.arange(kv_local, dtype=jnp.int32)
    bias = jnp.where(
        alive[None, :] & (column_kv[None, :] == kv_range[:, None]), 0.0, DEAD
    ).astype(F32)

    shape = (kv_local, token_count, group_size, token_count * kv_local)
    new_kv = lax.broadcasted_iota(jnp.int32, shape, 3) % kv_local
    new_depth = jnp.broadcast_to(decode_offsets[:, None], (token_count, kv_local)).reshape(-1)
    seen = (
        (new_depth[None, None, None, :] <= decode_offsets[None, :, None, None])
        & (new_kv == lax.broadcasted_iota(jnp.int32, shape, 0))
        & (seq_index == 0)
    )
    new_bias = jnp.where(seen, 0.0, DEAD).astype(F32)
    state = attend(
        queries,
        new_keys.reshape(token_count * kv_local, head_dim),
        new_values.reshape(token_count * kv_local, head_dim),
        new_bias.reshape(kv_local, token_count * group_size, token_count * kv_local),
        bias,
        blocks,
        score_scale,
    )
    stride = 1
    while stride < seq_count:
        last = 2 * stride >= seq_count
        other = lax.ppermute(state, "seq", [(s, s ^ stride) for s in range(seq_count)])
        state = merge(state, other, last)
        stride *= 2

    live = jnp.clip(length - shard_start, 0, shard_rows) * kv_local
    relaid_keys, relaid_values = relay(
        span_slots,
        live.reshape(1),
        got.reshape(cycle_size, 2, 2, span_rows * kv_local, head_dim),
    )
    whole = (shard_rows, kv_local, head_dim)
    return (
        relaid_keys.reshape(whole),
        relaid_values.reshape(whole),
        state.reshape(token_count, heads, head_dim),
    )


def solution(mesh):
    return jax.shard_map(
        step,
        mesh=mesh,
        in_specs=(
            P(("rep", "head", "seq"), None, None),
            P(("rep", "head", "seq"), None, None),
            P("rep"),
            P("rep"),
            P("rep", "head", None),
            P("rep", "head", None),
            P("rep", "head", None),
            P("rep"),
        ),
        out_specs=(
            P(("rep", "seq"), "head", None),
            P(("rep", "seq"), "head", None),
            P("rep", "head", None),
        ),
        check_vma=False,
    )
```

time: 55.5 us -> 48.7 us (0.88)
  waiting for transfers between devices: 22.2 us -> 19 us
  Pallas kernels: 10.8 us -> 8.1 us
  starting transfers between devices: 15.2 us -> 17.2 us
  local copies, waits for them, and re-layouts: 3.75 us -> 2.32 us
  other arithmetic: 1.55 us -> 0.41 us
    all_to_all x3 -> x1, waiting for transfers between devices: 22.2 us -> 0.01 us  [step(): lax.all_to_all(packed.reshape(cycle_size, 2, 2 * span_rows * kv_local, he...]
    ppermute x0 -> x4, waiting for transfers between devices: none -> 19 us  [the longest x3 11.7 us: step(): lax.ppermute(state, 'seq', [(s, s ^ stride) for s in range(seq_count)])]
    ppermute x0 -> x4, starting transfers between devices: none -> 8.68 us  [the longest x3 6.69 us: step(): lax.ppermute(state, 'seq', [(s, s ^ stride) for s in range(seq_count)])]
    all_to_all x3 -> x1, starting transfers between devices: 15.2 us -> 8.48 us  [step(): lax.all_to_all(packed.reshape(cycle_size, 2, 2 * span_rows * kv_local, he...]
    pallas_call x4 -> x5, Pallas kernels: 8.71 us -> 6.47 us  [the longest x1 2.81 us: pack(): pl.pallas_call(pack_kernel, out_shape=(jax.ShapeDtypeStruct((head_count,...]
    dynamic_slice x1 -> x0, local copies, waits for them, and re-layouts: 1.32 us -> none  [body(): lax.dynamic_slice_in_dim(queries.reshape(token_count * heads, head_dim),...]
    select_n x5 -> x2, other arithmetic: 1.34 us -> 0.06 us  [the longest x1 0.04 us: step(): new_bias = jnp.where(seen, 0.0, DEAD).astype(F32)]
    unnamed x9 -> x17, local copies, waits for them, and re-layouts: 2.12 us -> 1.41 us
  transfers between devices with their start and end apart: 3 -> 5, of which waited for: 3 -> 4; matrix products, arithmetic and copies ran while one was open for 6% -> 3% of each run, Pallas kernels for 7% -> 8%
where the time goes in v3:
time: 48.7 us; the launch traced here: 48.5 us
  waiting for transfers between devices  19 us (39%)
  starting transfers between devices  17.2 us (35%)
  Pallas kernels  8.1 us (17%)
  local copies, waits for them, and re-layouts  2.32 us (5%)
  between operations  1.46 us (3%)
    ppermute x3, waiting for transfers between devices, step(): lax.ppermute(state, 'seq', [(s, s ^ stride) for s in range(seq_count)])  11.7 us
    all_to_all x1, starting transfers between devices, step(): lax.all_to_all(packed.reshape(cycle_size, 2, 2 * span_rows * kv_local, he...  8.48 us
    ppermute x1, waiting for transfers between devices, step(): lax.ppermute(away[shift - 1].reshape(flat), 'head', [(h, (h + shift) % he...  7.31 us
    ppermute x3, starting transfers between devices, step(): lax.ppermute(state, 'seq', [(s, s ^ stride) for s in range(seq_count)])  6.69 us
    pallas_call x1, Pallas kernels, pack(): pl.pallas_call(pack_kernel, out_shape=(jax.ShapeDtypeStruct((head_count,...  2.81 us
    pallas_call x3, Pallas kernels, merge(): pl.pallas_call(functools.partial(merge_kernel, last), out_shape=jax.Shape...  2.21 us
    ppermute x1, starting transfers between devices, step(): lax.ppermute(away[shift - 1].reshape(flat), 'head', [(h, (h + shift) % he...  1.99 us
    pallas_call x1, Pallas kernels, relay(): pl.pallas_call(relay_kernel, out_shape=(shape, shape), in_specs=[SMEM, SM...  1.62 us
  transfers between devices with their start and end apart: 5, of which 4 were waited for; matrix products, arithmetic and copies ran while one was open for 3% of the time, Pallas kernels for 8%

profile of v3, /device:TPU:0, one launch (start us, length us, event | category | flops | bytes accessed | tf_op | source)
XLA Modules:
  0.0 48.5 jit_solution(5215436122107078298)
XLA Ops:
  0.6 2.8 %pack.1 = (bf16[2,8,2,32,2,128]{5,4,3,2,1,0:T(2,128)(2,1)}, bf16[2,8,32,2,128]{4,3,2,1,0:T(2,128)(2,1)}, bf16[1,2,8,32,2,128]{5,4,3,2,1,0:T(2,128)(2,1)}) custom-call(s32[1]{0:T(128)} %bitcast.2.head_index_ref, bf16[8,32,2,2,128]{4,3,2,1,0:T(2,128)(2,1)} %bitcast.36, bf16[8,32,2,2,128]{4,3,2,1,0:T(2,128)(2,1)} %bitcast.37), custom_call_target="tpu_custom_call" | custom-call | tf_op jit(solution)/shard_map/pack/pallas_call | solution.py:80
  3.4 0.0 copy-start.6
  3.5 8.5 %all-to-all-start = ((bf16[16,2,64,128]{3,2,1,0:T(8,128)(2,1)}), bf16[16,2,64,128]{3,2,1,0:T(8,128)(2,1)S(1)}, u32[]{:S(2)}, u32[]{:S(2)}) async-start(bf16[16,2,64,128]{3,2,1,0:T(8,128)(2,1)} %bitcast.35), calls=%async_computation | async-start | bytes 1048576 | tf_op jit(solution)/shard_map/all_to_all | solution.py:268
  12.0 2.0 %collective-permute-start = (bf16[2,512,128]{2,1,0:T(8,128)(2,1)S(1)}, bf16[2,512,128]{2,1,0:T(8,128)(2,1)S(1)}, u32[]{:S(2)}, u32[]{:S(2)}) collective-permute-start(bf16[2,512,128]{2,1,0:T(8,128)(2,1)S(1)} %bitcast.42), channel_id=1, source_target_pairs={{0,16},{16,0},{1,17},{17,1},{2,18},{18,2},{3,19},{19,3},{4,20},{20... | collective-permute-start | bytes 786440 | tf_op jit(solution)/shard_map/ppermute | solution.py:262
  14.7 0.0 copy-start.5
  14.7 0.6 %copy-done.5 = s32[16]{0:T(128)S(1)} copy-done((s32[16]{0:T(128)S(1)}, s32[16]{0:T(128)}, u32[]{:S(2)}) %copy-start.5) | copy-done | bytes 88
  15.3 0.1 broadcast_in_dim.70
  15.4 0.1 le.20
  15.5 0.2 reshape.151
  15.7 0.2 mul.53
  15.8 0.2 eq.65
  16.0 0.0 copy-start.4
  16.1 0.6 %copy-done.4 = s32[32]{0:T(128)S(1)} copy-done((s32[32]{0:T(128)S(1)}, s32[32]{0:T(128)}, u32[]{:S(2)}) %copy-start.4) | copy-done | bytes 152
  16.7 0.2 fusion.4
  16.9 0.1 broadcast_bitcast_fusion
  17.0 0.0 copy-start
  17.0 0.2 eq.71
  17.2 0.1 broadcast_compare_fusion
  17.3 0.0 copy-start.1
  17.4 0.0 copy-start.2
  17.4 7.3 %collective-permute-done.rest_1_ = bf16[2,512,128]{2,1,0:T(8,128)(2,1)S(1)} collective-permute-done((bf16[2,512,128]{2,1,0:T(8,128)(2,1)S(1)}, bf16[2,512,128]{2,1,0:T(8,128)(2,1)S(1)}, u32[]{:S(2)}, u32[]{:S(2)}) %collective-permute-start) | collective-permute-done | bytes 262176 | tf_op jit(solution)/shard_map/ppermute | solution.py:262
  24.8 1.5 %attend.1.one_ref = bf16[576,128]{1,0:T(8,128)(2,1)S(1)} custom-call(bf16[16,32,128]{2,1,0:T(8,128)(2,1)S(1)} %copy-done.1, bf16[32,128]{1,0:T(8,128)(2,1)S(1)} %bitcast.33, bf16[32,128]{1,0:T(8,128)(2,1)S(1)} %bitcast.34, f32[2,256,32]{2,1,0:T(8,128)S(1)} %fusion.2.new_bias_ref, f32[2,1024]{1,0:T(2,128)S(1)} %and_select_fusion.bias_ref, ...), custom_call_target="tpu_custom_call" | custom-call | tf_op jit(solution)/shard_map/attend/pallas_call | solution.py:140
  26.2 1.5 %collective-permute-start.1 = (bf16[576,128]{1,0:T(8,128)(2,1)S(1)}, bf16[576,128]{1,0:T(8,128)(2,1)S(1)}, u32[]{:S(2)}, u32[]{:S(2)}) collective-permute-start(bf16[576,128]{1,0:T(8,128)(2,1)S(1)} %attend.1.one_ref), channel_id=1, source_target_pairs={{0,2},{2,0},{4,6},{6,4},{8,10},{10,8},{12,14},{14,12},{1,3},{3,1},... | collective-permute-start | bytes 442376 | tf_op jit(solution)/shard_map/ppermute | solution.py:323
  27.8 3.7 %collective-permute-done.1.two_ref = bf16[576,128]{1,0:T(8,128)(2,1)S(1)} collective-permute-done((bf16[576,128]{1,0:T(8,128)(2,1)S(1)}, bf16[576,128]{1,0:T(8,128)(2,1)S(1)}, u32[]{:S(2)}, u32[]{:S(2)}) %collective-permute-start.1) | collective-permute-done | bytes 147488 | tf_op jit(solution)/shard_map/ppermute | solution.py:323
  31.4 0.5 %merge.3.one_ref = bf16[576,128]{1,0:T(8,128)(2,1)S(1)} custom-call(bf16[576,128]{1,0:T(8,128)(2,1)S(1)} %attend.1.one_ref, bf16[576,128]{1,0:T(8,128)(2,1)S(1)} %collective-permute-done.1.two_ref), custom_call_target="tpu_custom_call" | custom-call | tf_op jit(solution)/shard_map/merge/pallas_call | solution.py:190
  32.0 1.9 %collective-permute-start.2 = (bf16[576,128]{1,0:T(8,128)(2,1)S(1)}, bf16[576,128]{1,0:T(8,128)(2,1)S(1)}, u32[]{:S(2)}, u32[]{:S(2)}) collective-permute-start(bf16[576,128]{1,0:T(8,128)(2,1)S(1)} %merge.3.one_ref), channel_id=1, source_target_pairs={{0,4},{2,6},{4,0},{6,2},{8,12},{10,14},{12,8},{14,10},{1,5},{3,7},... | collective-permute-start | bytes 442376 | tf_op jit(solution)/shard_map/ppermute | solution.py:323
  33.8 3.3 %collective-permute-done.2.two_ref = bf16[576,128]{1,0:T(8,128)(2,1)S(1)} collective-permute-done((bf16[576,128]{1,0:T(8,128)(2,1)S(1)}, bf16[576,128]{1,0:T(8,128)(2,1)S(1)}, u32[]{:S(2)}, u32[]{:S(2)}) %collective-permute-start.2) | collective-permute-done | bytes 147488 | tf_op jit(solution)/shard_map/ppermute | solution.py:323
  37.2 0.5 %merge.4.one_ref = bf16[576,128]{1,0:T(8,128)(2,1)S(1)} custom-call(bf16[576,128]{1,0:T(8,128)(2,1)S(1)} %merge.3.one_ref, bf16[576,128]{1,0:T(8,128)(2,1)S(1)} %collective-permute-done.2.two_ref), custom_call_target="tpu_custom_call" | custom-call | tf_op jit(solution)/shard_map/merge/pallas_call | solution.py:190
  37.7 3.3 %collective-permute-start.3 = (bf16[576,128]{1,0:T(8,128)(2,1)S(1)}, bf16[576,128]{1,0:T(8,128)(2,1)S(1)}, u32[]{:S(2)}, u32[]{:S(2)}) collective-permute-start(bf16[576,128]{1,0:T(8,128)(2,1)S(1)} %merge.4.one_ref), channel_id=1, source_target_pairs={{0,8},{2,10},{4,12},{6,14},{8,0},{10,2},{12,4},{14,6},{1,9},{3,11}... | collective-permute-start | bytes 442376 | tf_op jit(solution)/shard_map/ppermute | solution.py:323
  41.0 4.7 %collective-permute-done.3.two_ref = bf16[576,128]{1,0:T(8,128)(2,1)S(1)} collective-permute-done((bf16[576,128]{1,0:T(8,128)(2,1)S(1)}, bf16[576,128]{1,0:T(8,128)(2,1)S(1)}, u32[]{:S(2)}, u32[]{:S(2)}) %collective-permute-start.3) | collective-permute-done | bytes 147488 | tf_op jit(solution)/shard_map/ppermute | solution.py:323
  45.7 1.2 %merge.5 = bf16[512,128]{1,0:T(8,128)(2,1)} custom-call(bf16[576,128]{1,0:T(8,128)(2,1)S(1)} %merge.4.one_ref, bf16[576,128]{1,0:T(8,128)(2,1)S(1)} %collective-permute-done.3.two_ref), custom_call_target="tpu_custom_call" | custom-call | tf_op jit(solution)/shard_map/merge/pallas_call | solution.py:190
  46.9 1.6 %relay.1 = (bf16[32,32,128]{2,1,0:T(8,128)(2,1)}, bf16[32,32,128]{2,1,0:T(8,128)(2,1)}) custom-call(s32[32]{0:T(128)S(1)} %copy-done.4, s32[1]{0:T(128)} %bitcast.1.live_ref, bf16[16,2,2,32,128]{4,3,2,1,0:T(8,128)(2,1)S(1)} %bitcast.31), custom_call_target="tpu_custom_call" | custom-call | tf_op jit(solution)/shard_map/relay/pallas_call | solution.py:219
  (20 shorter events, 0.2 us)
Async XLA Ops:
  3.4 8.5 %copy-start.6 = (bf16[1,2,8,32,2,128]{5,4,3,2,1,0:T(2,128)(2,1)S(1)}, bf16[1,2,8,32,2,128]{5,4,3,2,1,0:T(2,128)(2,1)}, u32[]{:S(2)}) copy-start(bf16[1,2,8,32,2,128]{5,4,3,2,1,0:T(2,128)(2,1)} %get-tuple-element.12) | copy-start | bytes 786436
  3.5 43.4 %all-to-all-start = ((bf16[16,2,64,128]{3,2,1,0:T(8,128)(2,1)}), bf16[16,2,64,128]{3,2,1,0:T(8,128)(2,1)S(1)}, u32[]{:S(2)}, u32[]{:S(2)}) async-start(bf16[16,2,64,128]{3,2,1,0:T(8,128)(2,1)} %bitcast.35), calls=%async_computation | async-start | bytes 1048576 | tf_op jit(solution)/shard_map/all_to_all | solution.py:268
  12.0 12.8 %collective-permute-start = (bf16[2,512,128]{2,1,0:T(8,128)(2,1)S(1)}, bf16[2,512,128]{2,1,0:T(8,128)(2,1)S(1)}, u32[]{:S(2)}, u32[]{:S(2)}) collective-permute-start(bf16[2,512,128]{2,1,0:T(8,128)(2,1)S(1)} %bitcast.42), channel_id=1, source_target_pairs={{0,16},{16,0},{1,17},{17,1},{2,18},{18,2},{3,19},{19,3},{4,20},{20... | collective-permute-start | bytes 786440 | tf_op jit(solution)/shard_map/ppermute | solution.py:262
  14.7 0.7 %copy-start.5 = (s32[16]{0:T(128)S(1)}, s32[16]{0:T(128)}, u32[]{:S(2)}) copy-start(s32[16]{0:T(128)} %param.15) | copy-start | bytes 196
  16.0 0.7 %copy-start.4 = (s32[32]{0:T(128)S(1)}, s32[32]{0:T(128)}, u32[]{:S(2)}) copy-start(s32[32]{0:T(128)} %slots_ref.1) | copy-start | bytes 388
  17.0 7.7 %copy-start = (bf16[2,8,32,2,128]{4,3,2,1,0:T(2,128)(2,1)S(1)}, bf16[2,8,32,2,128]{4,3,2,1,0:T(2,128)(2,1)}, u32[]{:S(2)}) copy-start(bf16[2,8,32,2,128]{4,3,2,1,0:T(2,128)(2,1)} %get-tuple-element.11) | copy-start | bytes 786436
  17.3 7.4 %copy-start.1 = (bf16[16,32,128]{2,1,0:T(8,128)(2,1)S(1)}, bf16[16,32,128]{2,1,0:T(8,128)(2,1)}, u32[]{:S(2)}) copy-start(bf16[16,32,128]{2,1,0:T(8,128)(2,1)} %query_ref.1) | copy-start | bytes 393220
  17.4 7.4 %copy-start.2 = (bf16[16,2,128]{2,1,0:T(2,128)(2,1)S(1)}, bf16[16,2,128]{2,1,0:T(2,128)(2,1)}, u32[]{:S(2)}) copy-start(bf16[16,2,128]{2,1,0:T(2,128)(2,1)} %param.13) | copy-start | bytes 24580
  17.4 7.4 %copy-start.3 = (bf16[16,2,128]{2,1,0:T(2,128)(2,1)S(1)}, bf16[16,2,128]{2,1,0:T(2,128)(2,1)}, u32[]{:S(2)}) copy-start(bf16[16,2,128]{2,1,0:T(2,128)(2,1)} %param.14) | copy-start | bytes 24580
  26.2 5.2 %collective-permute-start.1 = (bf16[576,128]{1,0:T(8,128)(2,1)S(1)}, bf16[576,128]{1,0:T(8,128)(2,1)S(1)}, u32[]{:S(2)}, u32[]{:S(2)}) collective-permute-start(bf16[576,128]{1,0:T(8,128)(2,1)S(1)} %attend.1.one_ref), channel_id=1, source_target_pairs={{0,2},{2,0},{4,6},{6,4},{8,10},{10,8},{12,14},{14,12},{1,3},{3,1},... | collective-permute-start | bytes 442376 | tf_op jit(solution)/shard_map/ppermute | solution.py:323
  32.0 5.2 %collective-permute-start.2 = (bf16[576,128]{1,0:T(8,128)(2,1)S(1)}, bf16[576,128]{1,0:T(8,128)(2,1)S(1)}, u32[]{:S(2)}, u32[]{:S(2)}) collective-permute-start(bf16[576,128]{1,0:T(8,128)(2,1)S(1)} %merge.3.one_ref), channel_id=1, source_target_pairs={{0,4},{2,6},{4,0},{6,2},{8,12},{10,14},{12,8},{14,10},{1,5},{3,7},... | collective-permute-start | bytes 442376 | tf_op jit(solution)/shard_map/ppermute | solution.py:323
  37.7 8.0 %collective-permute-start.3 = (bf16[576,128]{1,0:T(8,128)(2,1)S(1)}, bf16[576,128]{1,0:T(8,128)(2,1)S(1)}, u32[]{:S(2)}, u32[]{:S(2)}) collective-permute-start(bf16[576,128]{1,0:T(8,128)(2,1)S(1)} %merge.4.one_ref), channel_id=1, source_target_pairs={{0,8},{2,10},{4,12},{6,14},{8,0},{10,2},{12,4},{14,6},{1,9},{3,11}... | collective-permute-start | bytes 442376 | tf_op jit(solution)/shard_map/ppermute | solution.py:323

commit v4 on v3

--- a/solution.py
+++ b/solution.py
@@ -46,55 +46,133 @@
     ).astype(F32).astype(BF16)
 
 
-def pack_kernel(head_index_ref, keys_ref, values_ref, send_ref, mine_ref, away_ref, held, in_sems, out_sems, mine_sems, away_sems):
-    head_count = keys_ref.shape[2]
-    me = head_index_ref[0]
-    ins = {}
+def split_off(x, n):
+    if n & (n - 1) == 0:
+        return x & (n - 1), x >> (n.bit_length() - 1)
+    return lax.rem(x, n), lax.div(x, n)
+
+
+def pack_kernel(
+    span_rows,
+    group,
+    keys_ref,
+    values_ref,
+    slots_hbm,
+    length_hbm,
+    depth_hbm,
+    send_ref,
+    mine_ref,
+    away_ref,
+    bias_ref,
+    new_bias_ref,
+    slots_ref,
+    length_ref,
+    depth_ref,
+    in_sems,
+    out_sems,
+    fact_sems,
+):
+    seq_count, _, head_count, kv_count, _ = keys_ref.shape
+    slot_count = slots_hbm.shape[0]
+    token_count = depth_hbm.shape[0]
+    me = lax.axis_index("head")
+    seq_index = lax.axis_index("seq")
+    facts = [
+        pltpu.make_async_copy(source, target, fact_sems.at[at])
+        for at, (source, target) in enumerate(
+            ((slots_hbm, slots_ref), (length_hbm, length_ref), (depth_hbm, depth_ref))
+        )
+    ]
+    blocks = []
     for shift in list(range(1, head_count)) + [0]:
         h = lax.rem(me + shift, head_count)
         for c, source in enumerate((keys_ref, values_ref)):
-            copy = pltpu.make_async_copy(source.at[:, :, h], held.at[shift, c], in_sems.at[shift, c])
+            target = away_ref.at[shift - 1, c] if shift else mine_ref.at[c]
+            copy = pltpu.make_async_copy(source.at[:, :, h], target, in_sems.at[shift, c])
             copy.start()
-            ins[shift, c] = copy
-    outs = []
-    for (shift, c), copy in ins.items():
+            out = pltpu.make_async_copy(target, send_ref.at[h, :, c], out_sems.at[shift, c])
+            blocks.append((copy, out))
+    for fact in facts:
+        fact.start()
+    for fact in facts:
+        fact.wait()
+
+    wanted = []
+    for b in range(head_count):
+        first = 2 * (lax.rem(me + head_count - b, head_count) * seq_count + seq_index)
+        wanted += [first, first + 1]
+
+    def look(t, places):
+        slot = slots_ref[t]
+        return tuple(jnp.where(slot == w, t, p) for w, p in zip(wanted, places))
+
+    places = lax.fori_loop(0, slot_count, look, tuple(jnp.int32(0) for _ in wanted))
+    column = lax.broadcasted_iota(jnp.int32, (1, bias_ref.shape[1]), 1)
+    kv, rest = split_off(column, kv_count)
+    row, rest = split_off(rest, span_rows)
+    half, rest = split_off(rest, 2)
+    turn, block = split_off(rest, seq_count)
+    span = jnp.zeros_like(column)
+    for at, place in enumerate(places):
+        span = jnp.where(2 * block + half == at, place, span)
+    alive = (turn * slot_count + span) * span_rows + row < length_ref[0]
+    for g in range(kv_count):
+        bias_ref[g : g + 1, :] = jnp.where(alive & (kv == g), 0.0, DEAD)
+
+    column = lax.broadcasted_iota(jnp.int32, (1, new_bias_ref.shape[2]), 1)
+    kv, token = split_off(column, kv_count)
+    depth = jnp.zeros_like(column)
+    for t in range(token_count):
+        depth = jnp.where(token == t, depth_ref[t], depth)
+    for t in range(token_count):
+        limit = jnp.where(seq_index == 0, depth_ref[t], -1)
+        for g in range(kv_count):
+            seen = jnp.where((depth <= limit) & (kv == g), 0.0, DEAD)
+            new_bias_ref[g, t * group : (t + 1) * group, :] = jnp.broadcast_to(
+                seen, (group, seen.shape[1])
+            )
+
+    for copy, out in blocks:
         copy.wait()
-        h = lax.rem(me + shift, head_count)
-        block = held.at[shift, c]
-        if shift:
-            outs.append(pltpu.make_async_copy(block, away_ref.at[shift - 1, c], away_sems.at[shift - 1, c]))
-        else:
-            outs.append(pltpu.make_async_copy(block, mine_ref.at[c], mine_sems.at[c]))
-        outs[-1].start()
-        outs.append(pltpu.make_async_copy(block, send_ref.at[h, :, c], out_sems.at[shift, c]))
-        outs[-1].start()
-    for out in outs:
+        out.start()
+    for _, out in blocks:
         out.wait()
 
 
-def pack(head_index, cache_keys, cache_values, seq_count, head_count):
+def pack(cache_keys, cache_values, span_slots, prompt_length, depth, seq_count, head_count, heads):
     row_count, kv_all, head_dim = cache_keys.shape
-    split = (seq_count, row_count // seq_count, head_count, kv_all // head_count, head_dim)
-    rows, kv = split[1], split[3]
+    kv = kv_all // head_count
+    rows = row_count // seq_count
+    split = (seq_count, rows, head_count, kv, head_dim)
     block = (seq_count, rows, kv, head_dim)
+    tokens = depth.shape[0]
+    group = heads // kv
+    inputs = [
+        pltpu.with_memory_space_constraint(x.reshape(split), pltpu.HBM)
+        for x in (cache_keys, cache_values)
+    ]
     return pl.pallas_call(
-        pack_kernel,
+        functools.partial(pack_kernel, rows // 2, group),
         out_shape=(
             jax.ShapeDtypeStruct((head_count, seq_count, 2, rows, kv, head_dim), BF16),
             jax.ShapeDtypeStruct((2,) + block, BF16),
             jax.ShapeDtypeStruct((head_count - 1, 2) + block, BF16),
+            jax.ShapeDtypeStruct((kv, head_count * row_count * kv), F32),
+            jax.ShapeDtypeStruct((kv, tokens * group, tokens * kv), F32),
         ),
-        in_specs=[SMEM, HBM, HBM],
-        out_specs=(HBM, VMEM, HBM),
+        in_specs=[HBM] * 5,
+        out_specs=(HBM, VMEM, VMEM, VMEM, VMEM),
         scratch_shapes=[
-            pltpu.VMEM((head_count, 2) + block, BF16),
+            pltpu.SMEM(span_slots.shape, jnp.int32),
+            pltpu.SMEM(prompt_length.shape, jnp.int32),
+            pltpu.SMEM(depth.shape, jnp.int32),
             pltpu.SemaphoreType.DMA((head_count, 2)),
             pltpu.SemaphoreType.DMA((head_count, 2)),
-            pltpu.SemaphoreType.DMA((2,)),
-            pltpu.SemaphoreType.DMA((head_count - 1, 2)),
+            pltpu.SemaphoreType.DMA((3,)),
         ],
+        compiler_params=PARAMS,
         name="pack",
-    )(head_index, cache_keys.reshape(split), cache_values.reshape(split))
+    )(*inputs, span_slots, prompt_length, depth)
 
 
 def attend_kernel(score_scale, query_ref, new_keys_ref, new_values_ref, new_bias_ref, bias_ref, *rest):
@@ -151,50 +229,56 @@
     )(query, new_keys, new_values, new_bias, bias, *blocks)
 
 
-def merge_kernel(last, one_ref, two_ref, out_ref):
-    head_dim = one_ref.shape[1]
-    count = one_ref.shape[0] * LANES // (LANES + STAT_ROWS)
+def tree(combine, parts):
+    while len(parts) > 1:
+        parts = [combine(parts[k], parts[k + 1]) for k in range(0, len(parts), 2)]
+    return parts[0]
+
+
+def merge_kernel(last, *refs):
+    *in_refs, out_ref = refs
+    head_dim = out_ref.shape[1]
+    count = in_refs[0].shape[0] * LANES // (LANES + STAT_ROWS)
     turn = eye(LANES, LANES)
+    factor_rows = -(-3 * len(in_refs) // STAT_ROWS) * STAT_ROWS
     for at in range(count // LANES):
         start = count + at * STAT_ROWS
         peaks, totals = [], []
-        for ref in (one_ref, two_ref):
+        for ref in in_refs:
             stats = ref[start : start + STAT_ROWS, :].astype(F32)
             peaks.append(stats[0:1] + stats[1:2] + stats[2:3])
             totals.append(stats[3:4] + stats[4:5] + stats[5:6])
-        peak = jnp.maximum(*peaks)
+        peak = tree(jnp.maximum, peaks)
         factors = [jnp.exp(p - peak) for p in peaks]
-        total = factors[0] * totals[0] + factors[1] * totals[1]
+        total = tree(jnp.add, [f * t for f, t in zip(factors, totals)])
         if last:
             factors = [f / total for f in factors]
         else:
             out_ref[start : start + STAT_ROWS, :] = stacked(
                 three_parts(peak) + three_parts(total), (STAT_ROWS, LANES)
             )
-        columns = dot_rows(
-            turn, stacked(three_parts(factors[0]) + three_parts(factors[1]), (STAT_ROWS, LANES))
-        )
-        result = None
-        for k, ref in enumerate((one_ref, two_ref)):
+        parts = [part for f in factors for part in three_parts(f)]
+        columns = dot_rows(turn, stacked(parts, (factor_rows, LANES)))
+        terms = []
+        for k, ref in enumerate(in_refs):
             column = columns[:, 3 * k : 3 * k + 1] + columns[:, 3 * k + 1 : 3 * k + 2]
             column = jnp.broadcast_to(column + columns[:, 3 * k + 2 : 3 * k + 3], (LANES, head_dim))
-            term = ref[at * LANES : (at + 1) * LANES, :].astype(F32) * column
-            result = term if result is None else result + term
-        out_ref[at * LANES : (at + 1) * LANES, :] = result.astype(BF16)
-
-
-def merge(one, two, last):
-    rows, head_dim = one.shape
+            terms.append(ref[at * LANES : (at + 1) * LANES, :].astype(F32) * column)
+        out_ref[at * LANES : (at + 1) * LANES, :] = tree(jnp.add, terms).astype(BF16)
+
+
+def merge(states, last):
+    rows, head_dim = states[0].shape
     if last:
         rows = rows * LANES // (LANES + STAT_ROWS)
     return pl.pallas_call(
         functools.partial(merge_kernel, last),
         out_shape=jax.ShapeDtypeStruct((rows, head_dim), BF16),
-        in_specs=[VMEM, VMEM],
+        in_specs=[VMEM] * len(states),
         out_specs=VMEM,
         compiler_params=PARAMS,
         name="merge",
-    )(one, two)
+    )(*states)
 
 
 def relay_kernel(slots_ref, live_ref, got_ref, keys_ref, values_ref):
@@ -244,16 +328,21 @@
     span_rows = row_count // (2 * seq_count)
     kv_local = kv_all // head_count
     token_count, heads, _ = queries.shape
-    group_size = heads // kv_local
     length = prompt_length[0]
     score_scale = 1.0 / math.sqrt(head_dim)
     shard_rows = slot_count * span_rows
     seq_index = lax.axis_index("seq")
-    head_index = lax.axis_index("head")
     shard_start = seq_index * shard_rows
 
-    packed, mine, away = pack(
-        head_index.reshape(1), cache_keys, cache_values, seq_count, head_count
+    packed, mine, away, bias, new_bias = pack(
+        cache_keys,
+        cache_values,
+        span_slots,
+        prompt_length,
+        decode_offsets,
+        seq_count,
+        head_count,
+        heads,
     )
     flat = (2, row_count * kv_local, head_dim)
     blocks = [mine.reshape(flat)]
@@ -273,56 +362,25 @@
         tiled=True,
     )
 
-    columns = (head_count, seq_count, 2, span_rows, kv_local)
-
-    def index_of(axis):
-        return lax.broadcasted_iota(jnp.int32, columns, axis).reshape(head_count, -1)
-
-    source = lax.rem(head_index - index_of(0) + head_count, head_count) * seq_count + seq_index
-    slot = 2 * source + index_of(2)
-    spans = jnp.arange(slot_count, dtype=jnp.int32)
-    wanted = 2 * (
-        lax.rem(head_index - jnp.arange(head_count, dtype=jnp.int32) + head_count, head_count)
-        * seq_count
-        + seq_index
-    )
-    place = [
-        jnp.sum(jnp.where(span_slots[None, :] == (wanted + k)[:, None], spans[None, :], 0), axis=1)
-        for k in range(2)
-    ]
-    span_at = jnp.where(index_of(2) == 0, place[0][:, None], place[1][:, None])
-    position = (index_of(1) * slot_count + span_at) * span_rows + index_of(3)
-    alive = (position < length).reshape(-1)
-    column_kv = index_of(4).reshape(-1)
-    kv_range = jnp.arange(kv_local, dtype=jnp.int32)
-    bias = jnp.where(
-        alive[None, :] & (column_kv[None, :] == kv_range[:, None]), 0.0, DEAD
-    ).astype(F32)
-
-    shape = (kv_local, token_count, group_size, token_count * kv_local)
-    new_kv = lax.broadcasted_iota(jnp.int32, shape, 3) % kv_local
-    new_depth = jnp.broadcast_to(decode_offsets[:, None], (token_count, kv_local)).reshape(-1)
-    seen = (
-        (new_depth[None, None, None, :] <= decode_offsets[None, :, None, None])
-        & (new_kv == lax.broadcasted_iota(jnp.int32, shape, 0))
-        & (seq_index == 0)
-    )
-    new_bias = jnp.where(seen, 0.0, DEAD).astype(F32)
     state = attend(
         queries,
         new_keys.reshape(token_count * kv_local, head_dim),
         new_values.reshape(token_count * kv_local, head_dim),
-        new_bias.reshape(kv_local, token_count * group_size, token_count * kv_local),
+        new_bias,
         bias,
         blocks,
         score_scale,
     )
     stride = 1
     while stride < seq_count:
-        last = 2 * stride >= seq_count
-        other = lax.ppermute(state, "seq", [(s, s ^ stride) for s in range(seq_count)])
-        state = merge(state, other, last)
-        stride *= 2
+        ways = 4 if stride == 1 and seq_count > 4 else 2
+        last = stride * ways >= seq_count
+        states = [state]
+        for way in range(1, ways):
+            pairs = [(s, s ^ (way * stride)) for s in range(seq_count)]
+            states.append(lax.ppermute(state, "seq", pairs))
+        state = merge(states, last)
+        stride *= ways
 
     live = jnp.clip(length - shard_start, 0, shard_rows) * kv_local
     relaid_keys, relaid_values = relay(

time: 48.7 us -> 49.2 us (1.010)
  waiting for transfers between devices: 19 us -> 22.8 us
  local copies, waits for them, and re-layouts: 2.32 us -> 0.67 us
  Pallas kernels: 8.1 us -> 7.04 us
    ppermute x1, waiting for transfers between devices: 7.31 us -> 10.8 us  [step(): lax.ppermute(away[shift - 1].reshape(flat), 'head', [(h, (h + shift) % he...]
    pallas_call x1, Pallas kernels: 2.81 us -> 1.88 us  [pack(): pl.pallas_call(functools.partial(pack_kernel, rows // 2, group), out_shap...]
    unnamed x17 -> x10, local copies, waits for them, and re-layouts: 1.41 us -> 0.67 us
    ppermute x3 -> x4, waiting for transfers between devices: 11.7 us -> 12 us  [step(): states.append(lax.ppermute(state, 'seq', pairs))]
    ppermute x3 -> x4, starting transfers between devices: 6.69 us -> 6.56 us  [step(): states.append(lax.ppermute(state, 'seq', pairs))]
    pallas_call x3 -> x2, Pallas kernels: 2.21 us -> 2.09 us  [merge(): pl.pallas_call(functools.partial(merge_kernel, last), out_shape=jax.Shape...]
  transfers between devices with their start and end apart: 5 -> 6, of which waited for: 4 -> 5; matrix products, arithmetic and copies ran while one was open for 3% -> 0% of each run, Pallas kernels for 8% -> 7%
where the time goes in v4:
time: 49.2 us; the launch traced here: 48.9 us
  waiting for transfers between devices  22.8 us (46%)
  starting transfers between devices  17.1 us (35%)
  Pallas kernels  7.04 us (14%)
  between operations  1.35 us (3%)
  local copies, waits for them, and re-layouts  0.67 us (1%)
    ppermute x4, waiting for transfers between devices, step(): states.append(lax.ppermute(state, 'seq', pairs))  12 us
    ppermute x1, waiting for transfers between devices, step(): lax.ppermute(away[shift - 1].reshape(flat), 'head', [(h, (h + shift) % he...  10.8 us
    all_to_all x1, starting transfers between devices, step(): lax.all_to_all(packed.reshape(cycle_size, 2, 2 * span_rows * kv_local, he...  8.5 us
    ppermute x4, starting transfers between devices, step(): states.append(lax.ppermute(state, 'seq', pairs))  6.56 us
    pallas_call x2, Pallas kernels, merge(): pl.pallas_call(functools.partial(merge_kernel, last), out_shape=jax.Shape...  2.09 us
    ppermute x1, starting transfers between devices, step(): lax.ppermute(away[shift - 1].reshape(flat), 'head', [(h, (h + shift) % he...  1.99 us
    pallas_call x1, Pallas kernels, pack(): pl.pallas_call(functools.partial(pack_kernel, rows // 2, group), out_shap...  1.88 us
    pallas_call x1, Pallas kernels, relay(): pl.pallas_call(relay_kernel, out_shape=(shape, shape), in_specs=[SMEM, SM...  1.62 us
  transfers between devices with their start and end apart: 6, of which 5 were waited for; matrix products, arithmetic and copies ran while one was open for 0% of the time, Pallas kernels for 7%

profile of v4, /device:TPU:0, one launch (start us, length us, event | category | flops | bytes accessed | tf_op | source)
XLA Modules:
  0.0 48.9 jit_solution(18381035033399456030)
XLA Ops:
  1.3 0.0 copy-start.3
  1.3 0.0 copy-start.4
  1.3 0.6 %copy-done.3 = s32[32]{0:T(128)S(1)} copy-done((s32[32]{0:T(128)S(1)}, s32[32]{0:T(128)}, u32[]{:S(2)}) %copy-start.3) | copy-done | bytes 152
  1.9 0.0 copy-done.4
  1.9 1.9 %pack.1 = (bf16[2,8,2,32,2,128]{5,4,3,2,1,0:T(2,128)(2,1)}, bf16[2,8,32,2,128]{4,3,2,1,0:T(2,128)(2,1)S(1)}, bf16[1,2,8,32,2,128]{5,4,3,2,1,0:T(2,128)(2,1)S(1)}, f32[2,1024]{1,0:T(2,128)S(1)}, f32[2,256,32]{2,1,0:T(8,128)S(1)}) custom-call(bf16[8,32,2,2,128]{4,3,2,1,0:T(2,128)(2,1)} %bitcast.19, bf16[8,32,2,2,128]{4,3,2,1,0:T(2,128)(2,1)} %bitcast.20, ...), custom_call_target="tpu_custom_call" | custom-call | tf_op jit(solution)/shard_map/pack/pallas_call | solution.py:154
  3.8 0.0 copy-start
  3.9 0.0 copy-start.2
  3.9 8.5 %all-to-all-start = ((bf16[16,2,64,128]{3,2,1,0:T(8,128)(2,1)}), bf16[16,2,64,128]{3,2,1,0:T(8,128)(2,1)S(1)}, u32[]{:S(2)}, u32[]{:S(2)}) async-start(bf16[16,2,64,128]{3,2,1,0:T(8,128)(2,1)} %bitcast.4), calls=%async_computation | async-start | bytes 1048576 | tf_op jit(solution)/shard_map/all_to_all | solution.py:357
  12.4 0.0 copy-start.1
  12.4 2.0 %collective-permute-start = (bf16[2,512,128]{2,1,0:T(8,128)(2,1)S(1)}, bf16[2,512,128]{2,1,0:T(8,128)(2,1)S(1)}, u32[]{:S(2)}, u32[]{:S(2)}) collective-permute-start(bf16[2,512,128]{2,1,0:T(8,128)(2,1)S(1)} %bitcast.18), channel_id=1, source_target_pairs={{0,16},{16,0},{1,17},{17,1},{2,18},{18,2},{3,19},{19,3},{4,20},{20... | collective-permute-start | bytes 786440 | tf_op jit(solution)/shard_map/ppermute | solution.py:351
  14.4 10.8 %collective-permute-done.rest_1_ = bf16[2,512,128]{2,1,0:T(8,128)(2,1)S(1)} collective-permute-done((bf16[2,512,128]{2,1,0:T(8,128)(2,1)S(1)}, bf16[2,512,128]{2,1,0:T(8,128)(2,1)S(1)}, u32[]{:S(2)}, u32[]{:S(2)}) %collective-permute-start) | collective-permute-done | bytes 262176 | tf_op jit(solution)/shard_map/ppermute | solution.py:351
  25.2 0.0 copy-done
  25.2 0.0 copy-done.2
  25.2 0.0 copy-done.1
  25.2 1.5 %attend.1.refs_0_ = bf16[576,128]{1,0:T(8,128)(2,1)S(1)} custom-call(bf16[16,32,128]{2,1,0:T(8,128)(2,1)S(1)} %copy-done, bf16[32,128]{1,0:T(8,128)(2,1)S(1)} %bitcast.16, bf16[32,128]{1,0:T(8,128)(2,1)S(1)} %bitcast.17, f32[2,256,32]{2,1,0:T(8,128)S(1)} %get-tuple-element.13.new_bias_ref, f32[2,1024]{1,0:T(2,128)S(1)} %get-tuple-element.14.bias_ref, ...), custom_call_target="tpu_custom_call" | custom-call | tf_op jit(solution)/shard_map/attend/pallas_call | solution.py:218
  26.6 1.5 %collective-permute-start.1 = (bf16[576,128]{1,0:T(8,128)(2,1)S(1)}, bf16[576,128]{1,0:T(8,128)(2,1)S(1)}, u32[]{:S(2)}, u32[]{:S(2)}) collective-permute-start(bf16[576,128]{1,0:T(8,128)(2,1)S(1)} %attend.1.refs_0_), channel_id=1, source_target_pairs={{0,2},{2,0},{4,6},{6,4},{8,10},{10,8},{12,14},{14,12},{1,3},{3,1},... | collective-permute-start | bytes 442376 | tf_op jit(solution)/shard_map/ppermute | solution.py:381
  28.1 1.8 %collective-permute-start.2 = (bf16[576,128]{1,0:T(8,128)(2,1)S(1)}, bf16[576,128]{1,0:T(8,128)(2,1)S(1)}, u32[]{:S(2)}, u32[]{:S(2)}) collective-permute-start(bf16[576,128]{1,0:T(8,128)(2,1)S(1)} %attend.1.refs_0_), channel_id=1, source_target_pairs={{0,4},{2,6},{4,0},{6,2},{8,12},{10,14},{12,8},{14,10},{1,5},{3,7},... | collective-permute-start | bytes 442376 | tf_op jit(solution)/shard_map/ppermute | solution.py:381
  30.0 0.2 collective-permute-start.3
  30.2 1.7 %collective-permute-done.1.refs_1_ = bf16[576,128]{1,0:T(8,128)(2,1)S(1)} collective-permute-done((bf16[576,128]{1,0:T(8,128)(2,1)S(1)}, bf16[576,128]{1,0:T(8,128)(2,1)S(1)}, u32[]{:S(2)}, u32[]{:S(2)}) %collective-permute-start.1) | collective-permute-done | bytes 147488 | tf_op jit(solution)/shard_map/ppermute | solution.py:381
  31.8 3.0 %collective-permute-done.2.refs_2_ = bf16[576,128]{1,0:T(8,128)(2,1)S(1)} collective-permute-done((bf16[576,128]{1,0:T(8,128)(2,1)S(1)}, bf16[576,128]{1,0:T(8,128)(2,1)S(1)}, u32[]{:S(2)}, u32[]{:S(2)}) %collective-permute-start.2) | collective-permute-done | bytes 147488 | tf_op jit(solution)/shard_map/ppermute | solution.py:381
  34.8 1.6 %collective-permute-done.3.refs_3_ = bf16[576,128]{1,0:T(8,128)(2,1)S(1)} collective-permute-done((bf16[576,128]{1,0:T(8,128)(2,1)S(1)}, bf16[576,128]{1,0:T(8,128)(2,1)S(1)}, u32[]{:S(2)}, u32[]{:S(2)}) %collective-permute-start.3) | collective-permute-done | bytes 147488 | tf_op jit(solution)/shard_map/ppermute | solution.py:381
  36.5 0.9 %merge.2.refs_0_ = bf16[576,128]{1,0:T(8,128)(2,1)S(1)} custom-call(bf16[576,128]{1,0:T(8,128)(2,1)S(1)} %attend.1.refs_0_, bf16[576,128]{1,0:T(8,128)(2,1)S(1)} %collective-permute-done.1.refs_1_, bf16[576,128]{1,0:T(8,128)(2,1)S(1)} %collective-permute-done.2.refs_2_, bf16[576,128]{1,0:T(8,128)(2,1)S(1)} %collective-permute-done.3.refs_3_), custom_call_target="tpu_custom_call" | custom-call | tf_op jit(solution)/shard_map/merge/pallas_call | solution.py:274
  37.4 3.0 %collective-permute-start.4 = (bf16[576,128]{1,0:T(8,128)(2,1)S(1)}, bf16[576,128]{1,0:T(8,128)(2,1)S(1)}, u32[]{:S(2)}, u32[]{:S(2)}) collective-permute-start(bf16[576,128]{1,0:T(8,128)(2,1)S(1)} %merge.2.refs_0_), channel_id=1, source_target_pairs={{0,8},{2,10},{4,12},{6,14},{8,0},{10,2},{12,4},{14,6},{1,9},{3,11}... | collective-permute-start | bytes 442376 | tf_op jit(solution)/shard_map/ppermute | solution.py:381
  40.4 5.7 %collective-permute-done.4.refs_1_ = bf16[576,128]{1,0:T(8,128)(2,1)S(1)} collective-permute-done((bf16[576,128]{1,0:T(8,128)(2,1)S(1)}, bf16[576,128]{1,0:T(8,128)(2,1)S(1)}, u32[]{:S(2)}, u32[]{:S(2)}) %collective-permute-start.4) | collective-permute-done | bytes 147488 | tf_op jit(solution)/shard_map/ppermute | solution.py:381
  46.1 1.2 %merge.3 = bf16[512,128]{1,0:T(8,128)(2,1)} custom-call(bf16[576,128]{1,0:T(8,128)(2,1)S(1)} %merge.2.refs_0_, bf16[576,128]{1,0:T(8,128)(2,1)S(1)} %collective-permute-done.4.refs_1_), custom_call_target="tpu_custom_call" | custom-call | tf_op jit(solution)/shard_map/merge/pallas_call | solution.py:274
  47.3 0.0 all-to-all-done
  47.3 1.6 %relay.1 = (bf16[32,32,128]{2,1,0:T(8,128)(2,1)}, bf16[32,32,128]{2,1,0:T(8,128)(2,1)}) custom-call(s32[32]{0:T(128)S(1)} %copy-done.3, s32[1]{0:T(128)} %bitcast.1.live_ref, bf16[16,2,2,32,128]{4,3,2,1,0:T(8,128)(2,1)S(1)} %bitcast.14), custom_call_target="tpu_custom_call" | custom-call | tf_op jit(solution)/shard_map/relay/pallas_call | solution.py:303
Async XLA Ops:
  1.3 0.7 %copy-start.3 = (s32[32]{0:T(128)S(1)}, s32[32]{0:T(128)}, u32[]{:S(2)}) copy-start(s32[32]{0:T(128)} %slots_ref.1) | copy-start | bytes 388
  1.3 0.7 %copy-start.4 = (s32[16]{0:T(128)S(1)}, s32[16]{0:T(128)}, u32[]{:S(2)}) copy-start(s32[16]{0:T(128)} %depth_hbm.1) | copy-start | bytes 196
  3.8 21.3 %copy-start = (bf16[16,32,128]{2,1,0:T(8,128)(2,1)S(1)}, bf16[16,32,128]{2,1,0:T(8,128)(2,1)}, u32[]{:S(2)}) copy-start(bf16[16,32,128]{2,1,0:T(8,128)(2,1)} %query_ref.1) | copy-start | bytes 393220
  3.9 21.3 %copy-start.2 = (bf16[16,2,128]{2,1,0:T(2,128)(2,1)S(1)}, bf16[16,2,128]{2,1,0:T(2,128)(2,1)}, u32[]{:S(2)}) copy-start(bf16[16,2,128]{2,1,0:T(2,128)(2,1)} %param.14) | copy-start | bytes 24580
  3.9 43.4 %all-to-all-start = ((bf16[16,2,64,128]{3,2,1,0:T(8,128)(2,1)}), bf16[16,2,64,128]{3,2,1,0:T(8,128)(2,1)S(1)}, u32[]{:S(2)}, u32[]{:S(2)}) async-start(bf16[16,2,64,128]{3,2,1,0:T(8,128)(2,1)} %bitcast.4), calls=%async_computation | async-start | bytes 1048576 | tf_op jit(solution)/shard_map/all_to_all | solution.py:357
  12.4 12.8 %copy-start.1 = (bf16[16,2,128]{2,1,0:T(2,128)(2,1)S(1)}, bf16[16,2,128]{2,1,0:T(2,128)(2,1)}, u32[]{:S(2)}) copy-start(bf16[16,2,128]{2,1,0:T(2,128)(2,1)} %param.13) | copy-start | bytes 24580
  12.4 12.8 %collective-permute-start = (bf16[2,512,128]{2,1,0:T(8,128)(2,1)S(1)}, bf16[2,512,128]{2,1,0:T(8,128)(2,1)S(1)}, u32[]{:S(2)}, u32[]{:S(2)}) collective-permute-start(bf16[2,512,128]{2,1,0:T(8,128)(2,1)S(1)} %bitcast.18), channel_id=1, source_target_pairs={{0,16},{16,0},{1,17},{17,1},{2,18},{18,2},{3,19},{19,3},{4,20},{20... | collective-permute-start | bytes 786440 | tf_op jit(solution)/shard_map/ppermute | solution.py:351
  26.6 5.2 %collective-permute-start.1 = (bf16[576,128]{1,0:T(8,128)(2,1)S(1)}, bf16[576,128]{1,0:T(8,128)(2,1)S(1)}, u32[]{:S(2)}, u32[]{:S(2)}) collective-permute-start(bf16[576,128]{1,0:T(8,128)(2,1)S(1)} %attend.1.refs_0_), channel_id=1, source_target_pairs={{0,2},{2,0},{4,6},{6,4},{8,10},{10,8},{12,14},{14,12},{1,3},{3,1},... | collective-permute-start | bytes 442376 | tf_op jit(solution)/shard_map/ppermute | solution.py:381
  28.1 6.7 %collective-permute-start.2 = (bf16[576,128]{1,0:T(8,128)(2,1)S(1)}, bf16[576,128]{1,0:T(8,128)(2,1)S(1)}, u32[]{:S(2)}, u32[]{:S(2)}) collective-permute-start(bf16[576,128]{1,0:T(8,128)(2,1)S(1)} %attend.1.refs_0_), channel_id=1, source_target_pairs={{0,4},{2,6},{4,0},{6,2},{8,12},{10,14},{12,8},{14,10},{1,5},{3,7},... | collective-permute-start | bytes 442376 | tf_op jit(solution)/shard_map/ppermute | solution.py:381
  30.0 6.5 %collective-permute-start.3 = (bf16[576,128]{1,0:T(8,128)(2,1)S(1)}, bf16[576,128]{1,0:T(8,128)(2,1)S(1)}, u32[]{:S(2)}, u32[]{:S(2)}) collective-permute-start(bf16[576,128]{1,0:T(8,128)(2,1)S(1)} %attend.1.refs_0_), channel_id=1, source_target_pairs={{0,6},{2,4},{4,2},{6,0},{8,14},{10,12},{12,10},{14,8},{1,7},{3,5},... | collective-permute-start | bytes 442376 | tf_op jit(solution)/shard_map/ppermute | solution.py:381
  37.4 8.8 %collective-permute-start.4 = (bf16[576,128]{1,0:T(8,128)(2,1)S(1)}, bf16[576,128]{1,0:T(8,128)(2,1)S(1)}, u32[]{:S(2)}, u32[]{:S(2)}) collective-permute-start(bf16[576,128]{1,0:T(8,128)(2,1)S(1)} %merge.2.refs_0_), channel_id=1, source_target_pairs={{0,8},{2,10},{4,12},{6,14},{8,0},{10,2},{12,4},{14,6},{1,9},{3,11}... | collective-permute-start | bytes 442376 | tf_op jit(solution)/shard_map/ppermute | solution.py:381

commit v5 on v4

--- a/solution.py
+++ b/solution.py
@@ -13,6 +13,7 @@
 F32 = jnp.float32
 DEAD = -1e30
 STAT_ROWS = 16
+WIDE_ROWS = 8
 LANES = 128
 VMEM = pl.BlockSpec(memory_space=pltpu.VMEM)
 SMEM = pl.BlockSpec(memory_space=pltpu.SMEM)
@@ -58,20 +59,13 @@
     keys_ref,
     values_ref,
     slots_hbm,
-    length_hbm,
+    length_ref,
     depth_hbm,
-    send_ref,
-    mine_ref,
-    away_ref,
-    bias_ref,
-    new_bias_ref,
-    slots_ref,
-    length_ref,
-    depth_ref,
-    in_sems,
-    out_sems,
-    fact_sems,
+    *rest,
 ):
+    staged, (send_ref, mine_ref, away_ref, bias_ref, new_bias_ref) = rest[:3], rest[3:8]
+    targets = rest[8:11]
+    slots_ref, depth_ref, in_sems, out_sems, fact_sems, stage_sems = rest[11:]
     seq_count, _, head_count, kv_count, _ = keys_ref.shape
     slot_count = slots_hbm.shape[0]
     token_count = depth_hbm.shape[0]
@@ -80,7 +74,7 @@
     facts = [
         pltpu.make_async_copy(source, target, fact_sems.at[at])
         for at, (source, target) in enumerate(
-            ((slots_hbm, slots_ref), (length_hbm, length_ref), (depth_hbm, depth_ref))
+            ((slots_hbm, slots_ref), (depth_hbm, depth_ref))
         )
     ]
     blocks = []
@@ -92,8 +86,12 @@
             copy.start()
             out = pltpu.make_async_copy(target, send_ref.at[h, :, c], out_sems.at[shift, c])
             blocks.append((copy, out))
-    for fact in facts:
-        fact.start()
+    stages = [
+        pltpu.make_async_copy(source, target, stage_sems.at[at])
+        for at, (source, target) in enumerate(zip(staged, targets))
+    ]
+    for copy in facts + stages:
+        copy.start()
     for fact in facts:
         fact.wait()
 
@@ -137,19 +135,42 @@
         out.start()
     for _, out in blocks:
         out.wait()
-
-
-def pack(cache_keys, cache_values, span_slots, prompt_length, depth, seq_count, head_count, heads):
+    for copy in stages:
+        copy.wait()
+
+
+def pack(
+    cache_keys,
+    cache_values,
+    span_slots,
+    prompt_length,
+    depth,
+    queries,
+    new_keys,
+    new_values,
+    seq_count,
+    head_count,
+):
     row_count, kv_all, head_dim = cache_keys.shape
     kv = kv_all // head_count
     rows = row_count // seq_count
     split = (seq_count, rows, head_count, kv, head_dim)
     block = (seq_count, rows, kv, head_dim)
-    tokens = depth.shape[0]
+    tokens, heads, _ = queries.shape
     group = heads // kv
+    fresh = (tokens * kv, head_dim)
     inputs = [
-        pltpu.with_memory_space_constraint(x.reshape(split), pltpu.HBM)
-        for x in (cache_keys, cache_values)
+        x if x is prompt_length else pltpu.with_memory_space_constraint(x, pltpu.HBM)
+        for x in (
+            cache_keys.reshape(split),
+            cache_values.reshape(split),
+            span_slots,
+            prompt_length,
+            depth,
+            queries,
+            new_keys.reshape(fresh),
+            new_values.reshape(fresh),
+        )
     ]
     return pl.pallas_call(
         functools.partial(pack_kernel, rows // 2, group),
@@ -159,24 +180,30 @@
             jax.ShapeDtypeStruct((head_count - 1, 2) + block, BF16),
             jax.ShapeDtypeStruct((kv, head_count * row_count * kv), F32),
             jax.ShapeDtypeStruct((kv, tokens * group, tokens * kv), F32),
+            jax.ShapeDtypeStruct(queries.shape, BF16),
+            jax.ShapeDtypeStruct(fresh, BF16),
+            jax.ShapeDtypeStruct(fresh, BF16),
         ),
-        in_specs=[HBM] * 5,
-        out_specs=(HBM, VMEM, VMEM, VMEM, VMEM),
+        in_specs=[HBM] * 3 + [SMEM] + [HBM] * 4,
+        out_specs=(HBM,) + (VMEM,) * 7,
         scratch_shapes=[
             pltpu.SMEM(span_slots.shape, jnp.int32),
-            pltpu.SMEM(prompt_length.shape, jnp.int32),
             pltpu.SMEM(depth.shape, jnp.int32),
             pltpu.SemaphoreType.DMA((head_count, 2)),
             pltpu.SemaphoreType.DMA((head_count, 2)),
+            pltpu.SemaphoreType.DMA((2,)),
             pltpu.SemaphoreType.DMA((3,)),
         ],
         compiler_params=PARAMS,
         name="pack",
-    )(*inputs, span_slots, prompt_length, depth)
-
-
-def attend_kernel(score_scale, query_ref, new_keys_ref, new_values_ref, new_bias_ref, bias_ref, *rest):
-    *block_refs, out_ref, rows_buf, stat_buf = rest
+    )(*inputs)
+
+
+def attend_kernel(
+    score_scale, ways, query_ref, new_keys_ref, new_values_ref, new_bias_ref, bias_ref, *rest
+):
+    *block_refs, rows_buf, stat_buf = rest
+    block_refs, out_refs = block_refs[:-ways], block_refs[-ways:]
     tokens, heads, head_dim = query_ref.shape
     kv_count = bias_ref.shape[0]
     group = heads // kv_count
@@ -202,24 +229,30 @@
             stats = jnp.where(lane == at, part, stats)
         rows_buf[:, g] = weighted.astype(BF16).reshape(tokens, group, head_dim)
         stat_buf[:, g] = stats.astype(BF16).reshape(tokens, group, head_dim)
-    count = tokens * heads
-    out_ref[:count, :] = rows_buf[...].reshape(count, head_dim)
-    turned = dot_rows(eye(STAT_ROWS, head_dim), stat_buf[...].reshape(count, head_dim))
-    for at in range(count // LANES):
-        start = count + at * STAT_ROWS
-        out_ref[start : start + STAT_ROWS, :] = turned[:, at * LANES : (at + 1) * LANES].astype(BF16)
-
-
-def attend(query, new_keys, new_values, new_bias, bias, blocks, score_scale):
+    here = lax.rem(lax.axis_index("seq"), ways)
+    share = tokens // ways
+    per = share * heads
+    pick = eye(STAT_ROWS, head_dim)
+    for way, out_ref in enumerate(out_refs):
+        first = lax.bitwise_xor(here, way) * share
+        out_ref[:per, :] = rows_buf[pl.ds(first, share)].reshape(per, head_dim)
+        turned = dot_rows(pick, stat_buf[pl.ds(first, share)].reshape(per, head_dim)).astype(BF16)
+        for at in range(per // LANES):
+            start = per + at * STAT_ROWS
+            out_ref[start : start + STAT_ROWS, :] = turned[:, at * LANES : (at + 1) * LANES]
+
+
+def attend(query, new_keys, new_values, new_bias, bias, blocks, score_scale, ways):
     tokens, heads, head_dim = query.shape
     kv_count = bias.shape[0]
     group = heads // kv_count
-    count = tokens * heads
+    per = tokens * heads // ways
+    piece = jax.ShapeDtypeStruct((per + per // LANES * STAT_ROWS, head_dim), BF16)
     return pl.pallas_call(
-        functools.partial(attend_kernel, score_scale),
-        out_shape=jax.ShapeDtypeStruct((count + count // LANES * STAT_ROWS, head_dim), BF16),
+        functools.partial(attend_kernel, score_scale, ways),
+        out_shape=(piece,) * ways,
         in_specs=[VMEM] * (5 + len(blocks)),
-        out_specs=VMEM,
+        out_specs=(VMEM,) * ways,
         scratch_shapes=[
             pltpu.VMEM((tokens, kv_count, group, head_dim), BF16),
             pltpu.VMEM((tokens, kv_count, group, head_dim), BF16),
@@ -235,28 +268,33 @@
     return parts[0]
 
 
-def merge_kernel(last, *refs):
+def merge_kernel(per, last, *refs):
     *in_refs, out_ref = refs
     head_dim = out_ref.shape[1]
-    count = in_refs[0].shape[0] * LANES // (LANES + STAT_ROWS)
+    chunks = per // LANES
+    rows_in = (in_refs[0].shape[0] - per) // chunks
+    split = in_refs[0].dtype == BF16
     turn = eye(LANES, LANES)
     factor_rows = -(-3 * len(in_refs) // STAT_ROWS) * STAT_ROWS
-    for at in range(count // LANES):
-        start = count + at * STAT_ROWS
+    for at in range(chunks):
         peaks, totals = [], []
         for ref in in_refs:
-            stats = ref[start : start + STAT_ROWS, :].astype(F32)
-            peaks.append(stats[0:1] + stats[1:2] + stats[2:3])
-            totals.append(stats[3:4] + stats[4:5] + stats[5:6])
+            stats = ref[per + at * rows_in : per + (at + 1) * rows_in, :].astype(F32)
+            if split:
+                peaks.append(stats[0:1] + stats[1:2] + stats[2:3])
+                totals.append(stats[3:4] + stats[4:5] + stats[5:6])
+            else:
+                peaks.append(stats[0:1])
+                totals.append(stats[1:2])
         peak = tree(jnp.maximum, peaks)
         factors = [jnp.exp(p - peak) for p in peaks]
         total = tree(jnp.add, [f * t for f, t in zip(factors, totals)])
         if last:
             factors = [f / total for f in factors]
         else:
-            out_ref[start : start + STAT_ROWS, :] = stacked(
-                three_parts(peak) + three_parts(total), (STAT_ROWS, LANES)
-            )
+            start = per + at * WIDE_ROWS
+            row = lax.broadcasted_iota(jnp.int32, (WIDE_ROWS, LANES), 0)
+            out_ref[start : start + WIDE_ROWS, :] = jnp.where(row == 0, peak, total)
         parts = [part for f in factors for part in three_parts(f)]
         columns = dot_rows(turn, stacked(parts, (factor_rows, LANES)))
         terms = []
@@ -264,16 +302,18 @@
             column = columns[:, 3 * k : 3 * k + 1] + columns[:, 3 * k + 1 : 3 * k + 2]
             column = jnp.broadcast_to(column + columns[:, 3 * k + 2 : 3 * k + 3], (LANES, head_dim))
             terms.append(ref[at * LANES : (at + 1) * LANES, :].astype(F32) * column)
-        out_ref[at * LANES : (at + 1) * LANES, :] = tree(jnp.add, terms).astype(BF16)
-
-
-def merge(states, last):
-    rows, head_dim = states[0].shape
+        out_ref[at * LANES : (at + 1) * LANES, :] = tree(jnp.add, terms).astype(out_ref.dtype)
+
+
+def merge(states, per, last):
+    head_dim = states[0].shape[1]
     if last:
-        rows = rows * LANES // (LANES + STAT_ROWS)
+        out = jax.ShapeDtypeStruct((per, head_dim), BF16)
+    else:
+        out = jax.ShapeDtypeStruct((per + per // LANES * WIDE_ROWS, head_dim), F32)
     return pl.pallas_call(
-        functools.partial(merge_kernel, last),
-        out_shape=jax.ShapeDtypeStruct((rows, head_dim), BF16),
+        functools.partial(merge_kernel, per, last),
+        out_shape=out,
         in_specs=[VMEM] * len(states),
         out_specs=VMEM,
         compiler_params=PARAMS,
@@ -281,10 +321,40 @@
     )(*states)
 
 
-def relay_kernel(slots_ref, live_ref, got_ref, keys_ref, values_ref):
+def join_kernel(*refs):
+    *in_refs, out_ref, sems = refs
+    ways = len(in_refs)
+    per = in_refs[0].shape[0]
+    here = lax.rem(lax.axis_index("seq"), ways)
+    copies = []
+    for way, ref in enumerate(in_refs):
+        start = pl.multiple_of(lax.bitwise_xor(here, way) * per, per)
+        copies.append(pltpu.make_async_copy(ref, out_ref.at[pl.ds(start, per)], sems.at[way]))
+        copies[-1].start()
+    for copy in copies:
+        copy.wait()
+
+
+def join(pieces):
+    per, head_dim = pieces[0].shape
+    return pl.pallas_call(
+        join_kernel,
+        out_shape=jax.ShapeDtypeStruct((len(pieces) * per, head_dim), BF16),
+        in_specs=[VMEM] * len(pieces),
+        out_specs=HBM,
+        scratch_shapes=[pltpu.SemaphoreType.DMA((len(pieces),))],
+        compiler_params=PARAMS,
+        name="join",
+    )(*pieces)
+
+
+def relay_kernel(kv_count, slots_hbm, length_ref, got_ref, keys_ref, values_ref, slots_ref, sem):
+    copy = pltpu.make_async_copy(slots_hbm, slots_ref, sem)
+    copy.start()
+    copy.wait()
     slot_count, span, head_dim = keys_ref.shape
     row = lax.broadcasted_iota(jnp.int32, (span, head_dim), 0)
-    live = live_ref[0]
+    live = length_ref[0] * kv_count - lax.axis_index("seq") * (slot_count * span)
 
     def one(t, carry):
         slot = slots_ref[t]
@@ -297,17 +367,18 @@
     lax.fori_loop(0, slot_count, one, 0, unroll=4)
 
 
-def relay(span_slots, live, got):
+def relay(span_slots, prompt_length, got, kv_count):
     _, _, _, span, head_dim = got.shape
     shape = jax.ShapeDtypeStruct((span_slots.shape[0], span, head_dim), BF16)
     return pl.pallas_call(
-        relay_kernel,
+        functools.partial(relay_kernel, kv_count),
         out_shape=(shape, shape),
-        in_specs=[SMEM, SMEM, VMEM],
+        in_specs=[HBM, SMEM, VMEM],
         out_specs=(VMEM, VMEM),
+        scratch_shapes=[pltpu.SMEM(span_slots.shape, jnp.int32), pltpu.SemaphoreType.DMA],
         compiler_params=PARAMS,
         name="relay",
-    )(span_slots, live, got)
+    )(pltpu.with_memory_space_constraint(span_slots, pltpu.HBM), prompt_length, got)
 
 
 def step(
@@ -328,21 +399,21 @@
     span_rows = row_count // (2 * seq_count)
     kv_local = kv_all // head_count
     token_count, heads, _ = queries.shape
-    length = prompt_length[0]
     score_scale = 1.0 / math.sqrt(head_dim)
     shard_rows = slot_count * span_rows
-    seq_index = lax.axis_index("seq")
-    shard_start = seq_index * shard_rows
-
-    packed, mine, away, bias, new_bias = pack(
+    ways = math.gcd(4, seq_count)
+
+    packed, mine, away, bias, new_bias, query, fresh_keys, fresh_values = pack(
         cache_keys,
         cache_values,
         span_slots,
         prompt_length,
         decode_offsets,
+        queries,
+        new_keys,
+        new_values,
         seq_count,
         head_count,
-        heads,
     )
     flat = (2, row_count * kv_local, head_dim)
     blocks = [mine.reshape(flat)]
@@ -362,37 +433,35 @@
         tiled=True,
     )
 
-    state = attend(
-        queries,
-        new_keys.reshape(token_count * kv_local, head_dim),
-        new_values.reshape(token_count * kv_local, head_dim),
-        new_bias,
-        bias,
-        blocks,
-        score_scale,
-    )
-    stride = 1
-    while stride < seq_count:
-        ways = 4 if stride == 1 and seq_count > 4 else 2
-        last = stride * ways >= seq_count
-        states = [state]
-        for way in range(1, ways):
-            pairs = [(s, s ^ (way * stride)) for s in range(seq_count)]
-            states.append(lax.ppermute(state, "seq", pairs))
-        state = merge(states, last)
-        stride *= ways
-
-    live = jnp.clip(length - shard_start, 0, shard_rows) * kv_local
+    pieces = attend(
+        query, fresh_keys, fresh_values, new_bias, bias, blocks, score_scale, ways
+    )
+    per = token_count * heads // ways
+
+    def swapped(x, distance):
+        return lax.ppermute(x, "seq", [(s, s ^ distance) for s in range(seq_count)])
+
+    states = [pieces[0]] + [swapped(pieces[way], way) for way in range(1, ways)]
+    distance = ways
+    state = merge(states, per, distance >= seq_count)
+    while distance < seq_count:
+        other = swapped(state, distance)
+        distance *= 2
+        state = merge([state, other], per, distance >= seq_count)
+    finished = [state] + [swapped(state, way) for way in range(1, ways)]
+    attended = join(finished)
+
     relaid_keys, relaid_values = relay(
         span_slots,
-        live.reshape(1),
+        prompt_length,
         got.reshape(cycle_size, 2, 2, span_rows * kv_local, head_dim),
+        kv_local,
     )
     whole = (shard_rows, kv_local, head_dim)
     return (
         relaid_keys.reshape(whole),
         relaid_values.reshape(whole),
-        state.reshape(token_count, heads, head_dim),
+        attended.reshape(token_count, heads, head_dim),
     )
 
 

time: 49.2 us -> 49.4 us (level)
  starting transfers between devices: 17.1 us -> 20.3 us
  waiting for transfers between devices: 22.8 us -> 20.6 us
  local copies, waits for them, and re-layouts: 0.67 us -> 0 us
    ppermute x4 -> x7, starting transfers between devices: 6.56 us -> 10 us  [swapped(): return lax.ppermute(x, 'seq', [(s, s ^ distance) for s in range(seq_count)])]
    ppermute x4 -> x7, waiting for transfers between devices: 12 us -> 9.77 us  [swapped(): return lax.ppermute(x, 'seq', [(s, s ^ distance) for s in range(seq_count)])]
    unnamed x10 -> x0, local copies, waits for them, and re-layouts: 0.67 us -> none
    pallas_call x4 -> x5, Pallas kernels: 5.16 us -> 4.66 us  [the longest x1 1.76 us: relay(): pl.pallas_call(functools.partial(relay_kernel, kv_count), out_shape=(shap...]
  transfers between devices with their start and end apart: 6 -> 9, of which waited for: 5 -> 8; matrix products, arithmetic and copies ran while one was open for 0% -> 0% of each run, Pallas kernels for 7% -> 6%
where the time goes in v5:
time: 49.4 us; the launch traced here: 49.1 us
  waiting for transfers between devices  20.6 us (42%)
  starting transfers between devices  20.3 us (41%)
  Pallas kernels  6.84 us (14%)
  between operations  1.33 us (3%)
    ppermute x1, waiting for transfers between devices, step(): lax.ppermute(away[shift - 1].reshape(flat), 'head', [(h, (h + shift) % he...  10.9 us
    ppermute x7, starting transfers between devices, swapped(): return lax.ppermute(x, 'seq', [(s, s ^ distance) for s in range(seq_count)])  10 us
    ppermute x7, waiting for transfers between devices, swapped(): return lax.ppermute(x, 'seq', [(s, s ^ distance) for s in range(seq_count)])  9.77 us
    all_to_all x1, starting transfers between devices, step(): lax.all_to_all(packed.reshape(cycle_size, 2, 2 * span_rows * kv_local, he...  8.37 us
    pallas_call x1, Pallas kernels, pack(): pl.pallas_call(functools.partial(pack_kernel, rows // 2, group), out_shap...  2.19 us
    ppermute x1, starting transfers between devices, step(): lax.ppermute(away[shift - 1].reshape(flat), 'head', [(h, (h + shift) % he...  1.93 us
    pallas_call x1, Pallas kernels, relay(): pl.pallas_call(functools.partial(relay_kernel, kv_count), out_shape=(shap...  1.76 us
    pallas_call x1, Pallas kernels, attend(): pl.pallas_call(functools.partial(attend_kernel, score_scale, ways), out_s...  1.52 us
  transfers between devices with their start and end apart: 9, of which 8 were waited for; matrix products, arithmetic and copies ran while one was open for 0% of the time, Pallas kernels for 6%

profile of v5, /device:TPU:0, one launch (start us, length us, event | category | flops | bytes accessed | tf_op | source)
XLA Modules:
  0.0 49.1 jit_solution(7446545095770073583)
XLA Ops:
  1.3 2.2 %pack.1 = (bf16[2,8,2,32,2,128]{5,4,3,2,1,0:T(2,128)(2,1)}, bf16[2,8,32,2,128]{4,3,2,1,0:T(2,128)(2,1)S(1)}, bf16[1,2,8,32,2,128]{5,4,3,2,1,0:T(2,128)(2,1)S(1)}...) custom-call(bf16[8,32,2,2,128]{4,3,2,1,0:T(2,128)(2,1)} %bitcast.14,, ...), custom_call_target="tpu_custom_call" | custom-call | tf_op jit(solution)/shard_map/pack/pallas_call | solution.py:175
  3.5 8.4 %all-to-all-start = ((bf16[16,2,64,128]{3,2,1,0:T(8,128)(2,1)}), bf16[16,2,64,128]{3,2,1,0:T(8,128)(2,1)S(1)}, u32[]{:S(2)}, u32[]{:S(2)}) async-start(bf16[16,2,64,128]{3,2,1,0:T(8,128)(2,1)} %bitcast.4), calls=%async_computation | async-start | bytes 1048576 | tf_op jit(solution)/shard_map/all_to_all | solution.py:428
  11.9 1.9 %collective-permute-start = (bf16[2,512,128]{2,1,0:T(8,128)(2,1)S(1)}, bf16[2,512,128]{2,1,0:T(8,128)(2,1)S(1)}, u32[]{:S(2)}, u32[]{:S(2)}) collective-permute-start(bf16[2,512,128]{2,1,0:T(8,128)(2,1)S(1)} %bitcast.13), channel_id=1, source_target_pairs={{0,16},{16,0},{1,17},{17,1},{2,18},{18,2},{3,19},{19,3},{4,20},{20... | collective-permute-start | bytes 786440 | tf_op jit(solution)/shard_map/ppermute | solution.py:422
  13.8 10.9 %collective-permute-done.rest_1_ = bf16[2,512,128]{2,1,0:T(8,128)(2,1)S(1)} collective-permute-done((bf16[2,512,128]{2,1,0:T(8,128)(2,1)S(1)}, bf16[2,512,128]{2,1,0:T(8,128)(2,1)S(1)}, u32[]{:S(2)}, u32[]{:S(2)}) %collective-permute-start) | collective-permute-done | bytes 262176 | tf_op jit(solution)/shard_map/ppermute | solution.py:422
  24.6 1.5 %attend.1 = (bf16[144,128]{1,0:T(8,128)(2,1)S(1)}, bf16[144,128]{1,0:T(8,128)(2,1)S(1)}, bf16[144,128]{1,0:T(8,128)(2,1)S(1)}, bf16[144,128]{1,0:T(8,128)(2,1)S(1)}) custom-call(bf16[16,32,128]{2,1,0:T(8,128)(2,1)S(1)} %get-tuple-element.20.query_ref, bf16[32,128]{1,0:T(8,128)(2,1)S(1)} %get-tuple-element.21.new_keys_ref, ...), custom_call_target="tpu_custom_call" | custom-call | tf_op jit(solution)/shard_map/attend/pallas_call | solution.py:251
  26.2 1.5 %collective-permute-start.1 = (bf16[144,128]{1,0:T(8,128)(2,1)S(1)}, bf16[144,128]{1,0:T(8,128)(2,1)S(1)}, u32[]{:S(2)}, u32[]{:S(2)}) collective-permute-start(bf16[144,128]{1,0:T(8,128)(2,1)S(1)} %get-tuple-element.28), channel_id=1, source_target_pairs={{0,2},{2,0},{4,6},{6,4},{8,10},{10,8},{12,14},{14,12},{1,3},{3,1},... | collective-permute-start | bytes 110600 | tf_op jit(solution)/shard_map/ppermute | solution.py:442
  27.7 1.8 %collective-permute-start.2 = (bf16[144,128]{1,0:T(8,128)(2,1)S(1)}, bf16[144,128]{1,0:T(8,128)(2,1)S(1)}, u32[]{:S(2)}, u32[]{:S(2)}) collective-permute-start(bf16[144,128]{1,0:T(8,128)(2,1)S(1)} %get-tuple-element.29), channel_id=1, source_target_pairs={{0,4},{2,6},{4,0},{6,2},{8,12},{10,14},{12,8},{14,10},{1,5},{3,7},... | collective-permute-start | bytes 110600 | tf_op jit(solution)/shard_map/ppermute | solution.py:442
  29.5 0.2 collective-permute-start.3
  29.7 0.5 collective-permute-done.1.refs_1_
  30.2 1.5 %collective-permute-done.2.refs_2_ = bf16[144,128]{1,0:T(8,128)(2,1)S(1)} collective-permute-done((bf16[144,128]{1,0:T(8,128)(2,1)S(1)}, bf16[144,128]{1,0:T(8,128)(2,1)S(1)}, u32[]{:S(2)}, u32[]{:S(2)}) %collective-permute-start.2) | collective-permute-done | bytes 36896 | tf_op jit(solution)/shard_map/ppermute | solution.py:442
  31.7 2.7 %collective-permute-done.3.refs_3_ = bf16[144,128]{1,0:T(8,128)(2,1)S(1)} collective-permute-done((bf16[144,128]{1,0:T(8,128)(2,1)S(1)}, bf16[144,128]{1,0:T(8,128)(2,1)S(1)}, u32[]{:S(2)}, u32[]{:S(2)}) %collective-permute-start.3) | collective-permute-done | bytes 36896 | tf_op jit(solution)/shard_map/ppermute | solution.py:442
  34.4 0.4 merge.2.refs_0_
  34.7 2.9 %collective-permute-start.4 = (f32[136,128]{1,0:T(8,128)S(1)}, f32[136,128]{1,0:T(8,128)S(1)}, u32[]{:S(2)}, u32[]{:S(2)}) collective-permute-start(f32[136,128]{1,0:T(8,128)S(1)} %merge.2.refs_0_), channel_id=1, source_target_pairs={{0,8},{2,10},{4,12},{6,14},{8,0},{10,2},{12,4},{14,6},{1,9},{3,11}... | collective-permute-start | bytes 208904 | tf_op jit(solution)/shard_map/ppermute | solution.py:442
  37.7 2.9 %collective-permute-done.4.refs_1_ = f32[136,128]{1,0:T(8,128)S(1)} collective-permute-done((f32[136,128]{1,0:T(8,128)S(1)}, f32[136,128]{1,0:T(8,128)S(1)}, u32[]{:S(2)}, u32[]{:S(2)}) %collective-permute-start.4) | collective-permute-done | bytes 69664 | tf_op jit(solution)/shard_map/ppermute | solution.py:442
  40.5 0.3 merge.3.refs_0_
  40.9 0.7 %collective-permute-start.5 = (bf16[128,128]{1,0:T(8,128)(2,1)S(1)}, bf16[128,128]{1,0:T(8,128)(2,1)S(1)}, u32[]{:S(2)}, u32[]{:S(2)}) collective-permute-start(bf16[128,128]{1,0:T(8,128)(2,1)S(1)} %merge.3.refs_0_), channel_id=1, source_target_pairs={{0,2},{2,0},{4,6},{6,4},{8,10},{10,8},{12,14},{14,12},{1,3},{3,1},... | collective-permute-start | bytes 98312 | tf_op jit(solution)/shard_map/ppermute | solution.py:442
  41.5 0.1 collective-permute-start.6
  41.6 2.8 %collective-permute-start.7 = (bf16[128,128]{1,0:T(8,128)(2,1)S(1)}, bf16[128,128]{1,0:T(8,128)(2,1)S(1)}, u32[]{:S(2)}, u32[]{:S(2)}) collective-permute-start(bf16[128,128]{1,0:T(8,128)(2,1)S(1)} %merge.3.refs_0_), channel_id=1, source_target_pairs={{0,6},{2,4},{4,2},{6,0},{8,14},{10,12},{12,10},{14,8},{1,7},{3,5},... | collective-permute-start | bytes 98312 | tf_op jit(solution)/shard_map/ppermute | solution.py:442
  44.4 0.4 collective-permute-done.5.refs_1_
  44.9 0.6 %collective-permute-done.6.refs_2_ = bf16[128,128]{1,0:T(8,128)(2,1)S(1)} collective-permute-done((bf16[128,128]{1,0:T(8,128)(2,1)S(1)}, bf16[128,128]{1,0:T(8,128)(2,1)S(1)}, u32[]{:S(2)}, u32[]{:S(2)}) %collective-permute-start.6) | collective-permute-done | bytes 32800 | tf_op jit(solution)/shard_map/ppermute | solution.py:442
  45.5 1.2 %collective-permute-done.7.refs_3_ = bf16[128,128]{1,0:T(8,128)(2,1)S(1)} collective-permute-done((bf16[128,128]{1,0:T(8,128)(2,1)S(1)}, bf16[128,128]{1,0:T(8,128)(2,1)S(1)}, u32[]{:S(2)}, u32[]{:S(2)}) %collective-permute-start.7) | collective-permute-done | bytes 32800 | tf_op jit(solution)/shard_map/ppermute | solution.py:442
  46.7 0.7 %join.1 = bf16[512,128]{1,0:T(8,128)(2,1)} custom-call(bf16[128,128]{1,0:T(8,128)(2,1)S(1)} %merge.3.refs_0_, bf16[128,128]{1,0:T(8,128)(2,1)S(1)} %collective-permute-done.5.refs_1_, bf16[128,128]{1,0:T(8,128)(2,1)S(1)} %collective-permute-done.6.refs_2_, bf16[128,128]{1,0:T(8,128)(2,1)S(1)} %collective-permute-done.7.refs_3_), custom_call_target="tpu_custom_call" | custom-call | tf_op jit(solution)/shard_map/join/pallas_call | solution.py:340
  47.4 0.0 all-to-all-done
  47.4 1.8 %relay.1 = (bf16[32,32,128]{2,1,0:T(8,128)(2,1)}, bf16[32,32,128]{2,1,0:T(8,128)(2,1)}) custom-call(s32[32]{0:T(128)} %slots_hbm.3, s32[1]{0:T(128)S(6)} %copy.11.length_ref, bf16[16,2,2,32,128]{4,3,2,1,0:T(8,128)(2,1)S(1)} %bitcast.11), custom_call_target="tpu_custom_call" | custom-call | tf_op jit(solution)/shard_map/relay/pallas_call | solution.py:373
Async XLA Ops:
  3.5 43.9 %all-to-all-start = ((bf16[16,2,64,128]{3,2,1,0:T(8,128)(2,1)}), bf16[16,2,64,128]{3,2,1,0:T(8,128)(2,1)S(1)}, u32[]{:S(2)}, u32[]{:S(2)}) async-start(bf16[16,2,64,128]{3,2,1,0:T(8,128)(2,1)} %bitcast.4), calls=%async_computation | async-start | bytes 1048576 | tf_op jit(solution)/shard_map/all_to_all | solution.py:428
  11.9 12.8 %collective-permute-start = (bf16[2,512,128]{2,1,0:T(8,128)(2,1)S(1)}, bf16[2,512,128]{2,1,0:T(8,128)(2,1)S(1)}, u32[]{:S(2)}, u32[]{:S(2)}) collective-permute-start(bf16[2,512,128]{2,1,0:T(8,128)(2,1)S(1)} %bitcast.13), channel_id=1, source_target_pairs={{0,16},{16,0},{1,17},{17,1},{2,18},{18,2},{3,19},{19,3},{4,20},{20... | collective-permute-start | bytes 786440 | tf_op jit(solution)/shard_map/ppermute | solution.py:422
  26.2 4.0 %collective-permute-start.1 = (bf16[144,128]{1,0:T(8,128)(2,1)S(1)}, bf16[144,128]{1,0:T(8,128)(2,1)S(1)}, u32[]{:S(2)}, u32[]{:S(2)}) collective-permute-start(bf16[144,128]{1,0:T(8,128)(2,1)S(1)} %get-tuple-element.28), channel_id=1, source_target_pairs={{0,2},{2,0},{4,6},{6,4},{8,10},{10,8},{12,14},{14,12},{1,3},{3,1},... | collective-permute-start | bytes 110600 | tf_op jit(solution)/shard_map/ppermute | solution.py:442
  27.7 4.0 %collective-permute-start.2 = (bf16[144,128]{1,0:T(8,128)(2,1)S(1)}, bf16[144,128]{1,0:T(8,128)(2,1)S(1)}, u32[]{:S(2)}, u32[]{:S(2)}) collective-permute-start(bf16[144,128]{1,0:T(8,128)(2,1)S(1)} %get-tuple-element.29), channel_id=1, source_target_pairs={{0,4},{2,6},{4,0},{6,2},{8,12},{10,14},{12,8},{14,10},{1,5},{3,7},... | collective-permute-start | bytes 110600 | tf_op jit(solution)/shard_map/ppermute | solution.py:442
  29.5 4.9 %collective-permute-start.3 = (bf16[144,128]{1,0:T(8,128)(2,1)S(1)}, bf16[144,128]{1,0:T(8,128)(2,1)S(1)}, u32[]{:S(2)}, u32[]{:S(2)}) collective-permute-start(bf16[144,128]{1,0:T(8,128)(2,1)S(1)} %get-tuple-element.30), channel_id=1, source_target_pairs={{0,6},{2,4},{4,2},{6,0},{8,14},{10,12},{12,10},{14,8},{1,7},{3,5},... | collective-permute-start | bytes 110600 | tf_op jit(solution)/shard_map/ppermute | solution.py:442
  34.7 5.8 %collective-permute-start.4 = (f32[136,128]{1,0:T(8,128)S(1)}, f32[136,128]{1,0:T(8,128)S(1)}, u32[]{:S(2)}, u32[]{:S(2)}) collective-permute-start(f32[136,128]{1,0:T(8,128)S(1)} %merge.2.refs_0_), channel_id=1, source_target_pairs={{0,8},{2,10},{4,12},{6,14},{8,0},{10,2},{12,4},{14,6},{1,9},{3,11}... | collective-permute-start | bytes 208904 | tf_op jit(solution)/shard_map/ppermute | solution.py:442
  40.9 4.0 %collective-permute-start.5 = (bf16[128,128]{1,0:T(8,128)(2,1)S(1)}, bf16[128,128]{1,0:T(8,128)(2,1)S(1)}, u32[]{:S(2)}, u32[]{:S(2)}) collective-permute-start(bf16[128,128]{1,0:T(8,128)(2,1)S(1)} %merge.3.refs_0_), channel_id=1, source_target_pairs={{0,2},{2,0},{4,6},{6,4},{8,10},{10,8},{12,14},{14,12},{1,3},{3,1},... | collective-permute-start | bytes 98312 | tf_op jit(solution)/shard_map/ppermute | solution.py:442
  41.5 3.9 %collective-permute-start.6 = (bf16[128,128]{1,0:T(8,128)(2,1)S(1)}, bf16[128,128]{1,0:T(8,128)(2,1)S(1)}, u32[]{:S(2)}, u32[]{:S(2)}) collective-permute-start(bf16[128,128]{1,0:T(8,128)(2,1)S(1)} %merge.3.refs_0_), channel_id=1, source_target_pairs={{0,4},{2,6},{4,0},{6,2},{8,12},{10,14},{12,8},{14,10},{1,5},{3,7},... | collective-permute-start | bytes 98312 | tf_op jit(solution)/shard_map/ppermute | solution.py:442
  41.6 5.0 %collective-permute-start.7 = (bf16[128,128]{1,0:T(8,128)(2,1)S(1)}, bf16[128,128]{1,0:T(8,128)(2,1)S(1)}, u32[]{:S(2)}, u32[]{:S(2)}) collective-permute-start(bf16[128,128]{1,0:T(8,128)(2,1)S(1)} %merge.3.refs_0_), channel_id=1, source_target_pairs={{0,6},{2,4},{4,2},{6,0},{8,14},{10,12},{12,10},{14,8},{1,7},{3,5},... | collective-permute-start | bytes 98312 | tf_op jit(solution)/shard_map/ppermute | solution.py:442

commit v6 on v5

--- a/solution.py
+++ b/solution.py
@@ -12,6 +12,7 @@
 BF16 = jnp.bfloat16
 F32 = jnp.float32
 DEAD = -1e30
+NOWHERE = 1 << 30
 STAT_ROWS = 16
 WIDE_ROWS = 8
 LANES = 128
@@ -55,28 +56,27 @@
 
 def pack_kernel(
     span_rows,
-    group,
     keys_ref,
     values_ref,
     slots_hbm,
-    length_ref,
-    depth_hbm,
-    *rest,
+    query_hbm,
+    send_ref,
+    mine_ref,
+    away_ref,
+    place_ref,
+    query_ref,
+    slots_ref,
+    in_sems,
+    out_sems,
+    sems,
 ):
-    staged, (send_ref, mine_ref, away_ref, bias_ref, new_bias_ref) = rest[:3], rest[3:8]
-    targets = rest[8:11]
-    slots_ref, depth_ref, in_sems, out_sems, fact_sems, stage_sems = rest[11:]
     seq_count, _, head_count, kv_count, _ = keys_ref.shape
     slot_count = slots_hbm.shape[0]
-    token_count = depth_hbm.shape[0]
     me = lax.axis_index("head")
     seq_index = lax.axis_index("seq")
-    facts = [
-        pltpu.make_async_copy(source, target, fact_sems.at[at])
-        for at, (source, target) in enumerate(
-            ((slots_hbm, slots_ref), (depth_hbm, depth_ref))
-        )
-    ]
+    facts = pltpu.make_async_copy(slots_hbm, slots_ref, sems.at[0])
+    facts.start()
+    staged = pltpu.make_async_copy(query_hbm, query_ref, sems.at[1])
     blocks = []
     for shift in list(range(1, head_count)) + [0]:
         h = lax.rem(me + shift, head_count)
@@ -86,14 +86,11 @@
             copy.start()
             out = pltpu.make_async_copy(target, send_ref.at[h, :, c], out_sems.at[shift, c])
             blocks.append((copy, out))
-    stages = [
-        pltpu.make_async_copy(source, target, stage_sems.at[at])
-        for at, (source, target) in enumerate(zip(staged, targets))
-    ]
-    for copy in facts + stages:
-        copy.start()
-    for fact in facts:
-        fact.wait()
+    staged.start()
+    for copy, out in blocks:
+        copy.wait()
+        out.start()
+    facts.wait()
 
     wanted = []
     for b in range(head_count):
@@ -105,7 +102,7 @@
         return tuple(jnp.where(slot == w, t, p) for w, p in zip(wanted, places))
 
     places = lax.fori_loop(0, slot_count, look, tuple(jnp.int32(0) for _ in wanted))
-    column = lax.broadcasted_iota(jnp.int32, (1, bias_ref.shape[1]), 1)
+    column = lax.broadcasted_iota(jnp.int32, (1, place_ref.shape[1]), 1)
     kv, rest = split_off(column, kv_count)
     row, rest = split_off(rest, span_rows)
     half, rest = split_off(rest, 2)
@@ -113,122 +110,76 @@
     span = jnp.zeros_like(column)
     for at, place in enumerate(places):
         span = jnp.where(2 * block + half == at, place, span)
-    alive = (turn * slot_count + span) * span_rows + row < length_ref[0]
+    position = (turn * slot_count + span) * span_rows + row
     for g in range(kv_count):
-        bias_ref[g : g + 1, :] = jnp.where(alive & (kv == g), 0.0, DEAD)
-
-    column = lax.broadcasted_iota(jnp.int32, (1, new_bias_ref.shape[2]), 1)
-    kv, token = split_off(column, kv_count)
-    depth = jnp.zeros_like(column)
-    for t in range(token_count):
-        depth = jnp.where(token == t, depth_ref[t], depth)
-    for t in range(token_count):
-        limit = jnp.where(seq_index == 0, depth_ref[t], -1)
-        for g in range(kv_count):
-            seen = jnp.where((depth <= limit) & (kv == g), 0.0, DEAD)
-            new_bias_ref[g, t * group : (t + 1) * group, :] = jnp.broadcast_to(
-                seen, (group, seen.shape[1])
-            )
-
-    for copy, out in blocks:
-        copy.wait()
-        out.start()
+        place_ref[g : g + 1, :] = jnp.where(kv == g, position, NOWHERE)
     for _, out in blocks:
         out.wait()
-    for copy in stages:
-        copy.wait()
-
-
-def pack(
-    cache_keys,
-    cache_values,
-    span_slots,
-    prompt_length,
-    depth,
-    queries,
-    new_keys,
-    new_values,
-    seq_count,
-    head_count,
-):
+    staged.wait()
+
+
+def pack(cache_keys, cache_values, span_slots, queries, seq_count, head_count):
     row_count, kv_all, head_dim = cache_keys.shape
     kv = kv_all // head_count
     rows = row_count // seq_count
     split = (seq_count, rows, head_count, kv, head_dim)
     block = (seq_count, rows, kv, head_dim)
-    tokens, heads, _ = queries.shape
-    group = heads // kv
-    fresh = (tokens * kv, head_dim)
     inputs = [
-        x if x is prompt_length else pltpu.with_memory_space_constraint(x, pltpu.HBM)
-        for x in (
-            cache_keys.reshape(split),
-            cache_values.reshape(split),
-            span_slots,
-            prompt_length,
-            depth,
-            queries,
-            new_keys.reshape(fresh),
-            new_values.reshape(fresh),
-        )
+        pltpu.with_memory_space_constraint(x, pltpu.HBM)
+        for x in (cache_keys.reshape(split), cache_values.reshape(split), span_slots, queries)
     ]
     return pl.pallas_call(
-        functools.partial(pack_kernel, rows // 2, group),
+        functools.partial(pack_kernel, rows // 2),
         out_shape=(
             jax.ShapeDtypeStruct((head_count, seq_count, 2, rows, kv, head_dim), BF16),
             jax.ShapeDtypeStruct((2,) + block, BF16),
             jax.ShapeDtypeStruct((head_count - 1, 2) + block, BF16),
-            jax.ShapeDtypeStruct((kv, head_count * row_count * kv), F32),
-            jax.ShapeDtypeStruct((kv, tokens * group, tokens * kv), F32),
+            jax.ShapeDtypeStruct((kv, head_count * row_count * kv), jnp.int32),
             jax.ShapeDtypeStruct(queries.shape, BF16),
-            jax.ShapeDtypeStruct(fresh, BF16),
-            jax.ShapeDtypeStruct(fresh, BF16),
         ),
-        in_specs=[HBM] * 3 + [SMEM] + [HBM] * 4,
-        out_specs=(HBM,) + (VMEM,) * 7,
+        in_specs=[HBM] * len(inputs),
+        out_specs=(HBM,) + (VMEM,) * 4,
         scratch_shapes=[
             pltpu.SMEM(span_slots.shape, jnp.int32),
-            pltpu.SMEM(depth.shape, jnp.int32),
             pltpu.SemaphoreType.DMA((head_count, 2)),
             pltpu.SemaphoreType.DMA((head_count, 2)),
             pltpu.SemaphoreType.DMA((2,)),
-            pltpu.SemaphoreType.DMA((3,)),
         ],
         compiler_params=PARAMS,
         name="pack",
     )(*inputs)
 
 
-def attend_kernel(
-    score_scale, ways, query_ref, new_keys_ref, new_values_ref, new_bias_ref, bias_ref, *rest
-):
+def softmax_parts(scores, values):
+    peak = jnp.max(scores, axis=1, keepdims=True)
+    weights = jnp.exp(scores - peak)
+    total = jnp.sum(weights, axis=1, keepdims=True)
+    weighted = jnp.dot(weights.astype(BF16), values, preferred_element_type=F32)
+    return peak, total, weighted
+
+
+def stat_lanes(peak, total, head_dim):
+    lane = lax.broadcasted_iota(jnp.int32, (peak.shape[0], head_dim), 1)
+    stats = jnp.zeros((peak.shape[0], head_dim), F32)
+    for at, part in enumerate(three_parts(peak) + three_parts(total)):
+        stats = jnp.where(lane == at, part, stats)
+    return stats.astype(BF16)
+
+
+def attend_kernel(score_scale, ways, length_ref, query_ref, place_ref, *rest):
     *block_refs, rows_buf, stat_buf = rest
     block_refs, out_refs = block_refs[:-ways], block_refs[-ways:]
     tokens, heads, head_dim = query_ref.shape
-    kv_count = bias_ref.shape[0]
+    kv_count = place_ref.shape[0]
     group = heads // kv_count
-    lane = lax.broadcasted_iota(jnp.int32, (tokens * group, head_dim), 1)
     keys = jnp.concatenate([ref[0] for ref in block_refs], axis=0)
     values = jnp.concatenate([ref[1] for ref in block_refs], axis=0)
     for g in range(kv_count):
         query = query_ref[:, g * group : (g + 1) * group, :].reshape(tokens * group, head_dim)
-        scores = dot_rows(query, keys) * score_scale + bias_ref[g : g + 1, :]
-        fresh = dot_rows(query, new_keys_ref[...]) * score_scale + new_bias_ref[g]
-        peak = jnp.maximum(
-            jnp.max(scores, axis=1, keepdims=True), jnp.max(fresh, axis=1, keepdims=True)
-        )
-        weights = jnp.exp(scores - peak)
-        fresh = jnp.exp(fresh - peak)
-        total = jnp.sum(weights, axis=1, keepdims=True) + jnp.sum(fresh, axis=1, keepdims=True)
-        weighted = jnp.dot(weights.astype(BF16), values, preferred_element_type=F32)
-        weighted = weighted + jnp.dot(
-            fresh.astype(BF16), new_values_ref[...], preferred_element_type=F32
-        )
-        stats = jnp.zeros((tokens * group, head_dim), F32)
-        for at, part in enumerate(three_parts(peak) + three_parts(total)):
-            stats = jnp.where(lane == at, part, stats)
+        bias = jnp.where(place_ref[g : g + 1, :] < length_ref[0], 0.0, DEAD)
+        peak, total, weighted = softmax_parts(dot_rows(query, keys) * score_scale + bias, values)
         rows_buf[:, g] = weighted.astype(BF16).reshape(tokens, group, head_dim)
-        stat_buf[:, g] = stats.astype(BF16).reshape(tokens, group, head_dim)
+        stat_buf[:, g] = stat_lanes(peak, total, head_dim).reshape(tokens, group, head_dim)
     here = lax.rem(lax.axis_index("seq"), ways)
     share = tokens // ways
     per = share * heads
@@ -242,16 +193,16 @@
             out_ref[start : start + STAT_ROWS, :] = turned[:, at * LANES : (at + 1) * LANES]
 
 
-def attend(query, new_keys, new_values, new_bias, bias, blocks, score_scale, ways):
+def attend(length, query, place, blocks, score_scale, ways):
     tokens, heads, head_dim = query.shape
-    kv_count = bias.shape[0]
+    kv_count = place.shape[0]
     group = heads // kv_count
     per = tokens * heads // ways
     piece = jax.ShapeDtypeStruct((per + per // LANES * STAT_ROWS, head_dim), BF16)
     return pl.pallas_call(
         functools.partial(attend_kernel, score_scale, ways),
         out_shape=(piece,) * ways,
-        in_specs=[VMEM] * (5 + len(blocks)),
+        in_specs=[SMEM] + [VMEM] * (2 + len(blocks)),
         out_specs=(VMEM,) * ways,
         scratch_shapes=[
             pltpu.VMEM((tokens, kv_count, group, head_dim), BF16),
@@ -259,12 +210,80 @@
         ],
         compiler_params=PARAMS,
         name="attend",
-    )(query, new_keys, new_values, new_bias, bias, *blocks)
+    )(length, query, place, *blocks)
+
+
+def fresh_kernel(
+    score_scale, ways, query_ref, keys_hbm, values_hbm, depth_hbm, out_ref, keys_ref, values_ref, depth_ref, sems
+):
+    copies = [
+        pltpu.make_async_copy(source, target, sems.at[at])
+        for at, (source, target) in enumerate(
+            ((keys_hbm, keys_ref), (values_hbm, values_ref), (depth_hbm, depth_ref))
+        )
+    ]
+    for copy in copies:
+        copy.start()
+    tokens, heads, head_dim = query_ref.shape
+    kv_count = keys_ref.shape[0] // tokens
+    share = tokens // ways
+    per = share * heads
+    first = lax.rem(lax.axis_index("seq"), ways) * share
+    shape = (per, tokens * kv_count)
+    _, own = split_off(lax.broadcasted_iota(jnp.int32, shape, 0), heads // kv_count)
+    own_kv, own_token = split_off(own, kv_count)
+    new_kv, new_token = split_off(lax.broadcasted_iota(jnp.int32, (1, shape[1]), 1), kv_count)
+    for copy in copies:
+        copy.wait()
+    new_depth = jnp.zeros_like(new_token)
+    for t in range(tokens):
+        new_depth = jnp.where(new_token == t, depth_ref[t], new_depth)
+    own_depth = jnp.zeros_like(own_token)
+    for t in range(share):
+        own_depth = jnp.where(own_token == t, depth_ref[first + t], own_depth)
+    seen = (new_depth <= own_depth) & (new_kv == own_kv)
+    query = query_ref[pl.ds(first, share)].reshape(per, head_dim)
+    scores = dot_rows(query, keys_ref[...]) * score_scale + jnp.where(seen, 0.0, DEAD)
+    peak, total, weighted = softmax_parts(scores, values_ref[...])
+    out_ref[:per, :] = weighted
+    stats = stat_lanes(peak, total, head_dim)
+    row = lax.broadcasted_iota(jnp.int32, (WIDE_ROWS, LANES), 0)
+    for at in range(per // LANES):
+        turned = dot_rows(eye(STAT_ROWS, head_dim), stats[at * LANES : (at + 1) * LANES])
+        peaks = turned[0:1] + turned[1:2] + turned[2:3]
+        totals = turned[3:4] + turned[4:5] + turned[5:6]
+        start = per + at * WIDE_ROWS
+        out_ref[start : start + WIDE_ROWS, :] = jnp.where(row == 0, peaks, totals)
+
+
+def fresh_rows(query, new_keys, new_values, depth, score_scale, ways):
+    tokens, heads, head_dim = query.shape
+    per = tokens * heads // ways
+    flat = (new_keys.shape[0] * new_keys.shape[1], head_dim)
+    inputs = [
+        pltpu.with_memory_space_constraint(x, pltpu.HBM)
+        for x in (new_keys.reshape(flat), new_values.reshape(flat), depth)
+    ]
+    return pl.pallas_call(
+        functools.partial(fresh_kernel, score_scale, ways),
+        out_shape=jax.ShapeDtypeStruct((per + per // LANES * WIDE_ROWS, head_dim), F32),
+        in_specs=[VMEM, HBM, HBM, HBM],
+        out_specs=VMEM,
+        scratch_shapes=[
+            pltpu.VMEM(flat, BF16),
+            pltpu.VMEM(flat, BF16),
+            pltpu.SMEM(depth.shape, jnp.int32),
+            pltpu.SemaphoreType.DMA((3,)),
+        ],
+        compiler_params=PARAMS,
+        name="fresh",
+    )(query, *inputs)
 
 
 def tree(combine, parts):
     while len(parts) > 1:
-        parts = [combine(parts[k], parts[k + 1]) for k in range(0, len(parts), 2)]
+        pairs = [combine(parts[k], parts[k + 1]) for k in range(0, len(parts) - 1, 2)]
+        parts = pairs + parts[len(parts) & ~1 :]
     return parts[0]
 
 
@@ -272,15 +291,14 @@
     *in_refs, out_ref = refs
     head_dim = out_ref.shape[1]
     chunks = per // LANES
-    rows_in = (in_refs[0].shape[0] - per) // chunks
-    split = in_refs[0].dtype == BF16
     turn = eye(LANES, LANES)
     factor_rows = -(-3 * len(in_refs) // STAT_ROWS) * STAT_ROWS
     for at in range(chunks):
         peaks, totals = [], []
         for ref in in_refs:
+            rows_in = (ref.shape[0] - per) // chunks
             stats = ref[per + at * rows_in : per + (at + 1) * rows_in, :].astype(F32)
-            if split:
+            if ref.dtype == BF16:
                 peaks.append(stats[0:1] + stats[1:2] + stats[2:3])
                 totals.append(stats[3:4] + stats[4:5] + stats[5:6])
             else:
@@ -403,17 +421,8 @@
     shard_rows = slot_count * span_rows
     ways = math.gcd(4, seq_count)
 
-    packed, mine, away, bias, new_bias, query, fresh_keys, fresh_values = pack(
-        cache_keys,
-        cache_values,
-        span_slots,
-        prompt_length,
-        decode_offsets,
-        queries,
-        new_keys,
-        new_values,
-        seq_count,
-        head_count,
+    packed, mine, away, place, query = pack(
+        cache_keys, cache_values, span_slots, queries, seq_count, head_count
     )
     flat = (2, row_count * kv_local, head_dim)
     blocks = [mine.reshape(flat)]
@@ -433,21 +442,20 @@
         tiled=True,
     )
 
-    pieces = attend(
-        query, fresh_keys, fresh_values, new_bias, bias, blocks, score_scale, ways
-    )
+    pieces = attend(prompt_length, query, place, blocks, score_scale, ways)
     per = token_count * heads // ways
 
     def swapped(x, distance):
         return lax.ppermute(x, "seq", [(s, s ^ distance) for s in range(seq_count)])
 
     states = [pieces[0]] + [swapped(pieces[way], way) for way in range(1, ways)]
+    fresh = fresh_rows(query, new_keys, new_values, decode_offsets, score_scale, ways)
     distance = ways
-    state = merge(states, per, distance >= seq_count)
     while distance < seq_count:
-        other = swapped(state, distance)
+        state = merge(states, per, False)
+        states = [state, swapped(state, distance)]
         distance *= 2
-        state = merge([state, other], per, distance >= seq_count)
+    state = merge(states + [fresh], per, True)
     finished = [state] + [swapped(state, way) for way in range(1, ways)]
     attended = join(finished)
 

time: 49.4 us -> 48.2 us (0.976)
  waiting for transfers between devices: 20.6 us -> 18.7 us
  Pallas kernels: 6.84 us -> 7.54 us
    ppermute x7, waiting for transfers between devices: 9.77 us -> 8.49 us  [swapped(): return lax.ppermute(x, 'seq', [(s, s ^ distance) for s in range(seq_count)])]
    pallas_call x1 -> x2, Pallas kernels: 2.19 us -> 3.15 us  [the longest x1 1.87 us: pack(): pl.pallas_call(functools.partial(pack_kernel, rows // 2), out_shape=(jax....]
    ppermute x1, waiting for transfers between devices: 10.9 us -> 10.2 us  [step(): lax.ppermute(away[shift - 1].reshape(flat), 'head', [(h, (h + shift) % he...]
  transfers between devices with their start and end apart: 9 -> 9, of which waited for: 8 -> 8; matrix products, arithmetic and copies ran while one was open for 0% -> 0% of each run, Pallas kernels for 6% -> 8%
where the time goes in v6:
time: 48.2 us; the launch traced here: 47.9 us
  starting transfers between devices  20.3 us (42%)
  waiting for transfers between devices  18.7 us (39%)
  Pallas kernels  7.54 us (16%)
  between operations  1.34 us (3%)
    ppermute x1, waiting for transfers between devices, step(): lax.ppermute(away[shift - 1].reshape(flat), 'head', [(h, (h + shift) % he...  10.2 us
    ppermute x7, starting transfers between devices, swapped(): return lax.ppermute(x, 'seq', [(s, s ^ distance) for s in range(seq_count)])  10 us
    ppermute x7, waiting for transfers between devices, swapped(): return lax.ppermute(x, 'seq', [(s, s ^ distance) for s in range(seq_count)])  8.49 us
    all_to_all x1, starting transfers between devices, step(): lax.all_to_all(packed.reshape(cycle_size, 2, 2 * span_rows * kv_local, he...  8.34 us
    ppermute x1, starting transfers between devices, step(): lax.ppermute(away[shift - 1].reshape(flat), 'head', [(h, (h + shift) % he...  1.93 us
    pallas_call x1, Pallas kernels, pack(): pl.pallas_call(functools.partial(pack_kernel, rows // 2), out_shape=(jax....  1.87 us
    pallas_call x1, Pallas kernels, relay(): pl.pallas_call(functools.partial(relay_kernel, kv_count), out_shape=(shap...  1.76 us
    pallas_call x1, Pallas kernels, fresh_rows(): pl.pallas_call(functools.partial(fresh_kernel, score_scale, ways), out_sh...  1.27 us
  transfers between devices with their start and end apart: 9, of which 8 were waited for; matrix products, arithmetic and copies ran while one was open for 0% of the time, Pallas kernels for 8%

profile of v6, /device:TPU:0, one launch (start us, length us, event | category | flops | bytes accessed | tf_op | source)
XLA Modules:
  0.0 47.9 jit_solution(11720231038358278744)
XLA Ops:
  0.6 1.9 %pack.1 = (bf16[2,8,2,32,2,128]{5,4,3,2,1,0:T(2,128)(2,1)}, bf16[2,8,32,2,128]{4,3,2,1,0:T(2,128)(2,1)S(1)}, bf16[1,2,8,32,2,128]{5,4,3,2,1,0:T(2,128)(2,1)S(1)}...) custom-call(bf16[8,32,2,2,128]{4,3,2,1,0:T(2,128)(2,1)} %bitcast.14, bf16[8,32,2,2,128]{4,3,2,1,0:T(2,128)(2,1)} %bitcast.15, ...), custom_call_target="tpu_custom_call" | custom-call | tf_op jit(solution)/shard_map/pack/pallas_call | solution.py:131
  2.5 8.3 %all-to-all-start = ((bf16[16,2,64,128]{3,2,1,0:T(8,128)(2,1)}), bf16[16,2,64,128]{3,2,1,0:T(8,128)(2,1)S(1)}, u32[]{:S(2)}, u32[]{:S(2)}) async-start(bf16[16,2,64,128]{3,2,1,0:T(8,128)(2,1)} %bitcast.2), calls=%async_computation | async-start | bytes 1048576 | tf_op jit(solution)/shard_map/all_to_all | solution.py:437
  10.9 1.9 %collective-permute-start = (bf16[2,512,128]{2,1,0:T(8,128)(2,1)S(1)}, bf16[2,512,128]{2,1,0:T(8,128)(2,1)S(1)}, u32[]{:S(2)}, u32[]{:S(2)}) collective-permute-start(bf16[2,512,128]{2,1,0:T(8,128)(2,1)S(1)} %bitcast.13), channel_id=1, source_target_pairs={{0,16},{16,0},{1,17},{17,1},{2,18},{18,2},{3,19},{19,3},{4,20},{20... | collective-permute-start | bytes 786440 | tf_op jit(solution)/shard_map/ppermute | solution.py:431
  13.4 10.2 %collective-permute-done.rest_1_ = bf16[2,512,128]{2,1,0:T(8,128)(2,1)S(1)} collective-permute-done((bf16[2,512,128]{2,1,0:T(8,128)(2,1)S(1)}, bf16[2,512,128]{2,1,0:T(8,128)(2,1)S(1)}, u32[]{:S(2)}, u32[]{:S(2)}) %collective-permute-start) | collective-permute-done | bytes 262176 | tf_op jit(solution)/shard_map/ppermute | solution.py:431
  23.6 1.2 %attend.1 = (bf16[144,128]{1,0:T(8,128)(2,1)S(1)}, bf16[144,128]{1,0:T(8,128)(2,1)S(1)}, bf16[144,128]{1,0:T(8,128)(2,1)S(1)}, bf16[144,128]{1,0:T(8,128)(2,1)S(1)}) custom-call(s32[1]{0:T(128)S(6)} %copy.11.length_ref, bf16[16,32,128]{2,1,0:T(8,128)(2,1)S(1)} %get-tuple-element.17.query_ref, s32[2,1024]{1,0:T(2,128)S(1)} %get-tuple-element.18.place_ref, ...), custom_call_target="tpu_custom_call" | custom-call | tf_op jit(solution)/shard_map/attend/pallas_call | solution.py:202
  24.9 1.5 %collective-permute-start.1 = (bf16[144,128]{1,0:T(8,128)(2,1)S(1)}, bf16[144,128]{1,0:T(8,128)(2,1)S(1)}, u32[]{:S(2)}, u32[]{:S(2)}) collective-permute-start(bf16[144,128]{1,0:T(8,128)(2,1)S(1)} %get-tuple-element.22), channel_id=1, source_target_pairs={{0,2},{2,0},{4,6},{6,4},{8,10},{10,8},{12,14},{14,12},{1,3},{3,1},... | collective-permute-start | bytes 110600 | tf_op jit(solution)/shard_map/ppermute | solution.py:449
  26.4 1.8 %collective-permute-start.2 = (bf16[144,128]{1,0:T(8,128)(2,1)S(1)}, bf16[144,128]{1,0:T(8,128)(2,1)S(1)}, u32[]{:S(2)}, u32[]{:S(2)}) collective-permute-start(bf16[144,128]{1,0:T(8,128)(2,1)S(1)} %get-tuple-element.23), channel_id=1, source_target_pairs={{0,4},{2,6},{4,0},{6,2},{8,12},{10,14},{12,8},{14,10},{1,5},{3,7},... | collective-permute-start | bytes 110600 | tf_op jit(solution)/shard_map/ppermute | solution.py:449
  28.2 0.2 collective-permute-start.3
  28.4 0.5 collective-permute-done.1.refs_1_
  28.9 1.5 %collective-permute-done.2.refs_2_ = bf16[144,128]{1,0:T(8,128)(2,1)S(1)} collective-permute-done((bf16[144,128]{1,0:T(8,128)(2,1)S(1)}, bf16[144,128]{1,0:T(8,128)(2,1)S(1)}, u32[]{:S(2)}, u32[]{:S(2)}) %collective-permute-start.2) | collective-permute-done | bytes 36896 | tf_op jit(solution)/shard_map/ppermute | solution.py:449
  30.4 2.7 %collective-permute-done.3.refs_3_ = bf16[144,128]{1,0:T(8,128)(2,1)S(1)} collective-permute-done((bf16[144,128]{1,0:T(8,128)(2,1)S(1)}, bf16[144,128]{1,0:T(8,128)(2,1)S(1)}, u32[]{:S(2)}, u32[]{:S(2)}) %collective-permute-start.3) | collective-permute-done | bytes 36896 | tf_op jit(solution)/shard_map/ppermute | solution.py:449
  33.1 0.4 merge.2.refs_0_
  33.4 2.9 %collective-permute-start.4 = (f32[136,128]{1,0:T(8,128)S(1)}, f32[136,128]{1,0:T(8,128)S(1)}, u32[]{:S(2)}, u32[]{:S(2)}) collective-permute-start(f32[136,128]{1,0:T(8,128)S(1)} %merge.2.refs_0_), channel_id=1, source_target_pairs={{0,8},{2,10},{4,12},{6,14},{8,0},{10,2},{12,4},{14,6},{1,9},{3,11}... | collective-permute-start | bytes 208904 | tf_op jit(solution)/shard_map/ppermute | solution.py:449
  36.4 1.3 %fresh.1.refs_2_ = f32[136,128]{1,0:T(8,128)S(1)} custom-call(bf16[16,32,128]{2,1,0:T(8,128)(2,1)S(1)} %get-tuple-element.17.query_ref, bf16[32,128]{1,0:T(8,128)(2,1)} %bitcast.17, bf16[32,128]{1,0:T(8,128)(2,1)} %bitcast.18, s32[16]{0:T(128)} %depth_hbm.1), custom_call_target="tpu_custom_call" | custom-call | tf_op jit(solution)/shard_map/fresh/pallas_call | solution.py:267
  37.7 1.6 %collective-permute-done.4.refs_1_ = f32[136,128]{1,0:T(8,128)S(1)} collective-permute-done((f32[136,128]{1,0:T(8,128)S(1)}, f32[136,128]{1,0:T(8,128)S(1)}, u32[]{:S(2)}, u32[]{:S(2)}) %collective-permute-start.4) | collective-permute-done | bytes 69664 | tf_op jit(solution)/shard_map/ppermute | solution.py:449
  39.3 0.3 merge.3.refs_0_
  39.6 0.7 %collective-permute-start.5 = (bf16[128,128]{1,0:T(8,128)(2,1)S(1)}, bf16[128,128]{1,0:T(8,128)(2,1)S(1)}, u32[]{:S(2)}, u32[]{:S(2)}) collective-permute-start(bf16[128,128]{1,0:T(8,128)(2,1)S(1)} %merge.3.refs_0_), channel_id=1, source_target_pairs={{0,2},{2,0},{4,6},{6,4},{8,10},{10,8},{12,14},{14,12},{1,3},{3,1},... | collective-permute-start | bytes 98312 | tf_op jit(solution)/shard_map/ppermute | solution.py:449
  40.3 0.1 collective-permute-start.6
  40.4 2.8 %collective-permute-start.7 = (bf16[128,128]{1,0:T(8,128)(2,1)S(1)}, bf16[128,128]{1,0:T(8,128)(2,1)S(1)}, u32[]{:S(2)}, u32[]{:S(2)}) collective-permute-start(bf16[128,128]{1,0:T(8,128)(2,1)S(1)} %merge.3.refs_0_), channel_id=1, source_target_pairs={{0,6},{2,4},{4,2},{6,0},{8,14},{10,12},{12,10},{14,8},{1,7},{3,5},... | collective-permute-start | bytes 98312 | tf_op jit(solution)/shard_map/ppermute | solution.py:449
  43.2 0.4 collective-permute-done.5.refs_1_
  43.6 0.6 %collective-permute-done.6.refs_2_ = bf16[128,128]{1,0:T(8,128)(2,1)S(1)} collective-permute-done((bf16[128,128]{1,0:T(8,128)(2,1)S(1)}, bf16[128,128]{1,0:T(8,128)(2,1)S(1)}, u32[]{:S(2)}, u32[]{:S(2)}) %collective-permute-start.6) | collective-permute-done | bytes 32800 | tf_op jit(solution)/shard_map/ppermute | solution.py:449
  44.2 1.2 %collective-permute-done.7.refs_3_ = bf16[128,128]{1,0:T(8,128)(2,1)S(1)} collective-permute-done((bf16[128,128]{1,0:T(8,128)(2,1)S(1)}, bf16[128,128]{1,0:T(8,128)(2,1)S(1)}, u32[]{:S(2)}, u32[]{:S(2)}) %collective-permute-start.7) | collective-permute-done | bytes 32800 | tf_op jit(solution)/shard_map/ppermute | solution.py:449
  45.4 0.7 %join.1 = bf16[512,128]{1,0:T(8,128)(2,1)} custom-call(bf16[128,128]{1,0:T(8,128)(2,1)S(1)} %merge.3.refs_0_, bf16[128,128]{1,0:T(8,128)(2,1)S(1)} %collective-permute-done.5.refs_1_, bf16[128,128]{1,0:T(8,128)(2,1)S(1)} %collective-permute-done.6.refs_2_, bf16[128,128]{1,0:T(8,128)(2,1)S(1)} %collective-permute-done.7.refs_3_), custom_call_target="tpu_custom_call" | custom-call | tf_op jit(solution)/shard_map/join/pallas_call | solution.py:358
  46.1 0.0 all-to-all-done
  46.1 1.8 %relay.1 = (bf16[32,32,128]{2,1,0:T(8,128)(2,1)}, bf16[32,32,128]{2,1,0:T(8,128)(2,1)}) custom-call(s32[32]{0:T(128)} %slots_hbm.3, s32[1]{0:T(128)S(6)} %copy.11.length_ref, bf16[16,2,2,32,128]{4,3,2,1,0:T(8,128)(2,1)S(1)} %bitcast.11), custom_call_target="tpu_custom_call" | custom-call | tf_op jit(solution)/shard_map/relay/pallas_call | solution.py:391
Async XLA Ops:
  2.5 43.6 %all-to-all-start = ((bf16[16,2,64,128]{3,2,1,0:T(8,128)(2,1)}), bf16[16,2,64,128]{3,2,1,0:T(8,128)(2,1)S(1)}, u32[]{:S(2)}, u32[]{:S(2)}) async-start(bf16[16,2,64,128]{3,2,1,0:T(8,128)(2,1)} %bitcast.2), calls=%async_computation | async-start | bytes 1048576 | tf_op jit(solution)/shard_map/all_to_all | solution.py:437
  10.9 12.8 %collective-permute-start = (bf16[2,512,128]{2,1,0:T(8,128)(2,1)S(1)}, bf16[2,512,128]{2,1,0:T(8,128)(2,1)S(1)}, u32[]{:S(2)}, u32[]{:S(2)}) collective-permute-start(bf16[2,512,128]{2,1,0:T(8,128)(2,1)S(1)} %bitcast.13), channel_id=1, source_target_pairs={{0,16},{16,0},{1,17},{17,1},{2,18},{18,2},{3,19},{19,3},{4,20},{20... | collective-permute-start | bytes 786440 | tf_op jit(solution)/shard_map/ppermute | solution.py:431
  24.9 4.0 %collective-permute-start.1 = (bf16[144,128]{1,0:T(8,128)(2,1)S(1)}, bf16[144,128]{1,0:T(8,128)(2,1)S(1)}, u32[]{:S(2)}, u32[]{:S(2)}) collective-permute-start(bf16[144,128]{1,0:T(8,128)(2,1)S(1)} %get-tuple-element.22), channel_id=1, source_target_pairs={{0,2},{2,0},{4,6},{6,4},{8,10},{10,8},{12,14},{14,12},{1,3},{3,1},... | collective-permute-start | bytes 110600 | tf_op jit(solution)/shard_map/ppermute | solution.py:449
  26.4 4.0 %collective-permute-start.2 = (bf16[144,128]{1,0:T(8,128)(2,1)S(1)}, bf16[144,128]{1,0:T(8,128)(2,1)S(1)}, u32[]{:S(2)}, u32[]{:S(2)}) collective-permute-start(bf16[144,128]{1,0:T(8,128)(2,1)S(1)} %get-tuple-element.23), channel_id=1, source_target_pairs={{0,4},{2,6},{4,0},{6,2},{8,12},{10,14},{12,8},{14,10},{1,5},{3,7},... | collective-permute-start | bytes 110600 | tf_op jit(solution)/shard_map/ppermute | solution.py:449
  28.2 4.9 %collective-permute-start.3 = (bf16[144,128]{1,0:T(8,128)(2,1)S(1)}, bf16[144,128]{1,0:T(8,128)(2,1)S(1)}, u32[]{:S(2)}, u32[]{:S(2)}) collective-permute-start(bf16[144,128]{1,0:T(8,128)(2,1)S(1)} %get-tuple-element.24), channel_id=1, source_target_pairs={{0,6},{2,4},{4,2},{6,0},{8,14},{10,12},{12,10},{14,8},{1,7},{3,5},... | collective-permute-start | bytes 110600 | tf_op jit(solution)/shard_map/ppermute | solution.py:449
  33.4 5.8 %collective-permute-start.4 = (f32[136,128]{1,0:T(8,128)S(1)}, f32[136,128]{1,0:T(8,128)S(1)}, u32[]{:S(2)}, u32[]{:S(2)}) collective-permute-start(f32[136,128]{1,0:T(8,128)S(1)} %merge.2.refs_0_), channel_id=1, source_target_pairs={{0,8},{2,10},{4,12},{6,14},{8,0},{10,2},{12,4},{14,6},{1,9},{3,11}... | collective-permute-start | bytes 208904 | tf_op jit(solution)/shard_map/ppermute | solution.py:449
  39.6 4.0 %collective-permute-start.5 = (bf16[128,128]{1,0:T(8,128)(2,1)S(1)}, bf16[128,128]{1,0:T(8,128)(2,1)S(1)}, u32[]{:S(2)}, u32[]{:S(2)}) collective-permute-start(bf16[128,128]{1,0:T(8,128)(2,1)S(1)} %merge.3.refs_0_), channel_id=1, source_target_pairs={{0,2},{2,0},{4,6},{6,4},{8,10},{10,8},{12,14},{14,12},{1,3},{3,1},... | collective-permute-start | bytes 98312 | tf_op jit(solution)/shard_map/ppermute | solution.py:449
  40.3 3.9 %collective-permute-start.6 = (bf16[128,128]{1,0:T(8,128)(2,1)S(1)}, bf16[128,128]{1,0:T(8,128)(2,1)S(1)}, u32[]{:S(2)}, u32[]{:S(2)}) collective-permute-start(bf16[128,128]{1,0:T(8,128)(2,1)S(1)} %merge.3.refs_0_), channel_id=1, source_target_pairs={{0,4},{2,6},{4,0},{6,2},{8,12},{10,14},{12,8},{14,10},{1,5},{3,7},... | collective-permute-start | bytes 98312 | tf_op jit(solution)/shard_map/ppermute | solution.py:449
  40.4 5.0 %collective-permute-start.7 = (bf16[128,128]{1,0:T(8,128)(2,1)S(1)}, bf16[128,128]{1,0:T(8,128)(2,1)S(1)}, u32[]{:S(2)}, u32[]{:S(2)}) collective-permute-start(bf16[128,128]{1,0:T(8,128)(2,1)S(1)} %merge.3.refs_0_), channel_id=1, source_target_pairs={{0,6},{2,4},{4,2},{6,0},{8,14},{10,12},{12,10},{14,8},{1,7},{3,5},... | collective-permute-start | bytes 98312 | tf_op jit(solution)/shard_map/ppermute | solution.py:449

commit v7 on v6

--- a/solution.py
+++ b/solution.py
@@ -12,7 +12,6 @@
 BF16 = jnp.bfloat16
 F32 = jnp.float32
 DEAD = -1e30
-NOWHERE = 1 << 30
 STAT_ROWS = 16
 WIDE_ROWS = 8
 LANES = 128
@@ -52,6 +51,14 @@
     if n & (n - 1) == 0:
         return x & (n - 1), x >> (n.bit_length() - 1)
     return lax.rem(x, n), lax.div(x, n)
+
+
+def place_of(index, ways):
+    return lax.rem(lax.bitwise_xor(index, lax.div(lax.rem(index, 2 * ways), ways) * (ways // 2)), ways)
+
+
+def hop_distance(distance, ways):
+    return distance + ways // 2 if distance == ways else distance
 
 
 def pack_kernel(
@@ -70,7 +77,7 @@
     out_sems,
     sems,
 ):
-    seq_count, _, head_count, kv_count, _ = keys_ref.shape
+    seq_count, _, head_count, _, _ = keys_ref.shape
     slot_count = slots_hbm.shape[0]
     me = lax.axis_index("head")
     seq_index = lax.axis_index("seq")
@@ -103,16 +110,13 @@
 
     places = lax.fori_loop(0, slot_count, look, tuple(jnp.int32(0) for _ in wanted))
     column = lax.broadcasted_iota(jnp.int32, (1, place_ref.shape[1]), 1)
-    kv, rest = split_off(column, kv_count)
-    row, rest = split_off(rest, span_rows)
+    row, rest = split_off(column, span_rows)
     half, rest = split_off(rest, 2)
     turn, block = split_off(rest, seq_count)
     span = jnp.zeros_like(column)
     for at, place in enumerate(places):
         span = jnp.where(2 * block + half == at, place, span)
-    position = (turn * slot_count + span) * span_rows + row
-    for g in range(kv_count):
-        place_ref[g : g + 1, :] = jnp.where(kv == g, position, NOWHERE)
+    place_ref[...] = (turn * slot_count + span) * span_rows + row
     for _, out in blocks:
         out.wait()
     staged.wait()
@@ -134,7 +138,7 @@
             jax.ShapeDtypeStruct((head_count, seq_count, 2, rows, kv, head_dim), BF16),
             jax.ShapeDtypeStruct((2,) + block, BF16),
             jax.ShapeDtypeStruct((head_count - 1, 2) + block, BF16),
-            jax.ShapeDtypeStruct((kv, head_count * row_count * kv), jnp.int32),
+            jax.ShapeDtypeStruct((1, head_count * row_count), jnp.int32),
             jax.ShapeDtypeStruct(queries.shape, BF16),
         ),
         in_specs=[HBM] * len(inputs),
@@ -167,20 +171,26 @@
 
 
 def attend_kernel(score_scale, ways, length_ref, query_ref, place_ref, *rest):
-    *block_refs, rows_buf, stat_buf = rest
+    *block_refs, rows_buf, stat_buf, wide_buf = rest
     block_refs, out_refs = block_refs[:-ways], block_refs[-ways:]
     tokens, heads, head_dim = query_ref.shape
-    kv_count = place_ref.shape[0]
+    kv_count = rows_buf.shape[1]
     group = heads // kv_count
-    keys = jnp.concatenate([ref[0] for ref in block_refs], axis=0)
-    values = jnp.concatenate([ref[1] for ref in block_refs], axis=0)
+    stored = block_refs[0].shape[1]
+    for at, ref in enumerate(block_refs):
+        for c in range(2):
+            wide_buf[c, at * stored : (at + 1) * stored, :] = ref[c].astype(F32)
+    columns = place_ref.shape[1]
+    bias = jnp.where(place_ref[...] < length_ref[0], 0.0, DEAD)
     for g in range(kv_count):
         query = query_ref[:, g * group : (g + 1) * group, :].reshape(tokens * group, head_dim)
-        bias = jnp.where(place_ref[g : g + 1, :] < length_ref[0], 0.0, DEAD)
+        own = pl.ds(g, columns, stride=kv_count)
+        keys = wide_buf[0, own, :].astype(BF16)
+        values = wide_buf[1, own, :].astype(BF16)
         peak, total, weighted = softmax_parts(dot_rows(query, keys) * score_scale + bias, values)
         rows_buf[:, g] = weighted.astype(BF16).reshape(tokens, group, head_dim)
         stat_buf[:, g] = stat_lanes(peak, total, head_dim).reshape(tokens, group, head_dim)
-    here = lax.rem(lax.axis_index("seq"), ways)
+    here = place_of(lax.axis_index("seq"), ways)
     share = tokens // ways
     per = share * heads
     pick = eye(STAT_ROWS, head_dim)
@@ -195,7 +205,8 @@
 
 def attend(length, query, place, blocks, score_scale, ways):
     tokens, heads, head_dim = query.shape
-    kv_count = place.shape[0]
+    rows = sum(block.shape[1] for block in blocks)
+    kv_count = rows // place.shape[1]
     group = heads // kv_count
     per = tokens * heads // ways
     piece = jax.ShapeDtypeStruct((per + per // LANES * STAT_ROWS, head_dim), BF16)
@@ -207,6 +218,7 @@
         scratch_shapes=[
             pltpu.VMEM((tokens, kv_count, group, head_dim), BF16),
             pltpu.VMEM((tokens, kv_count, group, head_dim), BF16),
+            pltpu.VMEM((2, rows, head_dim), F32),
         ],
         compiler_params=PARAMS,
         name="attend",
@@ -228,7 +240,7 @@
     kv_count = keys_ref.shape[0] // tokens
     share = tokens // ways
     per = share * heads
-    first = lax.rem(lax.axis_index("seq"), ways) * share
+    first = place_of(lax.axis_index("seq"), ways) * share
     shape = (per, tokens * kv_count)
     _, own = split_off(lax.broadcasted_iota(jnp.int32, shape, 0), heads // kv_count)
     own_kv, own_token = split_off(own, kv_count)
@@ -310,9 +322,10 @@
         if last:
             factors = [f / total for f in factors]
         else:
-            start = per + at * WIDE_ROWS
-            row = lax.broadcasted_iota(jnp.int32, (WIDE_ROWS, LANES), 0)
-            out_ref[start : start + WIDE_ROWS, :] = jnp.where(row == 0, peak, total)
+            start = per + at * STAT_ROWS
+            out_ref[start : start + STAT_ROWS, :] = stacked(
+                three_parts(peak) + three_parts(total), (STAT_ROWS, LANES)
+            )
         parts = [part for f in factors for part in three_parts(f)]
         columns = dot_rows(turn, stacked(parts, (factor_rows, LANES)))
         terms = []
@@ -328,7 +341,7 @@
     if last:
         out = jax.ShapeDtypeStruct((per, head_dim), BF16)
     else:
-        out = jax.ShapeDtypeStruct((per + per // LANES * WIDE_ROWS, head_dim), F32)
+        out = jax.ShapeDtypeStruct((per + per // LANES * STAT_ROWS, head_dim), BF16)
     return pl.pallas_call(
         functools.partial(merge_kernel, per, last),
         out_shape=out,
@@ -343,7 +356,7 @@
     *in_refs, out_ref, sems = refs
     ways = len(in_refs)
     per = in_refs[0].shape[0]
-    here = lax.rem(lax.axis_index("seq"), ways)
+    here = place_of(lax.axis_index("seq"), ways)
     copies = []
     for way, ref in enumerate(in_refs):
         start = pl.multiple_of(lax.bitwise_xor(here, way) * per, per)
@@ -448,15 +461,19 @@
     def swapped(x, distance):
         return lax.ppermute(x, "seq", [(s, s ^ distance) for s in range(seq_count)])
 
-    states = [pieces[0]] + [swapped(pieces[way], way) for way in range(1, ways)]
+    states = [pieces[0]]
+    for way in range(1, ways):
+        states.append(swapped(pieces[way], way))
     fresh = fresh_rows(query, new_keys, new_values, decode_offsets, score_scale, ways)
     distance = ways
     while distance < seq_count:
         state = merge(states, per, False)
-        states = [state, swapped(state, distance)]
+        states = [state, swapped(state, hop_distance(distance, ways))]
         distance *= 2
     state = merge(states + [fresh], per, True)
-    finished = [state] + [swapped(state, way) for way in range(1, ways)]
+    finished = [state]
+    for way in range(1, ways):
+        finished.append(swapped(state, way))
     attended = join(finished)
 
     relaid_keys, relaid_values = relay(

time: 48.2 us -> 47.9 us (level)
  no operation moved by 1% of the time
where the time goes in v7:
time: 47.9 us; the launch traced here: 47.6 us
  starting transfers between devices  20.2 us (42%)
  waiting for transfers between devices  18.9 us (39%)
  Pallas kernels  7.28 us (15%)
  between operations  1.34 us (3%)
    ppermute x1, waiting for transfers between devices, step(): lax.ppermute(away[shift - 1].reshape(flat), 'head', [(h, (h + shift) % he...  10.2 us
    ppermute x7, starting transfers between devices, swapped(): return lax.ppermute(x, 'seq', [(s, s ^ distance) for s in range(seq_count)])  9.89 us
    ppermute x7, waiting for transfers between devices, swapped(): return lax.ppermute(x, 'seq', [(s, s ^ distance) for s in range(seq_count)])  8.65 us
    all_to_all x1, starting transfers between devices, step(): lax.all_to_all(packed.reshape(cycle_size, 2, 2 * span_rows * kv_local, he...  8.34 us
    ppermute x1, starting transfers between devices, step(): lax.ppermute(away[shift - 1].reshape(flat), 'head', [(h, (h + shift) % he...  1.93 us
    pallas_call x1, Pallas kernels, pack(): pl.pallas_call(functools.partial(pack_kernel, rows // 2), out_shape=(jax....  1.87 us
    pallas_call x1, Pallas kernels, relay(): pl.pallas_call(functools.partial(relay_kernel, kv_count), out_shape=(shap...  1.76 us
    pallas_call x1, Pallas kernels, fresh_rows(): pl.pallas_call(functools.partial(fresh_kernel, score_scale, ways), out_sh...  1.27 us
  transfers between devices with their start and end apart: 9, of which 8 were waited for; matrix products, arithmetic and copies ran while one was open for 0% of the time, Pallas kernels for 8%

profile of v7, /device:TPU:0, one launch (start us, length us, event | category | flops | bytes accessed | tf_op | source)
XLA Modules:
  0.0 47.6 jit_solution(4155856527469204245)
XLA Ops:
  0.6 1.9 %pack.1 = (bf16[2,8,2,32,2,128]{5,4,3,2,1,0:T(2,128)(2,1)}, bf16[2,8,32,2,128]{4,3,2,1,0:T(2,128)(2,1)S(1)}, bf16[1,2,8,32,2,128]{5,4,3,2,1,0:T(2,128)(2,1)S(1)}...) custom-call(bf16[8,32,2,2,128]{4,3,2,1,0:T(2,128)(2,1)} %bitcast.14, bf16[8,32,2,2,128]{4,3,2,1,0:T(2,128)(2,1)} %bitcast.15, ...), custom_call_target="tpu_custom_call" | custom-call | tf_op jit(solution)/shard_map/pack/pallas_call | solution.py:135
  2.5 8.3 %all-to-all-start = ((bf16[16,2,64,128]{3,2,1,0:T(8,128)(2,1)}), bf16[16,2,64,128]{3,2,1,0:T(8,128)(2,1)S(1)}, u32[]{:S(2)}, u32[]{:S(2)}) async-start(bf16[16,2,64,128]{3,2,1,0:T(8,128)(2,1)} %bitcast.2), calls=%async_computation | async-start | bytes 1048576 | tf_op jit(solution)/shard_map/all_to_all | solution.py:450
  10.9 1.9 %collective-permute-start = (bf16[2,512,128]{2,1,0:T(8,128)(2,1)S(1)}, bf16[2,512,128]{2,1,0:T(8,128)(2,1)S(1)}, u32[]{:S(2)}, u32[]{:S(2)}) collective-permute-start(bf16[2,512,128]{2,1,0:T(8,128)(2,1)S(1)} %bitcast.13), channel_id=1, source_target_pairs={{0,16},{16,0},{1,17},{17,1},{2,18},{18,2},{3,19},{19,3},{4,20},{20... | collective-permute-start | bytes 786440 | tf_op jit(solution)/shard_map/ppermute | solution.py:444
  13.4 10.2 %collective-permute-done.rest_1_ = bf16[2,512,128]{2,1,0:T(8,128)(2,1)S(1)} collective-permute-done((bf16[2,512,128]{2,1,0:T(8,128)(2,1)S(1)}, bf16[2,512,128]{2,1,0:T(8,128)(2,1)S(1)}, u32[]{:S(2)}, u32[]{:S(2)}) %collective-permute-start) | collective-permute-done | bytes 262176 | tf_op jit(solution)/shard_map/ppermute | solution.py:444
  23.6 1.0 %attend.1 = (bf16[144,128]{1,0:T(8,128)(2,1)S(1)}, bf16[144,128]{1,0:T(8,128)(2,1)S(1)}, bf16[144,128]{1,0:T(8,128)(2,1)S(1)}, bf16[144,128]{1,0:T(8,128)(2,1)S(1)}) custom-call(s32[1]{0:T(128)S(6)} %copy.11.length_ref, bf16[16,32,128]{2,1,0:T(8,128)(2,1)S(1)} %get-tuple-element.17.query_ref, s32[1,512]{1,0:T(1,128)S(1)} %get-tuple-element.18.place_ref, ...), custom_call_target="tpu_custom_call" | custom-call | tf_op jit(solution)/shard_map/attend/pallas_call | solution.py:213
  24.6 1.5 %collective-permute-start.1 = (bf16[144,128]{1,0:T(8,128)(2,1)S(1)}, bf16[144,128]{1,0:T(8,128)(2,1)S(1)}, u32[]{:S(2)}, u32[]{:S(2)}) collective-permute-start(bf16[144,128]{1,0:T(8,128)(2,1)S(1)} %get-tuple-element.22), channel_id=1, source_target_pairs={{0,2},{2,0},{4,6},{6,4},{8,10},{10,8},{12,14},{14,12},{1,3},{3,1},... | collective-permute-start | bytes 110600 | tf_op jit(solution)/shard_map/ppermute | solution.py:462
  26.1 1.8 %collective-permute-start.2 = (bf16[144,128]{1,0:T(8,128)(2,1)S(1)}, bf16[144,128]{1,0:T(8,128)(2,1)S(1)}, u32[]{:S(2)}, u32[]{:S(2)}) collective-permute-start(bf16[144,128]{1,0:T(8,128)(2,1)S(1)} %get-tuple-element.23), channel_id=1, source_target_pairs={{0,4},{2,6},{4,0},{6,2},{8,12},{10,14},{12,8},{14,10},{1,5},{3,7},... | collective-permute-start | bytes 110600 | tf_op jit(solution)/shard_map/ppermute | solution.py:462
  28.0 0.2 collective-permute-start.3
  28.2 0.5 collective-permute-done.1.refs_1_
  28.6 1.5 %collective-permute-done.2.refs_2_ = bf16[144,128]{1,0:T(8,128)(2,1)S(1)} collective-permute-done((bf16[144,128]{1,0:T(8,128)(2,1)S(1)}, bf16[144,128]{1,0:T(8,128)(2,1)S(1)}, u32[]{:S(2)}, u32[]{:S(2)}) %collective-permute-start.2) | collective-permute-done | bytes 36896 | tf_op jit(solution)/shard_map/ppermute | solution.py:462
  30.1 2.7 %collective-permute-done.3.refs_3_ = bf16[144,128]{1,0:T(8,128)(2,1)S(1)} collective-permute-done((bf16[144,128]{1,0:T(8,128)(2,1)S(1)}, bf16[144,128]{1,0:T(8,128)(2,1)S(1)}, u32[]{:S(2)}, u32[]{:S(2)}) %collective-permute-start.3) | collective-permute-done | bytes 36896 | tf_op jit(solution)/shard_map/ppermute | solution.py:462
  32.8 0.4 merge.2.refs_0_
  33.2 2.8 %collective-permute-start.4 = (bf16[144,128]{1,0:T(8,128)(2,1)S(1)}, bf16[144,128]{1,0:T(8,128)(2,1)S(1)}, u32[]{:S(2)}, u32[]{:S(2)}) collective-permute-start(bf16[144,128]{1,0:T(8,128)(2,1)S(1)} %merge.2.refs_0_), channel_id=1, source_target_pairs={{0,12},{2,14},{4,8},{6,10},{8,4},{10,6},{12,0},{14,2},{1,13},{3,15... | collective-permute-start | bytes 110600 | tf_op jit(solution)/shard_map/ppermute | solution.py:462
  36.0 1.3 %fresh.1.refs_2_ = f32[136,128]{1,0:T(8,128)S(1)} custom-call(bf16[16,32,128]{2,1,0:T(8,128)(2,1)S(1)} %get-tuple-element.17.query_ref, bf16[32,128]{1,0:T(8,128)(2,1)} %bitcast.17, bf16[32,128]{1,0:T(8,128)(2,1)} %bitcast.18, s32[16]{0:T(128)} %depth_hbm.1), custom_call_target="tpu_custom_call" | custom-call | tf_op jit(solution)/shard_map/fresh/pallas_call | solution.py:279
  37.3 1.8 %collective-permute-done.4.refs_1_ = bf16[144,128]{1,0:T(8,128)(2,1)S(1)} collective-permute-done((bf16[144,128]{1,0:T(8,128)(2,1)S(1)}, bf16[144,128]{1,0:T(8,128)(2,1)S(1)}, u32[]{:S(2)}, u32[]{:S(2)}) %collective-permute-start.4) | collective-permute-done | bytes 36896 | tf_op jit(solution)/shard_map/ppermute | solution.py:462
  39.0 0.4 merge.3.refs_0_
  39.4 0.6 %collective-permute-start.5 = (bf16[128,128]{1,0:T(8,128)(2,1)S(1)}, bf16[128,128]{1,0:T(8,128)(2,1)S(1)}, u32[]{:S(2)}, u32[]{:S(2)}) collective-permute-start(bf16[128,128]{1,0:T(8,128)(2,1)S(1)} %merge.3.refs_0_), channel_id=1, source_target_pairs={{0,2},{2,0},{4,6},{6,4},{8,10},{10,8},{12,14},{14,12},{1,3},{3,1},... | collective-permute-start | bytes 98312 | tf_op jit(solution)/shard_map/ppermute | solution.py:462
  40.0 0.0 collective-permute-start.6
  40.0 2.9 %collective-permute-start.7 = (bf16[128,128]{1,0:T(8,128)(2,1)S(1)}, bf16[128,128]{1,0:T(8,128)(2,1)S(1)}, u32[]{:S(2)}, u32[]{:S(2)}) collective-permute-start(bf16[128,128]{1,0:T(8,128)(2,1)S(1)} %merge.3.refs_0_), channel_id=1, source_target_pairs={{0,6},{2,4},{4,2},{6,0},{8,14},{10,12},{12,10},{14,8},{1,7},{3,5},... | collective-permute-start | bytes 98312 | tf_op jit(solution)/shard_map/ppermute | solution.py:462
  42.9 0.4 collective-permute-done.5.refs_1_
  43.4 0.5 %collective-permute-done.6.refs_2_ = bf16[128,128]{1,0:T(8,128)(2,1)S(1)} collective-permute-done((bf16[128,128]{1,0:T(8,128)(2,1)S(1)}, bf16[128,128]{1,0:T(8,128)(2,1)S(1)}, u32[]{:S(2)}, u32[]{:S(2)}) %collective-permute-start.6) | collective-permute-done | bytes 32800 | tf_op jit(solution)/shard_map/ppermute | solution.py:462
  43.9 1.3 %collective-permute-done.7.refs_3_ = bf16[128,128]{1,0:T(8,128)(2,1)S(1)} collective-permute-done((bf16[128,128]{1,0:T(8,128)(2,1)S(1)}, bf16[128,128]{1,0:T(8,128)(2,1)S(1)}, u32[]{:S(2)}, u32[]{:S(2)}) %collective-permute-start.7) | collective-permute-done | bytes 32800 | tf_op jit(solution)/shard_map/ppermute | solution.py:462
  45.2 0.7 %join.1 = bf16[512,128]{1,0:T(8,128)(2,1)} custom-call(bf16[128,128]{1,0:T(8,128)(2,1)S(1)} %merge.3.refs_0_, bf16[128,128]{1,0:T(8,128)(2,1)S(1)} %collective-permute-done.5.refs_1_, bf16[128,128]{1,0:T(8,128)(2,1)S(1)} %collective-permute-done.6.refs_2_, bf16[128,128]{1,0:T(8,128)(2,1)S(1)} %collective-permute-done.7.refs_3_), custom_call_target="tpu_custom_call" | custom-call | tf_op jit(solution)/shard_map/join/pallas_call | solution.py:371
  45.9 0.0 all-to-all-done
  45.9 1.8 %relay.1 = (bf16[32,32,128]{2,1,0:T(8,128)(2,1)}, bf16[32,32,128]{2,1,0:T(8,128)(2,1)}) custom-call(s32[32]{0:T(128)} %slots_hbm.3, s32[1]{0:T(128)S(6)} %copy.11.length_ref, bf16[16,2,2,32,128]{4,3,2,1,0:T(8,128)(2,1)S(1)} %bitcast.11), custom_call_target="tpu_custom_call" | custom-call | tf_op jit(solution)/shard_map/relay/pallas_call | solution.py:404
Async XLA Ops:
  2.5 43.4 %all-to-all-start = ((bf16[16,2,64,128]{3,2,1,0:T(8,128)(2,1)}), bf16[16,2,64,128]{3,2,1,0:T(8,128)(2,1)S(1)}, u32[]{:S(2)}, u32[]{:S(2)}) async-start(bf16[16,2,64,128]{3,2,1,0:T(8,128)(2,1)} %bitcast.2), calls=%async_computation | async-start | bytes 1048576 | tf_op jit(solution)/shard_map/all_to_all | solution.py:450
  10.9 12.8 %collective-permute-start = (bf16[2,512,128]{2,1,0:T(8,128)(2,1)S(1)}, bf16[2,512,128]{2,1,0:T(8,128)(2,1)S(1)}, u32[]{:S(2)}, u32[]{:S(2)}) collective-permute-start(bf16[2,512,128]{2,1,0:T(8,128)(2,1)S(1)} %bitcast.13), channel_id=1, source_target_pairs={{0,16},{16,0},{1,17},{17,1},{2,18},{18,2},{3,19},{19,3},{4,20},{20... | collective-permute-start | bytes 786440 | tf_op jit(solution)/shard_map/ppermute | solution.py:444
  24.6 4.0 %collective-permute-start.1 = (bf16[144,128]{1,0:T(8,128)(2,1)S(1)}, bf16[144,128]{1,0:T(8,128)(2,1)S(1)}, u32[]{:S(2)}, u32[]{:S(2)}) collective-permute-start(bf16[144,128]{1,0:T(8,128)(2,1)S(1)} %get-tuple-element.22), channel_id=1, source_target_pairs={{0,2},{2,0},{4,6},{6,4},{8,10},{10,8},{12,14},{14,12},{1,3},{3,1},... | collective-permute-start | bytes 110600 | tf_op jit(solution)/shard_map/ppermute | solution.py:462
  26.1 4.0 %collective-permute-start.2 = (bf16[144,128]{1,0:T(8,128)(2,1)S(1)}, bf16[144,128]{1,0:T(8,128)(2,1)S(1)}, u32[]{:S(2)}, u32[]{:S(2)}) collective-permute-start(bf16[144,128]{1,0:T(8,128)(2,1)S(1)} %get-tuple-element.23), channel_id=1, source_target_pairs={{0,4},{2,6},{4,0},{6,2},{8,12},{10,14},{12,8},{14,10},{1,5},{3,7},... | collective-permute-start | bytes 110600 | tf_op jit(solution)/shard_map/ppermute | solution.py:462
  28.0 4.9 %collective-permute-start.3 = (bf16[144,128]{1,0:T(8,128)(2,1)S(1)}, bf16[144,128]{1,0:T(8,128)(2,1)S(1)}, u32[]{:S(2)}, u32[]{:S(2)}) collective-permute-start(bf16[144,128]{1,0:T(8,128)(2,1)S(1)} %get-tuple-element.24), channel_id=1, source_target_pairs={{0,6},{2,4},{4,2},{6,0},{8,14},{10,12},{12,10},{14,8},{1,7},{3,5},... | collective-permute-start | bytes 110600 | tf_op jit(solution)/shard_map/ppermute | solution.py:462
  33.2 5.8 %collective-permute-start.4 = (bf16[144,128]{1,0:T(8,128)(2,1)S(1)}, bf16[144,128]{1,0:T(8,128)(2,1)S(1)}, u32[]{:S(2)}, u32[]{:S(2)}) collective-permute-start(bf16[144,128]{1,0:T(8,128)(2,1)S(1)} %merge.2.refs_0_), channel_id=1, source_target_pairs={{0,12},{2,14},{4,8},{6,10},{8,4},{10,6},{12,0},{14,2},{1,13},{3,15... | collective-permute-start | bytes 110600 | tf_op jit(solution)/shard_map/ppermute | solution.py:462
  39.4 4.0 %collective-permute-start.5 = (bf16[128,128]{1,0:T(8,128)(2,1)S(1)}, bf16[128,128]{1,0:T(8,128)(2,1)S(1)}, u32[]{:S(2)}, u32[]{:S(2)}) collective-permute-start(bf16[128,128]{1,0:T(8,128)(2,1)S(1)} %merge.3.refs_0_), channel_id=1, source_target_pairs={{0,2},{2,0},{4,6},{6,4},{8,10},{10,8},{12,14},{14,12},{1,3},{3,1},... | collective-permute-start | bytes 98312 | tf_op jit(solution)/shard_map/ppermute | solution.py:462
  40.0 3.9 %collective-permute-start.6 = (bf16[128,128]{1,0:T(8,128)(2,1)S(1)}, bf16[128,128]{1,0:T(8,128)(2,1)S(1)}, u32[]{:S(2)}, u32[]{:S(2)}) collective-permute-start(bf16[128,128]{1,0:T(8,128)(2,1)S(1)} %merge.3.refs_0_), channel_id=1, source_target_pairs={{0,4},{2,6},{4,0},{6,2},{8,12},{10,14},{12,8},{14,10},{1,5},{3,7},... | collective-permute-start | bytes 98312 | tf_op jit(solution)/shard_map/ppermute | solution.py:462
  40.0 5.2 %collective-permute-start.7 = (bf16[128,128]{1,0:T(8,128)(2,1)S(1)}, bf16[128,128]{1,0:T(8,128)(2,1)S(1)}, u32[]{:S(2)}, u32[]{:S(2)}) collective-permute-start(bf16[128,128]{1,0:T(8,128)(2,1)S(1)} %merge.3.refs_0_), channel_id=1, source_target_pairs={{0,6},{2,4},{4,2},{6,0},{8,14},{10,12},{12,10},{14,8},{1,7},{3,5},... | collective-permute-start | bytes 98312 | tf_op jit(solution)/shard_map/ppermute | solution.py:462

commit v8 on v7

--- a/solution.py
+++ b/solution.py
@@ -12,7 +12,7 @@
 BF16 = jnp.bfloat16
 F32 = jnp.float32
 DEAD = -1e30
-STAT_ROWS = 16
+STAT_ROWS = 8
 WIDE_ROWS = 8
 LANES = 128
 VMEM = pl.BlockSpec(memory_space=pltpu.VMEM)
@@ -158,7 +158,10 @@
     peak = jnp.max(scores, axis=1, keepdims=True)
     weights = jnp.exp(scores - peak)
     total = jnp.sum(weights, axis=1, keepdims=True)
-    weighted = jnp.dot(weights.astype(BF16), values, preferred_element_type=F32)
+    high = weights.astype(BF16)
+    low = (weights - high.astype(F32)).astype(BF16)
+    weighted = jnp.dot(high, values, preferred_element_type=F32)
+    weighted = weighted + jnp.dot(low, values, preferred_element_type=F32)
     return peak, total, weighted
 
 
@@ -322,10 +325,9 @@
         if last:
             factors = [f / total for f in factors]
         else:
-            start = per + at * STAT_ROWS
-            out_ref[start : start + STAT_ROWS, :] = stacked(
-                three_parts(peak) + three_parts(total), (STAT_ROWS, LANES)
-            )
+            start = per + at * WIDE_ROWS
+            row = lax.broadcasted_iota(jnp.int32, (WIDE_ROWS, LANES), 0)
+            out_ref[start : start + WIDE_ROWS, :] = jnp.where(row == 0, peak, total)
         parts = [part for f in factors for part in three_parts(f)]
         columns = dot_rows(turn, stacked(parts, (factor_rows, LANES)))
         terms = []
@@ -341,7 +343,7 @@
     if last:
         out = jax.ShapeDtypeStruct((per, head_dim), BF16)
     else:
-        out = jax.ShapeDtypeStruct((per + per // LANES * STAT_ROWS, head_dim), BF16)
+        out = jax.ShapeDtypeStruct((per + per // LANES * WIDE_ROWS, head_dim), F32)
     return pl.pallas_call(
         functools.partial(merge_kernel, per, last),
         out_shape=out,

time: 47.9 us -> 48.4 us (1.010)
  no operation moved by 1% of the time
where the time goes in v8:
time: 48.4 us; the launch traced here: 48.1 us
  starting transfers between devices  20.1 us (42%)
  waiting for transfers between devices  19.2 us (40%)
  Pallas kernels  7.42 us (15%)
  between operations  1.34 us (3%)
    ppermute x1, waiting for transfers between devices, step(): lax.ppermute(away[shift - 1].reshape(flat), 'head', [(h, (h + shift) % he...  10.2 us
    ppermute x7, starting transfers between devices, swapped(): return lax.ppermute(x, 'seq', [(s, s ^ distance) for s in range(seq_count)])  9.84 us
    ppermute x7, waiting for transfers between devices, swapped(): return lax.ppermute(x, 'seq', [(s, s ^ distance) for s in range(seq_count)])  9.02 us
    all_to_all x1, starting transfers between devices, step(): lax.all_to_all(packed.reshape(cycle_size, 2, 2 * span_rows * kv_local, he...  8.34 us
    ppermute x1, starting transfers between devices, step(): lax.ppermute(away[shift - 1].reshape(flat), 'head', [(h, (h + shift) % he...  1.93 us
    pallas_call x1, Pallas kernels, pack(): pl.pallas_call(functools.partial(pack_kernel, rows // 2), out_shape=(jax....  1.87 us
    pallas_call x1, Pallas kernels, relay(): pl.pallas_call(functools.partial(relay_kernel, kv_count), out_shape=(shap...  1.76 us
    pallas_call x1, Pallas kernels, fresh_rows(): pl.pallas_call(functools.partial(fresh_kernel, score_scale, ways), out_sh...  1.27 us
  transfers between devices with their start and end apart: 9, of which 8 were waited for; matrix products, arithmetic and copies ran while one was open for 0% of the time, Pallas kernels for 8%

profile of v8, /device:TPU:0, one launch (start us, length us, event | category | flops | bytes accessed | tf_op | source)
XLA Modules:
  0.0 48.1 jit_solution(16371980372665651824)
XLA Ops:
  0.6 1.9 %pack.1 = (bf16[2,8,2,32,2,128]{5,4,3,2,1,0:T(2,128)(2,1)}, bf16[2,8,32,2,128]{4,3,2,1,0:T(2,128)(2,1)S(1)}, bf16[1,2,8,32,2,128]{5,4,3,2,1,0:T(2,128)(2,1)S(1)}...) custom-call(bf16[8,32,2,2,128]{4,3,2,1,0:T(2,128)(2,1)} %bitcast.14, bf16[8,32,2,2,128]{4,3,2,1,0:T(2,128)(2,1)} %bitcast.15, ...), custom_call_target="tpu_custom_call" | custom-call | tf_op jit(solution)/shard_map/pack/pallas_call | solution.py:135
  2.5 8.3 %all-to-all-start = ((bf16[16,2,64,128]{3,2,1,0:T(8,128)(2,1)}), bf16[16,2,64,128]{3,2,1,0:T(8,128)(2,1)S(1)}, u32[]{:S(2)}, u32[]{:S(2)}) async-start(bf16[16,2,64,128]{3,2,1,0:T(8,128)(2,1)} %bitcast.2), calls=%async_computation | async-start | bytes 1048576 | tf_op jit(solution)/shard_map/all_to_all | solution.py:452
  10.9 1.9 %collective-permute-start = (bf16[2,512,128]{2,1,0:T(8,128)(2,1)S(1)}, bf16[2,512,128]{2,1,0:T(8,128)(2,1)S(1)}, u32[]{:S(2)}, u32[]{:S(2)}) collective-permute-start(bf16[2,512,128]{2,1,0:T(8,128)(2,1)S(1)} %bitcast.13), channel_id=1, source_target_pairs={{0,16},{16,0},{1,17},{17,1},{2,18},{18,2},{3,19},{19,3},{4,20},{20... | collective-permute-start | bytes 786440 | tf_op jit(solution)/shard_map/ppermute | solution.py:446
  13.4 10.2 %collective-permute-done.rest_1_ = bf16[2,512,128]{2,1,0:T(8,128)(2,1)S(1)} collective-permute-done((bf16[2,512,128]{2,1,0:T(8,128)(2,1)S(1)}, bf16[2,512,128]{2,1,0:T(8,128)(2,1)S(1)}, u32[]{:S(2)}, u32[]{:S(2)}) %collective-permute-start) | collective-permute-done | bytes 262176 | tf_op jit(solution)/shard_map/ppermute | solution.py:446
  23.6 1.1 %attend.1 = (bf16[136,128]{1,0:T(8,128)(2,1)S(1)}, bf16[136,128]{1,0:T(8,128)(2,1)S(1)}, bf16[136,128]{1,0:T(8,128)(2,1)S(1)}, bf16[136,128]{1,0:T(8,128)(2,1)S(1)}) custom-call(s32[1]{0:T(128)S(6)} %copy.11.length_ref, bf16[16,32,128]{2,1,0:T(8,128)(2,1)S(1)} %get-tuple-element.17.query_ref, s32[1,512]{1,0:T(1,128)S(1)} %get-tuple-element.18.place_ref, ...), custom_call_target="tpu_custom_call" | custom-call | tf_op jit(solution)/shard_map/attend/pallas_call | solution.py:216
  24.8 1.5 %collective-permute-start.1 = (bf16[136,128]{1,0:T(8,128)(2,1)S(1)}, bf16[136,128]{1,0:T(8,128)(2,1)S(1)}, u32[]{:S(2)}, u32[]{:S(2)}) collective-permute-start(bf16[136,128]{1,0:T(8,128)(2,1)S(1)} %get-tuple-element.22), channel_id=1, source_target_pairs={{0,2},{2,0},{4,6},{6,4},{8,10},{10,8},{12,14},{14,12},{1,3},{3,1},... | collective-permute-start | bytes 104456 | tf_op jit(solution)/shard_map/ppermute | solution.py:464
  26.3 1.8 %collective-permute-start.2 = (bf16[136,128]{1,0:T(8,128)(2,1)S(1)}, bf16[136,128]{1,0:T(8,128)(2,1)S(1)}, u32[]{:S(2)}, u32[]{:S(2)}) collective-permute-start(bf16[136,128]{1,0:T(8,128)(2,1)S(1)} %get-tuple-element.23), channel_id=1, source_target_pairs={{0,4},{2,6},{4,0},{6,2},{8,12},{10,14},{12,8},{14,10},{1,5},{3,7},... | collective-permute-start | bytes 104456 | tf_op jit(solution)/shard_map/ppermute | solution.py:464
  28.1 0.2 collective-permute-start.3
  28.3 0.4 collective-permute-done.1.refs_1_
  28.7 1.5 %collective-permute-done.2.refs_2_ = bf16[136,128]{1,0:T(8,128)(2,1)S(1)} collective-permute-done((bf16[136,128]{1,0:T(8,128)(2,1)S(1)}, bf16[136,128]{1,0:T(8,128)(2,1)S(1)}, u32[]{:S(2)}, u32[]{:S(2)}) %collective-permute-start.2) | collective-permute-done | bytes 34848 | tf_op jit(solution)/shard_map/ppermute | solution.py:464
  30.2 2.7 %collective-permute-done.3.refs_3_ = bf16[136,128]{1,0:T(8,128)(2,1)S(1)} collective-permute-done((bf16[136,128]{1,0:T(8,128)(2,1)S(1)}, bf16[136,128]{1,0:T(8,128)(2,1)S(1)}, u32[]{:S(2)}, u32[]{:S(2)}) %collective-permute-start.3) | collective-permute-done | bytes 34848 | tf_op jit(solution)/shard_map/ppermute | solution.py:464
  32.9 0.4 merge.2.refs_0_
  33.3 2.8 %collective-permute-start.4 = (f32[136,128]{1,0:T(8,128)S(1)}, f32[136,128]{1,0:T(8,128)S(1)}, u32[]{:S(2)}, u32[]{:S(2)}) collective-permute-start(f32[136,128]{1,0:T(8,128)S(1)} %merge.2.refs_0_), channel_id=1, source_target_pairs={{0,12},{2,14},{4,8},{6,10},{8,4},{10,6},{12,0},{14,2},{1,13},{3,15... | collective-permute-start | bytes 208904 | tf_op jit(solution)/shard_map/ppermute | solution.py:464
  36.1 1.3 %fresh.1.refs_2_ = f32[136,128]{1,0:T(8,128)S(1)} custom-call(bf16[16,32,128]{2,1,0:T(8,128)(2,1)S(1)} %get-tuple-element.17.query_ref, bf16[32,128]{1,0:T(8,128)(2,1)} %bitcast.17, bf16[32,128]{1,0:T(8,128)(2,1)} %bitcast.18, s32[16]{0:T(128)} %depth_hbm.1), custom_call_target="tpu_custom_call" | custom-call | tf_op jit(solution)/shard_map/fresh/pallas_call | solution.py:282
  37.3 2.1 %collective-permute-done.4.refs_1_ = f32[136,128]{1,0:T(8,128)S(1)} collective-permute-done((f32[136,128]{1,0:T(8,128)S(1)}, f32[136,128]{1,0:T(8,128)S(1)}, u32[]{:S(2)}, u32[]{:S(2)}) %collective-permute-start.4) | collective-permute-done | bytes 69664 | tf_op jit(solution)/shard_map/ppermute | solution.py:464
  39.5 0.3 merge.3.refs_0_
  39.8 0.6 %collective-permute-start.5 = (bf16[128,128]{1,0:T(8,128)(2,1)S(1)}, bf16[128,128]{1,0:T(8,128)(2,1)S(1)}, u32[]{:S(2)}, u32[]{:S(2)}) collective-permute-start(bf16[128,128]{1,0:T(8,128)(2,1)S(1)} %merge.3.refs_0_), channel_id=1, source_target_pairs={{0,2},{2,0},{4,6},{6,4},{8,10},{10,8},{12,14},{14,12},{1,3},{3,1},... | collective-permute-start | bytes 98312 | tf_op jit(solution)/shard_map/ppermute | solution.py:464
  40.4 0.0 collective-permute-start.6
  40.4 3.0 %collective-permute-start.7 = (bf16[128,128]{1,0:T(8,128)(2,1)S(1)}, bf16[128,128]{1,0:T(8,128)(2,1)S(1)}, u32[]{:S(2)}, u32[]{:S(2)}) collective-permute-start(bf16[128,128]{1,0:T(8,128)(2,1)S(1)} %merge.3.refs_0_), channel_id=1, source_target_pairs={{0,6},{2,4},{4,2},{6,0},{8,14},{10,12},{12,10},{14,8},{1,7},{3,5},... | collective-permute-start | bytes 98312 | tf_op jit(solution)/shard_map/ppermute | solution.py:464
  43.4 0.4 collective-permute-done.5.refs_1_
  43.8 0.5 %collective-permute-done.6.refs_2_ = bf16[128,128]{1,0:T(8,128)(2,1)S(1)} collective-permute-done((bf16[128,128]{1,0:T(8,128)(2,1)S(1)}, bf16[128,128]{1,0:T(8,128)(2,1)S(1)}, u32[]{:S(2)}, u32[]{:S(2)}) %collective-permute-start.6) | collective-permute-done | bytes 32800 | tf_op jit(solution)/shard_map/ppermute | solution.py:464
  44.3 1.3 %collective-permute-done.7.refs_3_ = bf16[128,128]{1,0:T(8,128)(2,1)S(1)} collective-permute-done((bf16[128,128]{1,0:T(8,128)(2,1)S(1)}, bf16[128,128]{1,0:T(8,128)(2,1)S(1)}, u32[]{:S(2)}, u32[]{:S(2)}) %collective-permute-start.7) | collective-permute-done | bytes 32800 | tf_op jit(solution)/shard_map/ppermute | solution.py:464
  45.6 0.7 %join.1 = bf16[512,128]{1,0:T(8,128)(2,1)} custom-call(bf16[128,128]{1,0:T(8,128)(2,1)S(1)} %merge.3.refs_0_, bf16[128,128]{1,0:T(8,128)(2,1)S(1)} %collective-permute-done.5.refs_1_, bf16[128,128]{1,0:T(8,128)(2,1)S(1)} %collective-permute-done.6.refs_2_, bf16[128,128]{1,0:T(8,128)(2,1)S(1)} %collective-permute-done.7.refs_3_), custom_call_target="tpu_custom_call" | custom-call | tf_op jit(solution)/shard_map/join/pallas_call | solution.py:373
  46.3 0.0 all-to-all-done
  46.3 1.8 %relay.1 = (bf16[32,32,128]{2,1,0:T(8,128)(2,1)}, bf16[32,32,128]{2,1,0:T(8,128)(2,1)}) custom-call(s32[32]{0:T(128)} %slots_hbm.3, s32[1]{0:T(128)S(6)} %copy.11.length_ref, bf16[16,2,2,32,128]{4,3,2,1,0:T(8,128)(2,1)S(1)} %bitcast.11), custom_call_target="tpu_custom_call" | custom-call | tf_op jit(solution)/shard_map/relay/pallas_call | solution.py:406
Async XLA Ops:
  2.5 43.8 %all-to-all-start = ((bf16[16,2,64,128]{3,2,1,0:T(8,128)(2,1)}), bf16[16,2,64,128]{3,2,1,0:T(8,128)(2,1)S(1)}, u32[]{:S(2)}, u32[]{:S(2)}) async-start(bf16[16,2,64,128]{3,2,1,0:T(8,128)(2,1)} %bitcast.2), calls=%async_computation | async-start | bytes 1048576 | tf_op jit(solution)/shard_map/all_to_all | solution.py:452
  10.9 12.8 %collective-permute-start = (bf16[2,512,128]{2,1,0:T(8,128)(2,1)S(1)}, bf16[2,512,128]{2,1,0:T(8,128)(2,1)S(1)}, u32[]{:S(2)}, u32[]{:S(2)}) collective-permute-start(bf16[2,512,128]{2,1,0:T(8,128)(2,1)S(1)} %bitcast.13), channel_id=1, source_target_pairs={{0,16},{16,0},{1,17},{17,1},{2,18},{18,2},{3,19},{19,3},{4,20},{20... | collective-permute-start | bytes 786440 | tf_op jit(solution)/shard_map/ppermute | solution.py:446
  24.8 4.0 %collective-permute-start.1 = (bf16[136,128]{1,0:T(8,128)(2,1)S(1)}, bf16[136,128]{1,0:T(8,128)(2,1)S(1)}, u32[]{:S(2)}, u32[]{:S(2)}) collective-permute-start(bf16[136,128]{1,0:T(8,128)(2,1)S(1)} %get-tuple-element.22), channel_id=1, source_target_pairs={{0,2},{2,0},{4,6},{6,4},{8,10},{10,8},{12,14},{14,12},{1,3},{3,1},... | collective-permute-start | bytes 104456 | tf_op jit(solution)/shard_map/ppermute | solution.py:464
  26.3 4.0 %collective-permute-start.2 = (bf16[136,128]{1,0:T(8,128)(2,1)S(1)}, bf16[136,128]{1,0:T(8,128)(2,1)S(1)}, u32[]{:S(2)}, u32[]{:S(2)}) collective-permute-start(bf16[136,128]{1,0:T(8,128)(2,1)S(1)} %get-tuple-element.23), channel_id=1, source_target_pairs={{0,4},{2,6},{4,0},{6,2},{8,12},{10,14},{12,8},{14,10},{1,5},{3,7},... | collective-permute-start | bytes 104456 | tf_op jit(solution)/shard_map/ppermute | solution.py:464
  28.1 4.8 %collective-permute-start.3 = (bf16[136,128]{1,0:T(8,128)(2,1)S(1)}, bf16[136,128]{1,0:T(8,128)(2,1)S(1)}, u32[]{:S(2)}, u32[]{:S(2)}) collective-permute-start(bf16[136,128]{1,0:T(8,128)(2,1)S(1)} %get-tuple-element.24), channel_id=1, source_target_pairs={{0,6},{2,4},{4,2},{6,0},{8,14},{10,12},{12,10},{14,8},{1,7},{3,5},... | collective-permute-start | bytes 104456 | tf_op jit(solution)/shard_map/ppermute | solution.py:464
  33.3 6.2 %collective-permute-start.4 = (f32[136,128]{1,0:T(8,128)S(1)}, f32[136,128]{1,0:T(8,128)S(1)}, u32[]{:S(2)}, u32[]{:S(2)}) collective-permute-start(f32[136,128]{1,0:T(8,128)S(1)} %merge.2.refs_0_), channel_id=1, source_target_pairs={{0,12},{2,14},{4,8},{6,10},{8,4},{10,6},{12,0},{14,2},{1,13},{3,15... | collective-permute-start | bytes 208904 | tf_op jit(solution)/shard_map/ppermute | solution.py:464
  39.8 4.0 %collective-permute-start.5 = (bf16[128,128]{1,0:T(8,128)(2,1)S(1)}, bf16[128,128]{1,0:T(8,128)(2,1)S(1)}, u32[]{:S(2)}, u32[]{:S(2)}) collective-permute-start(bf16[128,128]{1,0:T(8,128)(2,1)S(1)} %merge.3.refs_0_), channel_id=1, source_target_pairs={{0,2},{2,0},{4,6},{6,4},{8,10},{10,8},{12,14},{14,12},{1,3},{3,1},... | collective-permute-start | bytes 98312 | tf_op jit(solution)/shard_map/ppermute | solution.py:464
  40.4 3.9 %collective-permute-start.6 = (bf16[128,128]{1,0:T(8,128)(2,1)S(1)}, bf16[128,128]{1,0:T(8,128)(2,1)S(1)}, u32[]{:S(2)}, u32[]{:S(2)}) collective-permute-start(bf16[128,128]{1,0:T(8,128)(2,1)S(1)} %merge.3.refs_0_), channel_id=1, source_target_pairs={{0,4},{2,6},{4,0},{6,2},{8,12},{10,14},{12,8},{14,10},{1,5},{3,7},... | collective-permute-start | bytes 98312 | tf_op jit(solution)/shard_map/ppermute | solution.py:464
  40.4 5.2 %collective-permute-start.7 = (bf16[128,128]{1,0:T(8,128)(2,1)S(1)}, bf16[128,128]{1,0:T(8,128)(2,1)S(1)}, u32[]{:S(2)}, u32[]{:S(2)}) collective-permute-start(bf16[128,128]{1,0:T(8,128)(2,1)S(1)} %merge.3.refs_0_), channel_id=1, source_target_pairs={{0,6},{2,4},{4,2},{6,0},{8,14},{10,12},{12,10},{14,8},{1,7},{3,5},... | collective-permute-start | bytes 98312 | tf_op jit(solution)/shard_map/ppermute | solution.py:464

commit v9 on v8

--- a/solution.py
+++ b/solution.py
@@ -160,8 +160,11 @@
     total = jnp.sum(weights, axis=1, keepdims=True)
     high = weights.astype(BF16)
     low = (weights - high.astype(F32)).astype(BF16)
-    weighted = jnp.dot(high, values, preferred_element_type=F32)
-    weighted = weighted + jnp.dot(low, values, preferred_element_type=F32)
+    weighted = jnp.dot(
+        jnp.concatenate([high, low], axis=1),
+        jnp.concatenate([values, values], axis=0),
+        preferred_element_type=F32,
+    )
     return peak, total, weighted
 
 

time: 48.4 us -> 48.4 us (level)
  no operation moved by 1% of the time
where the time goes in v9:
time: 48.4 us; the launch traced here: 48 us
  starting transfers between devices  20.1 us (42%)
  waiting for transfers between devices  19.2 us (40%)
  Pallas kernels  7.41 us (15%)
  between operations  1.34 us (3%)
    ppermute x1, waiting for transfers between devices, step(): lax.ppermute(away[shift - 1].reshape(flat), 'head', [(h, (h + shift) % he...  10.2 us
    ppermute x7, starting transfers between devices, swapped(): return lax.ppermute(x, 'seq', [(s, s ^ distance) for s in range(seq_count)])  9.84 us
    ppermute x7, waiting for transfers between devices, swapped(): return lax.ppermute(x, 'seq', [(s, s ^ distance) for s in range(seq_count)])  8.98 us
    all_to_all x1, starting transfers between devices, step(): lax.all_to_all(packed.reshape(cycle_size, 2, 2 * span_rows * kv_local, he...  8.34 us
    ppermute x1, starting transfers between devices, step(): lax.ppermute(away[shift - 1].reshape(flat), 'head', [(h, (h + shift) % he...  1.93 us
    pallas_call x1, Pallas kernels, pack(): pl.pallas_call(functools.partial(pack_kernel, rows // 2), out_shape=(jax....  1.87 us
    pallas_call x1, Pallas kernels, relay(): pl.pallas_call(functools.partial(relay_kernel, kv_count), out_shape=(shap...  1.76 us
    pallas_call x1, Pallas kernels, fresh_rows(): pl.pallas_call(functools.partial(fresh_kernel, score_scale, ways), out_sh...  1.29 us
  transfers between devices with their start and end apart: 9, of which 8 were waited for; matrix products, arithmetic and copies ran while one was open for 0% of the time, Pallas kernels for 8%

profile of v9, /device:TPU:0, one launch (start us, length us, event | category | flops | bytes accessed | tf_op | source)
XLA Modules:
  0.0 48.0 jit_solution(9000653157264694062)
XLA Ops:
  0.6 1.9 %pack.1 = (bf16[2,8,2,32,2,128]{5,4,3,2,1,0:T(2,128)(2,1)}, bf16[2,8,32,2,128]{4,3,2,1,0:T(2,128)(2,1)S(1)}, bf16[1,2,8,32,2,128]{5,4,3,2,1,0:T(2,128)(2,1)S(1)}...) custom-call(bf16[8,32,2,2,128]{4,3,2,1,0:T(2,128)(2,1)} %bitcast.14, bf16[8,32,2,2,128]{4,3,2,1,0:T(2,128)(2,1)} %bitcast.15, ...), custom_call_target="tpu_custom_call" | custom-call | tf_op jit(solution)/shard_map/pack/pallas_call | solution.py:135
  2.5 8.3 %all-to-all-start = ((bf16[16,2,64,128]{3,2,1,0:T(8,128)(2,1)}), bf16[16,2,64,128]{3,2,1,0:T(8,128)(2,1)S(1)}, u32[]{:S(2)}, u32[]{:S(2)}) async-start(bf16[16,2,64,128]{3,2,1,0:T(8,128)(2,1)} %bitcast.2), calls=%async_computation | async-start | bytes 1048576 | tf_op jit(solution)/shard_map/all_to_all | solution.py:455
  10.9 1.9 %collective-permute-start = (bf16[2,512,128]{2,1,0:T(8,128)(2,1)S(1)}, bf16[2,512,128]{2,1,0:T(8,128)(2,1)S(1)}, u32[]{:S(2)}, u32[]{:S(2)}) collective-permute-start(bf16[2,512,128]{2,1,0:T(8,128)(2,1)S(1)} %bitcast.13), channel_id=1, source_target_pairs={{0,16},{16,0},{1,17},{17,1},{2,18},{18,2},{3,19},{19,3},{4,20},{20... | collective-permute-start | bytes 786440 | tf_op jit(solution)/shard_map/ppermute | solution.py:449
  13.4 10.2 %collective-permute-done.rest_1_ = bf16[2,512,128]{2,1,0:T(8,128)(2,1)S(1)} collective-permute-done((bf16[2,512,128]{2,1,0:T(8,128)(2,1)S(1)}, bf16[2,512,128]{2,1,0:T(8,128)(2,1)S(1)}, u32[]{:S(2)}, u32[]{:S(2)}) %collective-permute-start) | collective-permute-done | bytes 262176 | tf_op jit(solution)/shard_map/ppermute | solution.py:449
  23.6 1.1 %attend.1 = (bf16[136,128]{1,0:T(8,128)(2,1)S(1)}, bf16[136,128]{1,0:T(8,128)(2,1)S(1)}, bf16[136,128]{1,0:T(8,128)(2,1)S(1)}, bf16[136,128]{1,0:T(8,128)(2,1)S(1)}) custom-call(s32[1]{0:T(128)S(6)} %copy.11.length_ref, bf16[16,32,128]{2,1,0:T(8,128)(2,1)S(1)} %get-tuple-element.17.query_ref, s32[1,512]{1,0:T(1,128)S(1)} %get-tuple-element.18.place_ref, ...), custom_call_target="tpu_custom_call" | custom-call | tf_op jit(solution)/shard_map/attend/pallas_call | solution.py:219
  24.7 1.5 %collective-permute-start.1 = (bf16[136,128]{1,0:T(8,128)(2,1)S(1)}, bf16[136,128]{1,0:T(8,128)(2,1)S(1)}, u32[]{:S(2)}, u32[]{:S(2)}) collective-permute-start(bf16[136,128]{1,0:T(8,128)(2,1)S(1)} %get-tuple-element.22), channel_id=1, source_target_pairs={{0,2},{2,0},{4,6},{6,4},{8,10},{10,8},{12,14},{14,12},{1,3},{3,1},... | collective-permute-start | bytes 104456 | tf_op jit(solution)/shard_map/ppermute | solution.py:467
  26.2 1.8 %collective-permute-start.2 = (bf16[136,128]{1,0:T(8,128)(2,1)S(1)}, bf16[136,128]{1,0:T(8,128)(2,1)S(1)}, u32[]{:S(2)}, u32[]{:S(2)}) collective-permute-start(bf16[136,128]{1,0:T(8,128)(2,1)S(1)} %get-tuple-element.23), channel_id=1, source_target_pairs={{0,4},{2,6},{4,0},{6,2},{8,12},{10,14},{12,8},{14,10},{1,5},{3,7},... | collective-permute-start | bytes 104456 | tf_op jit(solution)/shard_map/ppermute | solution.py:467
  28.0 0.2 collective-permute-start.3
  28.2 0.4 collective-permute-done.1.refs_1_
  28.7 1.5 %collective-permute-done.2.refs_2_ = bf16[136,128]{1,0:T(8,128)(2,1)S(1)} collective-permute-done((bf16[136,128]{1,0:T(8,128)(2,1)S(1)}, bf16[136,128]{1,0:T(8,128)(2,1)S(1)}, u32[]{:S(2)}, u32[]{:S(2)}) %collective-permute-start.2) | collective-permute-done | bytes 34848 | tf_op jit(solution)/shard_map/ppermute | solution.py:467
  30.2 2.7 %collective-permute-done.3.refs_3_ = bf16[136,128]{1,0:T(8,128)(2,1)S(1)} collective-permute-done((bf16[136,128]{1,0:T(8,128)(2,1)S(1)}, bf16[136,128]{1,0:T(8,128)(2,1)S(1)}, u32[]{:S(2)}, u32[]{:S(2)}) %collective-permute-start.3) | collective-permute-done | bytes 34848 | tf_op jit(solution)/shard_map/ppermute | solution.py:467
  32.9 0.4 merge.2.refs_0_
  33.2 2.8 %collective-permute-start.4 = (f32[136,128]{1,0:T(8,128)S(1)}, f32[136,128]{1,0:T(8,128)S(1)}, u32[]{:S(2)}, u32[]{:S(2)}) collective-permute-start(f32[136,128]{1,0:T(8,128)S(1)} %merge.2.refs_0_), channel_id=1, source_target_pairs={{0,12},{2,14},{4,8},{6,10},{8,4},{10,6},{12,0},{14,2},{1,13},{3,15... | collective-permute-start | bytes 208904 | tf_op jit(solution)/shard_map/ppermute | solution.py:467
  36.0 1.3 %fresh.1.refs_2_ = f32[136,128]{1,0:T(8,128)S(1)} custom-call(bf16[16,32,128]{2,1,0:T(8,128)(2,1)S(1)} %get-tuple-element.17.query_ref, bf16[32,128]{1,0:T(8,128)(2,1)} %bitcast.17, bf16[32,128]{1,0:T(8,128)(2,1)} %bitcast.18, s32[16]{0:T(128)} %depth_hbm.1), custom_call_target="tpu_custom_call" | custom-call | tf_op jit(solution)/shard_map/fresh/pallas_call | solution.py:285
  37.3 2.1 %collective-permute-done.4.refs_1_ = f32[136,128]{1,0:T(8,128)S(1)} collective-permute-done((f32[136,128]{1,0:T(8,128)S(1)}, f32[136,128]{1,0:T(8,128)S(1)}, u32[]{:S(2)}, u32[]{:S(2)}) %collective-permute-start.4) | collective-permute-done | bytes 69664 | tf_op jit(solution)/shard_map/ppermute | solution.py:467
  39.4 0.3 merge.3.refs_0_
  39.8 0.6 %collective-permute-start.5 = (bf16[128,128]{1,0:T(8,128)(2,1)S(1)}, bf16[128,128]{1,0:T(8,128)(2,1)S(1)}, u32[]{:S(2)}, u32[]{:S(2)}) collective-permute-start(bf16[128,128]{1,0:T(8,128)(2,1)S(1)} %merge.3.refs_0_), channel_id=1, source_target_pairs={{0,2},{2,0},{4,6},{6,4},{8,10},{10,8},{12,14},{14,12},{1,3},{3,1},... | collective-permute-start | bytes 98312 | tf_op jit(solution)/shard_map/ppermute | solution.py:467
  40.4 0.0 collective-permute-start.6
  40.4 2.9 %collective-permute-start.7 = (bf16[128,128]{1,0:T(8,128)(2,1)S(1)}, bf16[128,128]{1,0:T(8,128)(2,1)S(1)}, u32[]{:S(2)}, u32[]{:S(2)}) collective-permute-start(bf16[128,128]{1,0:T(8,128)(2,1)S(1)} %merge.3.refs_0_), channel_id=1, source_target_pairs={{0,6},{2,4},{4,2},{6,0},{8,14},{10,12},{12,10},{14,8},{1,7},{3,5},... | collective-permute-start | bytes 98312 | tf_op jit(solution)/shard_map/ppermute | solution.py:467
  43.3 0.4 collective-permute-done.5.refs_1_
  43.8 0.5 %collective-permute-done.6.refs_2_ = bf16[128,128]{1,0:T(8,128)(2,1)S(1)} collective-permute-done((bf16[128,128]{1,0:T(8,128)(2,1)S(1)}, bf16[128,128]{1,0:T(8,128)(2,1)S(1)}, u32[]{:S(2)}, u32[]{:S(2)}) %collective-permute-start.6) | collective-permute-done | bytes 32800 | tf_op jit(solution)/shard_map/ppermute | solution.py:467
  44.3 1.3 %collective-permute-done.7.refs_3_ = bf16[128,128]{1,0:T(8,128)(2,1)S(1)} collective-permute-done((bf16[128,128]{1,0:T(8,128)(2,1)S(1)}, bf16[128,128]{1,0:T(8,128)(2,1)S(1)}, u32[]{:S(2)}, u32[]{:S(2)}) %collective-permute-start.7) | collective-permute-done | bytes 32800 | tf_op jit(solution)/shard_map/ppermute | solution.py:467
  45.6 0.7 %join.1 = bf16[512,128]{1,0:T(8,128)(2,1)} custom-call(bf16[128,128]{1,0:T(8,128)(2,1)S(1)} %merge.3.refs_0_, bf16[128,128]{1,0:T(8,128)(2,1)S(1)} %collective-permute-done.5.refs_1_, bf16[128,128]{1,0:T(8,128)(2,1)S(1)} %collective-permute-done.6.refs_2_, bf16[128,128]{1,0:T(8,128)(2,1)S(1)} %collective-permute-done.7.refs_3_), custom_call_target="tpu_custom_call" | custom-call | tf_op jit(solution)/shard_map/join/pallas_call | solution.py:376
  46.3 0.0 all-to-all-done
  46.3 1.8 %relay.1 = (bf16[32,32,128]{2,1,0:T(8,128)(2,1)}, bf16[32,32,128]{2,1,0:T(8,128)(2,1)}) custom-call(s32[32]{0:T(128)} %slots_hbm.3, s32[1]{0:T(128)S(6)} %copy.11.length_ref, bf16[16,2,2,32,128]{4,3,2,1,0:T(8,128)(2,1)S(1)} %bitcast.11), custom_call_target="tpu_custom_call" | custom-call | tf_op jit(solution)/shard_map/relay/pallas_call | solution.py:409
Async XLA Ops:
  2.5 43.8 %all-to-all-start = ((bf16[16,2,64,128]{3,2,1,0:T(8,128)(2,1)}), bf16[16,2,64,128]{3,2,1,0:T(8,128)(2,1)S(1)}, u32[]{:S(2)}, u32[]{:S(2)}) async-start(bf16[16,2,64,128]{3,2,1,0:T(8,128)(2,1)} %bitcast.2), calls=%async_computation | async-start | bytes 1048576 | tf_op jit(solution)/shard_map/all_to_all | solution.py:455
  10.9 12.8 %collective-permute-start = (bf16[2,512,128]{2,1,0:T(8,128)(2,1)S(1)}, bf16[2,512,128]{2,1,0:T(8,128)(2,1)S(1)}, u32[]{:S(2)}, u32[]{:S(2)}) collective-permute-start(bf16[2,512,128]{2,1,0:T(8,128)(2,1)S(1)} %bitcast.13), channel_id=1, source_target_pairs={{0,16},{16,0},{1,17},{17,1},{2,18},{18,2},{3,19},{19,3},{4,20},{20... | collective-permute-start | bytes 786440 | tf_op jit(solution)/shard_map/ppermute | solution.py:449
  24.7 4.0 %collective-permute-start.1 = (bf16[136,128]{1,0:T(8,128)(2,1)S(1)}, bf16[136,128]{1,0:T(8,128)(2,1)S(1)}, u32[]{:S(2)}, u32[]{:S(2)}) collective-permute-start(bf16[136,128]{1,0:T(8,128)(2,1)S(1)} %get-tuple-element.22), channel_id=1, source_target_pairs={{0,2},{2,0},{4,6},{6,4},{8,10},{10,8},{12,14},{14,12},{1,3},{3,1},... | collective-permute-start | bytes 104456 | tf_op jit(solution)/shard_map/ppermute | solution.py:467
  26.2 4.0 %collective-permute-start.2 = (bf16[136,128]{1,0:T(8,128)(2,1)S(1)}, bf16[136,128]{1,0:T(8,128)(2,1)S(1)}, u32[]{:S(2)}, u32[]{:S(2)}) collective-permute-start(bf16[136,128]{1,0:T(8,128)(2,1)S(1)} %get-tuple-element.23), channel_id=1, source_target_pairs={{0,4},{2,6},{4,0},{6,2},{8,12},{10,14},{12,8},{14,10},{1,5},{3,7},... | collective-permute-start | bytes 104456 | tf_op jit(solution)/shard_map/ppermute | solution.py:467
  28.0 4.8 %collective-permute-start.3 = (bf16[136,128]{1,0:T(8,128)(2,1)S(1)}, bf16[136,128]{1,0:T(8,128)(2,1)S(1)}, u32[]{:S(2)}, u32[]{:S(2)}) collective-permute-start(bf16[136,128]{1,0:T(8,128)(2,1)S(1)} %get-tuple-element.24), channel_id=1, source_target_pairs={{0,6},{2,4},{4,2},{6,0},{8,14},{10,12},{12,10},{14,8},{1,7},{3,5},... | collective-permute-start | bytes 104456 | tf_op jit(solution)/shard_map/ppermute | solution.py:467
  33.2 6.2 %collective-permute-start.4 = (f32[136,128]{1,0:T(8,128)S(1)}, f32[136,128]{1,0:T(8,128)S(1)}, u32[]{:S(2)}, u32[]{:S(2)}) collective-permute-start(f32[136,128]{1,0:T(8,128)S(1)} %merge.2.refs_0_), channel_id=1, source_target_pairs={{0,12},{2,14},{4,8},{6,10},{8,4},{10,6},{12,0},{14,2},{1,13},{3,15... | collective-permute-start | bytes 208904 | tf_op jit(solution)/shard_map/ppermute | solution.py:467
  39.8 4.0 %collective-permute-start.5 = (bf16[128,128]{1,0:T(8,128)(2,1)S(1)}, bf16[128,128]{1,0:T(8,128)(2,1)S(1)}, u32[]{:S(2)}, u32[]{:S(2)}) collective-permute-start(bf16[128,128]{1,0:T(8,128)(2,1)S(1)} %merge.3.refs_0_), channel_id=1, source_target_pairs={{0,2},{2,0},{4,6},{6,4},{8,10},{10,8},{12,14},{14,12},{1,3},{3,1},... | collective-permute-start | bytes 98312 | tf_op jit(solution)/shard_map/ppermute | solution.py:467
  40.4 3.9 %collective-permute-start.6 = (bf16[128,128]{1,0:T(8,128)(2,1)S(1)}, bf16[128,128]{1,0:T(8,128)(2,1)S(1)}, u32[]{:S(2)}, u32[]{:S(2)}) collective-permute-start(bf16[128,128]{1,0:T(8,128)(2,1)S(1)} %merge.3.refs_0_), channel_id=1, source_target_pairs={{0,4},{2,6},{4,0},{6,2},{8,12},{10,14},{12,8},{14,10},{1,5},{3,7},... | collective-permute-start | bytes 98312 | tf_op jit(solution)/shard_map/ppermute | solution.py:467
  40.4 5.2 %collective-permute-start.7 = (bf16[128,128]{1,0:T(8,128)(2,1)S(1)}, bf16[128,128]{1,0:T(8,128)(2,1)S(1)}, u32[]{:S(2)}, u32[]{:S(2)}) collective-permute-start(bf16[128,128]{1,0:T(8,128)(2,1)S(1)} %merge.3.refs_0_), channel_id=1, source_target_pairs={{0,6},{2,4},{4,2},{6,0},{8,14},{10,12},{12,10},{14,8},{1,7},{3,5},... | collective-permute-start | bytes 98312 | tf_op jit(solution)/shard_map/ppermute | solution.py:467
